TPU v7x, 32 devices: a whole 2x2x4 slice. The times are simulated.
32 devices in a mesh: gx: 4 (over y, x), gy: 8 (over z, core).
Axes of the slice: x: 2, y: 2, z: 4, core: 2. Of those that a mesh axis runs over, the one named last changes fastest.
Arguments:
- electric: float32 [3, 128, 6144], P(None, 'gx', 'gy'), may hold values from -6 to 6
- magnetic: float32 [3, 128, 6144], P(None, 'gx', 'gy'), may hold values from -6 to 6
- tensor: float32 [9, 128, 6144], P(None, 'gx', 'gy'), may hold values from -0.15 to 1
- saved: bfloat16 [6, 3, 128, 6144], P(None, None, 'gx', 'gy'), may hold values from -6 to 6
Outputs:
- adj_electric: float32 [3, 128, 6144], P(None, 'gx', 'gy')
- adj_magnetic: float32 [3, 128, 6144], P(None, 'gx', 'gy')
- gradient: float32 [128, 6144], P('gx', 'gy')
All inputs are finite; a program needn't handle non-finite values.
Results may differ from a plain program's by a relative error of at most 0.0003.
Values sent between devices are 32-bit elements; how exact they have to be, the bound alone decides.
No kernel may reach another device: no remote copies, remote signals or barrier semaphores. Data moves between devices by JAX's collectives and lax.ppermute only.
A program may use at most 64 MiB of HBM per device.

v0:
```python
import jax
import jax.numpy as jnp
from jax import lax
from jax.sharding import PartitionSpec as P

NZ = 48
STEPS = 6
RADIUS = 8


courant = 0.45


def passed_along(block, axis, distance):
    devices = range(lax.axis_size(axis))
    route = [(i - distance, i) for i in devices if i - distance in devices]
    return lax.ppermute(block, axis, route)


def with_halo(block, sides, width):
    for axis, dim in sides:
        count = lax.axis_size(axis)
        forward = [(i, i + 1) for i in range(count - 1)]
        backward = [(target, source) for source, target in forward]
        low = lax.ppermute(
            lax.slice_in_dim(block, block.shape[dim] - width, None, axis=dim), axis, forward
        )
        high = lax.ppermute(lax.slice_in_dim(block, 0, width, axis=dim), axis, backward)
        block = jnp.concatenate([low, block, high], axis=dim)
    return block


def from_xside(faces, offset):
    return passed_along(faces, "gx", offset)


def from_yside(faces, offset):
    return passed_along(faces, "gy", offset)


def tent(offset):
    return (RADIUS + 1.0 - abs(offset)) / (RADIUS + 1.0)


def coverage(places, length):
    total = jnp.zeros(places.shape, jnp.float32)
    for offset in range(-RADIUS, RADIUS + 1):
        inside = ((places + offset >= 0) & (places + offset < length)).astype(jnp.float32)
        total = total + tent(offset) * inside
    return total


def filter_rows(extended, tile_rows):
    result = tent(-RADIUS) * extended[0:tile_rows]
    for offset in range(-RADIUS + 1, RADIUS + 1):
        result = result + tent(offset) * extended[RADIUS + offset : RADIUS + offset + tile_rows]
    return result


def filter_columns(extended, tile_width):
    result = tent(-RADIUS) * extended[:, 0:tile_width]
    for offset in range(-RADIUS + 1, RADIUS + 1):
        begin = (RADIUS + offset) * NZ
        result = result + tent(offset) * extended[:, begin : begin + tile_width]
    return result


def leapfrog(fields_e, fields_h, mats, fetch_ahead, fetch_behind):
    rows = fields_e[0].shape[0]
    width = fields_e[0].shape[1]
    depth = lax.broadcasted_iota(jnp.int32, (rows, width), 1) % NZ
    upper_mask = (depth != NZ - 1).astype(jnp.float32)
    lower_mask = (depth != 0).astype(jnp.float32)
    zero_column = jnp.zeros((rows, 1), jnp.float32)

    def next_x(field, border):
        return jnp.concatenate([field[1:], border], axis=0) - field

    def next_y(field, border):
        return jnp.concatenate([field[:, NZ:], border], axis=1) - field

    def next_z(field):
        return jnp.concatenate([field[:, 1:], zero_column], axis=1) * upper_mask - field

    def prev_x(field, border):
        return field - jnp.concatenate([border, field[:-1]], axis=0)

    def prev_y(field, border):
        return field - jnp.concatenate([border, field[:, :-NZ]], axis=1)

    def prev_z(field):
        return field - jnp.concatenate([zero_column, field[:, :-1]], axis=1) * lower_mask

    scaled_e = [
        mats[col] * fields_e[0] + mats[3 + col] * fields_e[1] + mats[6 + col] * fields_e[2]
        for col in range(3)
    ]
    border_x, border_y = fetch_ahead(scaled_e)
    curl_zero = next_y(scaled_e[2], border_y[1]) - next_z(scaled_e[1])
    curl_one = next_z(scaled_e[0]) - next_x(scaled_e[2], border_x[1])
    curl_two = next_x(scaled_e[1], border_x[0]) - next_y(scaled_e[0], border_y[0])
    fields_h = [
        fields_h[0] - courant * curl_zero,
        fields_h[1] - courant * curl_one,
        fields_h[2] - courant * curl_two,
    ]
    back_x, back_y = fetch_behind(fields_h)
    back_zero = prev_y(fields_h[2], back_y[1]) - prev_z(fields_h[1])
    back_one = prev_z(fields_h[0]) - prev_x(fields_h[2], back_x[1])
    back_two = prev_x(fields_h[1], back_x[0]) - prev_y(fields_h[0], back_y[0])
    fields_e = [
        fields_e[0] + courant * back_zero,
        fields_e[1] + courant * back_one,
        fields_e[2] + courant * back_two,
    ]
    return (fields_e, fields_h)


def shards(electric, magnetic, tensor, saved):
    tile_rows = electric.shape[1]
    tile_width = electric.shape[2]
    tile_cols = tile_width // NZ
    corr = jnp.zeros((tile_rows, tile_width), jnp.float32)
    fields_e = [electric[index] for index in range(3)]
    fields_h = [magnetic[index] for index in range(3)]
    mats = [tensor[index] for index in range(9)]

    def fetch_ahead(parts):
        border_x = from_xside(jnp.stack([parts[1][:1], parts[2][:1]]), -1)
        border_y = from_yside(jnp.stack([parts[0][:, :NZ], parts[2][:, :NZ]]), -1)
        return (border_x, border_y)

    def fetch_behind(parts):
        back_x = from_xside(jnp.stack([parts[1][-1:], parts[2][-1:]]), 1)
        back_y = from_yside(jnp.stack([parts[0][:, -NZ:], parts[2][:, -NZ:]]), 1)
        return (back_x, back_y)

    for section in range(STEPS):
        fields_e, fields_h = leapfrog(fields_e, fields_h, mats, fetch_ahead, fetch_behind)
        frame = saved[section].astype(jnp.float32)
        corr = corr + (fields_e[0] * frame[0] + fields_e[1] * frame[1] + fields_e[2] * frame[2])
    row_places = lax.axis_index("gx") * tile_rows + jnp.arange(tile_rows, dtype=jnp.int32)
    col_places = lax.axis_index("gy") * tile_cols + jnp.arange(tile_cols, dtype=jnp.int32)
    cover_rows = coverage(row_places, lax.axis_size("gx") * tile_rows)
    cover_cols = jnp.repeat(coverage(col_places, lax.axis_size("gy") * tile_cols), NZ)
    cover = cover_rows[:, None] * cover_cols[None, :]
    scaled = corr / cover
    extended = with_halo(scaled, (("gx", 0),), RADIUS)
    across = filter_rows(extended, tile_rows)
    widened = with_halo(across, (("gy", 1),), RADIUS * NZ)
    gradient = filter_columns(widened, tile_width)
    return (jnp.stack(fields_e), jnp.stack(fields_h), gradient)


def solution(mesh):
    in_specs = (
        P(None, "gx", "gy"),
        P(None, "gx", "gy"),
        P(None, "gx", "gy"),
        P(None, None, "gx", "gy"),
    )
    out_specs = (P(None, "gx", "gy"), P(None, "gx", "gy"), P("gx", "gy"))
    return jax.shard_map(shards, mesh=mesh, in_specs=in_specs, out_specs=out_specs, check_vma=False)
```

profile of v0, /device:TPU:11, one launch (start us, length us, event | category | flops | bytes accessed | tf_op | source)
XLA Modules:
  0.0 120.9 jit_solution(9001868544562229981)
XLA Ops:
  0.6 1.5 %fusion.308 = (f32[32,768]{1,0:T(8,128)S(1)}, f32[32,768]{1,0:T(8,128)S(1)}, f32[32,768]{1,0:T(8,128)S(1)}) fusion(f32[3,32,768]{2,1,0:T(8,128)} %param.4, f32[9,32,768]{2,1,0:T(8,128)} %param.6), kind=kLoop, calls=%fused_computation.481 | loop fusion | flops 368640 | bytes 1474560 | tf_op jit(solution)/shard_map/add | solution.py:95
  2.1 2.6 %collective-permute-start.1 = (f32[2,32,48]{2,1,0:T(8,128)S(1)}, f32[2,32,48]{2,1,0:T(8,128)S(1)}, u32[]{:S(2)}, u32[]{:S(2)}) collective-permute-start(f32[2,32,48]{2,1,0:T(8,128)S(1)} %pad_maximum_fusion.6), channel_id=1, source_target_pairs={{1,0},{2,1},{3,2},{4,3},{5,4},{6,5},{7,6},{9,8},{10,9},{11,10},{12... | collective-permute-start | bytes 36872 | tf_op jit(solution)/shard_map/ppermute | solution.py:17
  4.8 2.2 %collective-permute-start = (f32[2,1,768]{2,1,0:T(1,128)S(1)}, f32[2,1,768]{2,1,0:T(1,128)S(1)}, u32[]{:S(2)}, u32[]{:S(2)}) collective-permute-start(f32[2,1,768]{2,1,0:T(1,128)S(1)} %pad_maximum_fusion.18), channel_id=1, source_target_pairs={{8,0},{16,8},{24,16},{9,1},{17,9},{25,17},{10,2},{18,10},{26,18},{... | collective-permute-start | bytes 18440 | tf_op jit(solution)/shard_map/ppermute | solution.py:17
  7.0 0.2 slice_convert_fusion.5
  7.6 0.1 slice.1037
  7.8 2.2 %collective-permute-done = f32[2,1,768]{2,1,0:T(1,128)S(1)} collective-permute-done((f32[2,1,768]{2,1,0:T(1,128)S(1)}, f32[2,1,768]{2,1,0:T(1,128)S(1)}, u32[]{:S(2)}, u32[]{:S(2)}) %collective-permute-start) | collective-permute-done | bytes 6176 | tf_op jit(solution)/shard_map/ppermute | solution.py:17
  10.1 0.1 fusion.75
  10.3 2.5 %collective-permute-start.3 = (f32[2,1,768]{2,1,0:T(1,128)S(1)}, f32[2,1,768]{2,1,0:T(1,128)S(1)}, u32[]{:S(2)}, u32[]{:S(2)}) collective-permute-start(f32[2,1,768]{2,1,0:T(1,128)S(1)} %pad_maximum_fusion.19), channel_id=1, source_target_pairs={{0,8},{8,16},{16,24},{1,9},{9,17},{17,25},{2,10},{10,18},{18,26},{... | collective-permute-start | bytes 18440 | tf_op jit(solution)/shard_map/ppermute | solution.py:17
  12.9 4.4 %collective-permute-start.2 = (f32[2,32,48]{2,1,0:T(8,128)S(1)}, f32[2,32,48]{2,1,0:T(8,128)S(1)}, u32[]{:S(2)}, u32[]{:S(2)}) collective-permute-start(f32[2,32,48]{2,1,0:T(8,128)S(1)} %pad_maximum_fusion.7), channel_id=1, source_target_pairs={{0,1},{1,2},{2,3},{3,4},{4,5},{5,6},{6,7},{8,9},{9,10},{10,11},{11... | collective-permute-start | bytes 36872 | tf_op jit(solution)/shard_map/ppermute | solution.py:17
  17.3 1.0 collective-permute-done.2
  18.3 0.2 fusion.309
  18.6 3.1 %collective-permute-start.4 = (f32[2,1,768]{2,1,0:T(1,128)S(1)}, f32[2,1,768]{2,1,0:T(1,128)S(1)}, u32[]{:S(2)}, u32[]{:S(2)}) collective-permute-start(f32[2,1,768]{2,1,0:T(1,128)S(1)} %pad_maximum_fusion.20), channel_id=1, source_target_pairs={{8,0},{16,8},{24,16},{9,1},{17,9},{25,17},{10,2},{18,10},{26,18},{... | collective-permute-start | bytes 18440 | tf_op jit(solution)/shard_map/ppermute | solution.py:17
  22.1 3.3 %collective-permute-start.5 = (f32[2,32,48]{2,1,0:T(8,128)S(1)}, f32[2,32,48]{2,1,0:T(8,128)S(1)}, u32[]{:S(2)}, u32[]{:S(2)}) collective-permute-start(f32[2,32,48]{2,1,0:T(8,128)S(1)} %pad_maximum_fusion.8), channel_id=1, source_target_pairs={{1,0},{2,1},{3,2},{4,3},{5,4},{6,5},{7,6},{9,8},{10,9},{11,10},{12... | collective-permute-start | bytes 36872 | tf_op jit(solution)/shard_map/ppermute | solution.py:17
  25.5 2.7 %collective-permute-done.5 = f32[2,32,48]{2,1,0:T(8,128)S(1)} collective-permute-done((f32[2,32,48]{2,1,0:T(8,128)S(1)}, f32[2,32,48]{2,1,0:T(8,128)S(1)}, u32[]{:S(2)}, u32[]{:S(2)}) %collective-permute-start.5) | collective-permute-done | bytes 12320 | tf_op jit(solution)/shard_map/ppermute | solution.py:17
  28.2 0.1 fusion.83
  28.4 3.1 %collective-permute-start.7 = (f32[2,1,768]{2,1,0:T(1,128)S(1)}, f32[2,1,768]{2,1,0:T(1,128)S(1)}, u32[]{:S(2)}, u32[]{:S(2)}) collective-permute-start(f32[2,1,768]{2,1,0:T(1,128)S(1)} %pad_maximum_fusion.21), channel_id=1, source_target_pairs={{0,8},{8,16},{16,24},{1,9},{9,17},{17,25},{2,10},{10,18},{18,26},{... | collective-permute-start | bytes 18440 | tf_op jit(solution)/shard_map/ppermute | solution.py:17
  31.6 2.2 %collective-permute-start.6 = (f32[2,32,48]{2,1,0:T(8,128)S(1)}, f32[2,32,48]{2,1,0:T(8,128)S(1)}, u32[]{:S(2)}, u32[]{:S(2)}) collective-permute-start(f32[2,32,48]{2,1,0:T(8,128)S(1)} %pad_maximum_fusion.9), channel_id=1, source_target_pairs={{0,1},{1,2},{2,3},{3,4},{4,5},{5,6},{6,7},{8,9},{9,10},{10,11},{11... | collective-permute-start | bytes 36872 | tf_op jit(solution)/shard_map/ppermute | solution.py:17
  33.9 1.0 collective-permute-done.6
  34.8 0.2 fusion.310
  35.2 2.2 %collective-permute-start.8 = (f32[2,1,768]{2,1,0:T(1,128)S(1)}, f32[2,1,768]{2,1,0:T(1,128)S(1)}, u32[]{:S(2)}, u32[]{:S(2)}) collective-permute-start(f32[2,1,768]{2,1,0:T(1,128)S(1)} %pad_maximum_fusion.22), channel_id=1, source_target_pairs={{8,0},{16,8},{24,16},{9,1},{17,9},{25,17},{10,2},{18,10},{26,18},{... | collective-permute-start | bytes 18440 | tf_op jit(solution)/shard_map/ppermute | solution.py:17
  37.8 3.3 %collective-permute-start.9 = (f32[2,32,48]{2,1,0:T(8,128)S(1)}, f32[2,32,48]{2,1,0:T(8,128)S(1)}, u32[]{:S(2)}, u32[]{:S(2)}) collective-permute-start(f32[2,32,48]{2,1,0:T(8,128)S(1)} %pad_maximum_fusion.10), channel_id=1, source_target_pairs={{1,0},{2,1},{3,2},{4,3},{5,4},{6,5},{7,6},{9,8},{10,9},{11,10},{12... | collective-permute-start | bytes 36872 | tf_op jit(solution)/shard_map/ppermute | solution.py:17
  41.1 2.7 %collective-permute-done.9 = f32[2,32,48]{2,1,0:T(8,128)S(1)} collective-permute-done((f32[2,32,48]{2,1,0:T(8,128)S(1)}, f32[2,32,48]{2,1,0:T(8,128)S(1)}, u32[]{:S(2)}, u32[]{:S(2)}) %collective-permute-start.9) | collective-permute-done | bytes 12320 | tf_op jit(solution)/shard_map/ppermute | solution.py:17
  43.9 0.1 fusion.91
  44.1 4.0 %collective-permute-start.11 = (f32[2,1,768]{2,1,0:T(1,128)S(1)}, f32[2,1,768]{2,1,0:T(1,128)S(1)}, u32[]{:S(2)}, u32[]{:S(2)}) collective-permute-start(f32[2,1,768]{2,1,0:T(1,128)S(1)} %pad_maximum_fusion.23), channel_id=1, source_target_pairs={{0,8},{8,16},{16,24},{1,9},{9,17},{17,25},{2,10},{10,18},{18,26},{... | collective-permute-start | bytes 18440 | tf_op jit(solution)/shard_map/ppermute | solution.py:17
  48.2 2.2 %collective-permute-start.10 = (f32[2,32,48]{2,1,0:T(8,128)S(1)}, f32[2,32,48]{2,1,0:T(8,128)S(1)}, u32[]{:S(2)}, u32[]{:S(2)}) collective-permute-start(f32[2,32,48]{2,1,0:T(8,128)S(1)} %pad_maximum_fusion.11), channel_id=1, source_target_pairs={{0,1},{1,2},{2,3},{3,4},{4,5},{5,6},{6,7},{8,9},{9,10},{10,11},{11... | collective-permute-start | bytes 36872 | tf_op jit(solution)/shard_map/ppermute | solution.py:17
  50.4 1.0 collective-permute-done.10
  51.4 0.2 fusion.311
  51.7 1.9 %collective-permute-start.12 = (f32[2,1,768]{2,1,0:T(1,128)S(1)}, f32[2,1,768]{2,1,0:T(1,128)S(1)}, u32[]{:S(2)}, u32[]{:S(2)}) collective-permute-start(f32[2,1,768]{2,1,0:T(1,128)S(1)} %pad_maximum_fusion.24), channel_id=1, source_target_pairs={{8,0},{16,8},{24,16},{9,1},{17,9},{25,17},{10,2},{18,10},{26,18},{... | collective-permute-start | bytes 18440 | tf_op jit(solution)/shard_map/ppermute | solution.py:17
  53.7 0.1 slice.1114
  53.8 0.1 slice.1121
  54.1 3.0 %collective-permute-start.13 = (f32[2,32,48]{2,1,0:T(8,128)S(1)}, f32[2,32,48]{2,1,0:T(8,128)S(1)}, u32[]{:S(2)}, u32[]{:S(2)}) collective-permute-start(f32[2,32,48]{2,1,0:T(8,128)S(1)} %pad_maximum_fusion.12), channel_id=1, source_target_pairs={{1,0},{2,1},{3,2},{4,3},{5,4},{6,5},{7,6},{9,8},{10,9},{11,10},{12... | collective-permute-start | bytes 36872 | tf_op jit(solution)/shard_map/ppermute | solution.py:17
  57.1 2.7 %collective-permute-done.13 = f32[2,32,48]{2,1,0:T(8,128)S(1)} collective-permute-done((f32[2,32,48]{2,1,0:T(8,128)S(1)}, f32[2,32,48]{2,1,0:T(8,128)S(1)}, u32[]{:S(2)}, u32[]{:S(2)}) %collective-permute-start.13) | collective-permute-done | bytes 12320 | tf_op jit(solution)/shard_map/ppermute | solution.py:17
  59.9 0.1 fusion.99
  60.1 4.5 %collective-permute-start.15 = (f32[2,1,768]{2,1,0:T(1,128)S(1)}, f32[2,1,768]{2,1,0:T(1,128)S(1)}, u32[]{:S(2)}, u32[]{:S(2)}) collective-permute-start(f32[2,1,768]{2,1,0:T(1,128)S(1)} %pad_maximum_fusion.25), channel_id=1, source_target_pairs={{0,8},{8,16},{16,24},{1,9},{9,17},{17,25},{2,10},{10,18},{18,26},{... | collective-permute-start | bytes 18440 | tf_op jit(solution)/shard_map/ppermute | solution.py:17
  64.7 2.2 %collective-permute-start.14 = (f32[2,32,48]{2,1,0:T(8,128)S(1)}, f32[2,32,48]{2,1,0:T(8,128)S(1)}, u32[]{:S(2)}, u32[]{:S(2)}) collective-permute-start(f32[2,32,48]{2,1,0:T(8,128)S(1)} %pad_maximum_fusion.13), channel_id=1, source_target_pairs={{0,1},{1,2},{2,3},{3,4},{4,5},{5,6},{6,7},{8,9},{9,10},{10,11},{11... | collective-permute-start | bytes 36872 | tf_op jit(solution)/shard_map/ppermute | solution.py:17
  67.0 1.0 collective-permute-done.14
  67.9 0.2 fusion.312
  68.2 1.9 %collective-permute-start.16 = (f32[2,1,768]{2,1,0:T(1,128)S(1)}, f32[2,1,768]{2,1,0:T(1,128)S(1)}, u32[]{:S(2)}, u32[]{:S(2)}) collective-permute-start(f32[2,1,768]{2,1,0:T(1,128)S(1)} %pad_maximum_fusion.26), channel_id=1, source_target_pairs={{8,0},{16,8},{24,16},{9,1},{17,9},{25,17},{10,2},{18,10},{26,18},{... | collective-permute-start | bytes 18440 | tf_op jit(solution)/shard_map/ppermute | solution.py:17
  70.4 0.1 slice.1149
  70.6 3.0 %collective-permute-start.17 = (f32[2,32,48]{2,1,0:T(8,128)S(1)}, f32[2,32,48]{2,1,0:T(8,128)S(1)}, u32[]{:S(2)}, u32[]{:S(2)}) collective-permute-start(f32[2,32,48]{2,1,0:T(8,128)S(1)} %pad_maximum_fusion.14), channel_id=1, source_target_pairs={{1,0},{2,1},{3,2},{4,3},{5,4},{6,5},{7,6},{9,8},{10,9},{11,10},{12... | collective-permute-start | bytes 36872 | tf_op jit(solution)/shard_map/ppermute | solution.py:17
  73.7 2.7 %collective-permute-done.17 = f32[2,32,48]{2,1,0:T(8,128)S(1)} collective-permute-done((f32[2,32,48]{2,1,0:T(8,128)S(1)}, f32[2,32,48]{2,1,0:T(8,128)S(1)}, u32[]{:S(2)}, u32[]{:S(2)}) %collective-permute-start.17) | collective-permute-done | bytes 12320 | tf_op jit(solution)/shard_map/ppermute | solution.py:17
  76.4 0.1 fusion.107
  76.7 4.5 %collective-permute-start.19 = (f32[2,1,768]{2,1,0:T(1,128)S(1)}, f32[2,1,768]{2,1,0:T(1,128)S(1)}, u32[]{:S(2)}, u32[]{:S(2)}) collective-permute-start(f32[2,1,768]{2,1,0:T(1,128)S(1)} %pad_maximum_fusion.27), channel_id=1, source_target_pairs={{0,8},{8,16},{16,24},{1,9},{9,17},{17,25},{2,10},{10,18},{18,26},{... | collective-permute-start | bytes 18440 | tf_op jit(solution)/shard_map/ppermute | solution.py:17
  81.3 2.2 %collective-permute-start.18 = (f32[2,32,48]{2,1,0:T(8,128)S(1)}, f32[2,32,48]{2,1,0:T(8,128)S(1)}, u32[]{:S(2)}, u32[]{:S(2)}) collective-permute-start(f32[2,32,48]{2,1,0:T(8,128)S(1)} %pad_maximum_fusion.15), channel_id=1, source_target_pairs={{0,1},{1,2},{2,3},{3,4},{4,5},{5,6},{6,7},{8,9},{9,10},{10,11},{11... | collective-permute-start | bytes 36872 | tf_op jit(solution)/shard_map/ppermute | solution.py:17
  83.5 1.0 collective-permute-done.18
  84.5 0.2 fusion.313
  84.8 1.9 %collective-permute-start.20 = (f32[2,1,768]{2,1,0:T(1,128)S(1)}, f32[2,1,768]{2,1,0:T(1,128)S(1)}, u32[]{:S(2)}, u32[]{:S(2)}) collective-permute-start(f32[2,1,768]{2,1,0:T(1,128)S(1)} %pad_maximum_fusion.28), channel_id=1, source_target_pairs={{8,0},{16,8},{24,16},{9,1},{17,9},{25,17},{10,2},{18,10},{26,18},{... | collective-permute-start | bytes 18440 | tf_op jit(solution)/shard_map/ppermute | solution.py:17
  87.2 3.0 %collective-permute-start.21 = (f32[2,32,48]{2,1,0:T(8,128)S(1)}, f32[2,32,48]{2,1,0:T(8,128)S(1)}, u32[]{:S(2)}, u32[]{:S(2)}) collective-permute-start(f32[2,32,48]{2,1,0:T(8,128)S(1)} %pad_maximum_fusion.16), channel_id=1, source_target_pairs={{1,0},{2,1},{3,2},{4,3},{5,4},{6,5},{7,6},{9,8},{10,9},{11,10},{12... | collective-permute-start | bytes 36872 | tf_op jit(solution)/shard_map/ppermute | solution.py:17
  90.2 2.7 %collective-permute-done.21 = f32[2,32,48]{2,1,0:T(8,128)S(1)} collective-permute-done((f32[2,32,48]{2,1,0:T(8,128)S(1)}, f32[2,32,48]{2,1,0:T(8,128)S(1)}, u32[]{:S(2)}, u32[]{:S(2)}) %collective-permute-start.21) | collective-permute-done | bytes 12320 | tf_op jit(solution)/shard_map/ppermute | solution.py:17
  93.0 0.1 fusion.115
  93.2 4.5 %collective-permute-start.23 = (f32[2,1,768]{2,1,0:T(1,128)S(1)}, f32[2,1,768]{2,1,0:T(1,128)S(1)}, u32[]{:S(2)}, u32[]{:S(2)}) collective-permute-start(f32[2,1,768]{2,1,0:T(1,128)S(1)} %pad_maximum_fusion.29), channel_id=1, source_target_pairs={{0,8},{8,16},{16,24},{1,9},{9,17},{17,25},{2,10},{10,18},{18,26},{... | collective-permute-start | bytes 18440 | tf_op jit(solution)/shard_map/ppermute | solution.py:17
  97.8 2.2 %collective-permute-start.22 = (f32[2,32,48]{2,1,0:T(8,128)S(1)}, f32[2,32,48]{2,1,0:T(8,128)S(1)}, u32[]{:S(2)}, u32[]{:S(2)}) collective-permute-start(f32[2,32,48]{2,1,0:T(8,128)S(1)} %pad_maximum_fusion.17), channel_id=1, source_target_pairs={{0,1},{1,2},{2,3},{3,4},{4,5},{5,6},{6,7},{8,9},{9,10},{10,11},{11... | collective-permute-start | bytes 36872 | tf_op jit(solution)/shard_map/ppermute | solution.py:17
  100.0 1.0 collective-permute-done.22
  101.0 0.4 fusion.215
  101.4 2.0 %collective-permute-start.24 = (f32[8,768]{1,0:T(8,128)S(1)}, f32[8,768]{1,0:T(8,128)S(1)}, u32[]{:S(2)}, u32[]{:S(2)}) collective-permute-start(f32[8,768]{1,0:T(8,128)S(1)} %get-tuple-element.66), channel_id=1, source_target_pairs={{0,8},{8,16},{16,24},{1,9},{9,17},{17,25},{2,10},{10,18},{18,26},{... | collective-permute-start | bytes 73736 | tf_op jit(solution)/shard_map/ppermute | solution.py:25
  103.4 3.3 %collective-permute-start.25 = (f32[8,768]{1,0:T(8,128)S(1)}, f32[8,768]{1,0:T(8,128)S(1)}, u32[]{:S(2)}, u32[]{:S(2)}) collective-permute-start(f32[8,768]{1,0:T(8,128)S(1)} %get-tuple-element.67), channel_id=1, source_target_pairs={{8,0},{16,8},{24,16},{9,1},{17,9},{25,17},{10,2},{18,10},{26,18},{... | collective-permute-start | bytes 73736 | tf_op jit(solution)/shard_map/ppermute | solution.py:28
  106.7 0.7 pad_maximum_fusion.1
  107.4 1.5 %collective-permute-done.25 = f32[8,768]{1,0:T(8,128)S(1)} collective-permute-done((f32[8,768]{1,0:T(8,128)S(1)}, f32[8,768]{1,0:T(8,128)S(1)}, u32[]{:S(2)}, u32[]{:S(2)}) %collective-permute-start.25) | collective-permute-done | bytes 24608 | tf_op jit(solution)/shard_map/ppermute | solution.py:28
  108.9 0.2 fusion.123
  109.1 5.3 %collective-permute-start.26 = (f32[32,384]{1,0:T(8,128)S(1)}, f32[32,384]{1,0:T(8,128)S(1)}, u32[]{:S(2)}, u32[]{:S(2)}) collective-permute-start(f32[32,384]{1,0:T(8,128)S(1)} %get-tuple-element.64), channel_id=1, source_target_pairs={{0,1},{1,2},{2,3},{3,4},{4,5},{5,6},{6,7},{8,9},{9,10},{10,11},{11... | collective-permute-start | bytes 147464 | tf_op jit(solution)/shard_map/ppermute | solution.py:25
  114.4 1.9 %collective-permute-start.27 = (f32[32,384]{1,0:T(8,128)S(1)}, f32[32,384]{1,0:T(8,128)S(1)}, u32[]{:S(2)}, u32[]{:S(2)}) collective-permute-start(f32[32,384]{1,0:T(8,128)S(1)} %get-tuple-element.65), channel_id=1, source_target_pairs={{1,0},{2,1},{3,2},{4,3},{5,4},{6,5},{7,6},{9,8},{10,9},{11,10},{12... | collective-permute-start | bytes 147464 | tf_op jit(solution)/shard_map/ppermute | solution.py:28
  116.3 0.7 pad_maximum_fusion
  117.1 2.7 %collective-permute-done.27 = f32[32,384]{1,0:T(8,128)S(1)} collective-permute-done((f32[32,384]{1,0:T(8,128)S(1)}, f32[32,384]{1,0:T(8,128)S(1)}, u32[]{:S(2)}, u32[]{:S(2)}) %collective-permute-start.27) | collective-permute-done | bytes 49184 | tf_op jit(solution)/shard_map/ppermute | solution.py:28
  119.8 1.1 fusion.167
  (162 shorter events, 3.7 us)
Async XLA Ops:
  0.6 6.3 %copy-start.2 = (bf16[6,3,32,768]{3,2,1,0:T(8,128)(2,1)S(1)}, bf16[6,3,32,768]{3,2,1,0:T(8,128)(2,1)}, u32[]{:S(2)}) copy-start(bf16[6,3,32,768]{3,2,1,0:T(8,128)(2,1)} %param.7) | copy-start | bytes 2654212
  2.1 7.9 %collective-permute-start.1 = (f32[2,32,48]{2,1,0:T(8,128)S(1)}, f32[2,32,48]{2,1,0:T(8,128)S(1)}, u32[]{:S(2)}, u32[]{:S(2)}) collective-permute-start(f32[2,32,48]{2,1,0:T(8,128)S(1)} %pad_maximum_fusion.6), channel_id=1, source_target_pairs={{1,0},{2,1},{3,2},{4,3},{5,4},{6,5},{7,6},{9,8},{10,9},{11,10},{12... | collective-permute-start | bytes 36872 | tf_op jit(solution)/shard_map/ppermute | solution.py:17
  4.8 5.3 %collective-permute-start = (f32[2,1,768]{2,1,0:T(1,128)S(1)}, f32[2,1,768]{2,1,0:T(1,128)S(1)}, u32[]{:S(2)}, u32[]{:S(2)}) collective-permute-start(f32[2,1,768]{2,1,0:T(1,128)S(1)} %pad_maximum_fusion.18), channel_id=1, source_target_pairs={{8,0},{16,8},{24,16},{9,1},{17,9},{25,17},{10,2},{18,10},{26,18},{... | collective-permute-start | bytes 18440 | tf_op jit(solution)/shard_map/ppermute | solution.py:17
  7.5 2.6 %copy-start.3 = (f32[3,32,768]{2,1,0:T(8,128)S(1)}, f32[3,32,768]{2,1,0:T(8,128)}, u32[]{:S(2)}) copy-start(f32[3,32,768]{2,1,0:T(8,128)} %param.5) | copy-start | bytes 884740
  10.1 8.2 %copy-start = (f32[9,32,768]{2,1,0:T(8,128)S(1)}, f32[9,32,768]{2,1,0:T(8,128)}, u32[]{:S(2)}) copy-start(f32[9,32,768]{2,1,0:T(8,128)} %param.6) | copy-start | bytes 2654212
  10.1 8.2 %copy-start.1 = (f32[3,32,768]{2,1,0:T(8,128)S(1)}, f32[3,32,768]{2,1,0:T(8,128)}, u32[]{:S(2)}) copy-start(f32[3,32,768]{2,1,0:T(8,128)} %param.4) | copy-start | bytes 884740
  10.3 7.0 %collective-permute-start.3 = (f32[2,1,768]{2,1,0:T(1,128)S(1)}, f32[2,1,768]{2,1,0:T(1,128)S(1)}, u32[]{:S(2)}, u32[]{:S(2)}) collective-permute-start(f32[2,1,768]{2,1,0:T(1,128)S(1)} %pad_maximum_fusion.19), channel_id=1, source_target_pairs={{0,8},{8,16},{16,24},{1,9},{9,17},{17,25},{2,10},{10,18},{18,26},{... | collective-permute-start | bytes 18440 | tf_op jit(solution)/shard_map/ppermute | solution.py:17
  12.9 5.4 %collective-permute-start.2 = (f32[2,32,48]{2,1,0:T(8,128)S(1)}, f32[2,32,48]{2,1,0:T(8,128)S(1)}, u32[]{:S(2)}, u32[]{:S(2)}) collective-permute-start(f32[2,32,48]{2,1,0:T(8,128)S(1)} %pad_maximum_fusion.7), channel_id=1, source_target_pairs={{0,1},{1,2},{2,3},{3,4},{4,5},{5,6},{6,7},{8,9},{9,10},{10,11},{11... | collective-permute-start | bytes 36872 | tf_op jit(solution)/shard_map/ppermute | solution.py:17
  18.6 6.8 %collective-permute-start.4 = (f32[2,1,768]{2,1,0:T(1,128)S(1)}, f32[2,1,768]{2,1,0:T(1,128)S(1)}, u32[]{:S(2)}, u32[]{:S(2)}) collective-permute-start(f32[2,1,768]{2,1,0:T(1,128)S(1)} %pad_maximum_fusion.20), channel_id=1, source_target_pairs={{8,0},{16,8},{24,16},{9,1},{17,9},{25,17},{10,2},{18,10},{26,18},{... | collective-permute-start | bytes 18440 | tf_op jit(solution)/shard_map/ppermute | solution.py:17
  22.1 6.1 %collective-permute-start.5 = (f32[2,32,48]{2,1,0:T(8,128)S(1)}, f32[2,32,48]{2,1,0:T(8,128)S(1)}, u32[]{:S(2)}, u32[]{:S(2)}) collective-permute-start(f32[2,32,48]{2,1,0:T(8,128)S(1)} %pad_maximum_fusion.8), channel_id=1, source_target_pairs={{1,0},{2,1},{3,2},{4,3},{5,4},{6,5},{7,6},{9,8},{10,9},{11,10},{12... | collective-permute-start | bytes 36872 | tf_op jit(solution)/shard_map/ppermute | solution.py:17
  28.4 5.4 %collective-permute-start.7 = (f32[2,1,768]{2,1,0:T(1,128)S(1)}, f32[2,1,768]{2,1,0:T(1,128)S(1)}, u32[]{:S(2)}, u32[]{:S(2)}) collective-permute-start(f32[2,1,768]{2,1,0:T(1,128)S(1)} %pad_maximum_fusion.21), channel_id=1, source_target_pairs={{0,8},{8,16},{16,24},{1,9},{9,17},{17,25},{2,10},{10,18},{18,26},{... | collective-permute-start | bytes 18440 | tf_op jit(solution)/shard_map/ppermute | solution.py:17
  31.6 3.2 %collective-permute-start.6 = (f32[2,32,48]{2,1,0:T(8,128)S(1)}, f32[2,32,48]{2,1,0:T(8,128)S(1)}, u32[]{:S(2)}, u32[]{:S(2)}) collective-permute-start(f32[2,32,48]{2,1,0:T(8,128)S(1)} %pad_maximum_fusion.9), channel_id=1, source_target_pairs={{0,1},{1,2},{2,3},{3,4},{4,5},{5,6},{6,7},{8,9},{9,10},{10,11},{11... | collective-permute-start | bytes 36872 | tf_op jit(solution)/shard_map/ppermute | solution.py:17
  35.2 5.9 %collective-permute-start.8 = (f32[2,1,768]{2,1,0:T(1,128)S(1)}, f32[2,1,768]{2,1,0:T(1,128)S(1)}, u32[]{:S(2)}, u32[]{:S(2)}) collective-permute-start(f32[2,1,768]{2,1,0:T(1,128)S(1)} %pad_maximum_fusion.22), channel_id=1, source_target_pairs={{8,0},{16,8},{24,16},{9,1},{17,9},{25,17},{10,2},{18,10},{26,18},{... | collective-permute-start | bytes 18440 | tf_op jit(solution)/shard_map/ppermute | solution.py:17
  37.8 6.1 %collective-permute-start.9 = (f32[2,32,48]{2,1,0:T(8,128)S(1)}, f32[2,32,48]{2,1,0:T(8,128)S(1)}, u32[]{:S(2)}, u32[]{:S(2)}) collective-permute-start(f32[2,32,48]{2,1,0:T(8,128)S(1)} %pad_maximum_fusion.10), channel_id=1, source_target_pairs={{1,0},{2,1},{3,2},{4,3},{5,4},{6,5},{7,6},{9,8},{10,9},{11,10},{12... | collective-permute-start | bytes 36872 | tf_op jit(solution)/shard_map/ppermute | solution.py:17
  44.1 6.3 %collective-permute-start.11 = (f32[2,1,768]{2,1,0:T(1,128)S(1)}, f32[2,1,768]{2,1,0:T(1,128)S(1)}, u32[]{:S(2)}, u32[]{:S(2)}) collective-permute-start(f32[2,1,768]{2,1,0:T(1,128)S(1)} %pad_maximum_fusion.23), channel_id=1, source_target_pairs={{0,8},{8,16},{16,24},{1,9},{9,17},{17,25},{2,10},{10,18},{18,26},{... | collective-permute-start | bytes 18440 | tf_op jit(solution)/shard_map/ppermute | solution.py:17
  48.2 3.2 %collective-permute-start.10 = (f32[2,32,48]{2,1,0:T(8,128)S(1)}, f32[2,32,48]{2,1,0:T(8,128)S(1)}, u32[]{:S(2)}, u32[]{:S(2)}) collective-permute-start(f32[2,32,48]{2,1,0:T(8,128)S(1)} %pad_maximum_fusion.11), channel_id=1, source_target_pairs={{0,1},{1,2},{2,3},{3,4},{4,5},{5,6},{6,7},{8,9},{9,10},{10,11},{11... | collective-permute-start | bytes 36872 | tf_op jit(solution)/shard_map/ppermute | solution.py:17
  51.7 5.4 %collective-permute-start.12 = (f32[2,1,768]{2,1,0:T(1,128)S(1)}, f32[2,1,768]{2,1,0:T(1,128)S(1)}, u32[]{:S(2)}, u32[]{:S(2)}) collective-permute-start(f32[2,1,768]{2,1,0:T(1,128)S(1)} %pad_maximum_fusion.24), channel_id=1, source_target_pairs={{8,0},{16,8},{24,16},{9,1},{17,9},{25,17},{10,2},{18,10},{26,18},{... | collective-permute-start | bytes 18440 | tf_op jit(solution)/shard_map/ppermute | solution.py:17
  54.1 5.8 %collective-permute-start.13 = (f32[2,32,48]{2,1,0:T(8,128)S(1)}, f32[2,32,48]{2,1,0:T(8,128)S(1)}, u32[]{:S(2)}, u32[]{:S(2)}) collective-permute-start(f32[2,32,48]{2,1,0:T(8,128)S(1)} %pad_maximum_fusion.12), channel_id=1, source_target_pairs={{1,0},{2,1},{3,2},{4,3},{5,4},{6,5},{7,6},{9,8},{10,9},{11,10},{12... | collective-permute-start | bytes 36872 | tf_op jit(solution)/shard_map/ppermute | solution.py:17
  60.1 6.8 %collective-permute-start.15 = (f32[2,1,768]{2,1,0:T(1,128)S(1)}, f32[2,1,768]{2,1,0:T(1,128)S(1)}, u32[]{:S(2)}, u32[]{:S(2)}) collective-permute-start(f32[2,1,768]{2,1,0:T(1,128)S(1)} %pad_maximum_fusion.25), channel_id=1, source_target_pairs={{0,8},{8,16},{16,24},{1,9},{9,17},{17,25},{2,10},{10,18},{18,26},{... | collective-permute-start | bytes 18440 | tf_op jit(solution)/shard_map/ppermute | solution.py:17
  64.7 3.2 %collective-permute-start.14 = (f32[2,32,48]{2,1,0:T(8,128)S(1)}, f32[2,32,48]{2,1,0:T(8,128)S(1)}, u32[]{:S(2)}, u32[]{:S(2)}) collective-permute-start(f32[2,32,48]{2,1,0:T(8,128)S(1)} %pad_maximum_fusion.13), channel_id=1, source_target_pairs={{0,1},{1,2},{2,3},{3,4},{4,5},{5,6},{6,7},{8,9},{9,10},{10,11},{11... | collective-permute-start | bytes 36872 | tf_op jit(solution)/shard_map/ppermute | solution.py:17
  68.2 5.4 %collective-permute-start.16 = (f32[2,1,768]{2,1,0:T(1,128)S(1)}, f32[2,1,768]{2,1,0:T(1,128)S(1)}, u32[]{:S(2)}, u32[]{:S(2)}) collective-permute-start(f32[2,1,768]{2,1,0:T(1,128)S(1)} %pad_maximum_fusion.26), channel_id=1, source_target_pairs={{8,0},{16,8},{24,16},{9,1},{17,9},{25,17},{10,2},{18,10},{26,18},{... | collective-permute-start | bytes 18440 | tf_op jit(solution)/shard_map/ppermute | solution.py:17
  70.6 5.8 %collective-permute-start.17 = (f32[2,32,48]{2,1,0:T(8,128)S(1)}, f32[2,32,48]{2,1,0:T(8,128)S(1)}, u32[]{:S(2)}, u32[]{:S(2)}) collective-permute-start(f32[2,32,48]{2,1,0:T(8,128)S(1)} %pad_maximum_fusion.14), channel_id=1, source_target_pairs={{1,0},{2,1},{3,2},{4,3},{5,4},{6,5},{7,6},{9,8},{10,9},{11,10},{12... | collective-permute-start | bytes 36872 | tf_op jit(solution)/shard_map/ppermute | solution.py:17
  76.7 6.8 %collective-permute-start.19 = (f32[2,1,768]{2,1,0:T(1,128)S(1)}, f32[2,1,768]{2,1,0:T(1,128)S(1)}, u32[]{:S(2)}, u32[]{:S(2)}) collective-permute-start(f32[2,1,768]{2,1,0:T(1,128)S(1)} %pad_maximum_fusion.27), channel_id=1, source_target_pairs={{0,8},{8,16},{16,24},{1,9},{9,17},{17,25},{2,10},{10,18},{18,26},{... | collective-permute-start | bytes 18440 | tf_op jit(solution)/shard_map/ppermute | solution.py:17
  81.3 3.2 %collective-permute-start.18 = (f32[2,32,48]{2,1,0:T(8,128)S(1)}, f32[2,32,48]{2,1,0:T(8,128)S(1)}, u32[]{:S(2)}, u32[]{:S(2)}) collective-permute-start(f32[2,32,48]{2,1,0:T(8,128)S(1)} %pad_maximum_fusion.15), channel_id=1, source_target_pairs={{0,1},{1,2},{2,3},{3,4},{4,5},{5,6},{6,7},{8,9},{9,10},{10,11},{11... | collective-permute-start | bytes 36872 | tf_op jit(solution)/shard_map/ppermute | solution.py:17
  84.8 5.4 %collective-permute-start.20 = (f32[2,1,768]{2,1,0:T(1,128)S(1)}, f32[2,1,768]{2,1,0:T(1,128)S(1)}, u32[]{:S(2)}, u32[]{:S(2)}) collective-permute-start(f32[2,1,768]{2,1,0:T(1,128)S(1)} %pad_maximum_fusion.28), channel_id=1, source_target_pairs={{8,0},{16,8},{24,16},{9,1},{17,9},{25,17},{10,2},{18,10},{26,18},{... | collective-permute-start | bytes 18440 | tf_op jit(solution)/shard_map/ppermute | solution.py:17
  87.2 5.8 %collective-permute-start.21 = (f32[2,32,48]{2,1,0:T(8,128)S(1)}, f32[2,32,48]{2,1,0:T(8,128)S(1)}, u32[]{:S(2)}, u32[]{:S(2)}) collective-permute-start(f32[2,32,48]{2,1,0:T(8,128)S(1)} %pad_maximum_fusion.16), channel_id=1, source_target_pairs={{1,0},{2,1},{3,2},{4,3},{5,4},{6,5},{7,6},{9,8},{10,9},{11,10},{12... | collective-permute-start | bytes 36872 | tf_op jit(solution)/shard_map/ppermute | solution.py:17
  93.2 6.8 %collective-permute-start.23 = (f32[2,1,768]{2,1,0:T(1,128)S(1)}, f32[2,1,768]{2,1,0:T(1,128)S(1)}, u32[]{:S(2)}, u32[]{:S(2)}) collective-permute-start(f32[2,1,768]{2,1,0:T(1,128)S(1)} %pad_maximum_fusion.29), channel_id=1, source_target_pairs={{0,8},{8,16},{16,24},{1,9},{9,17},{17,25},{2,10},{10,18},{18,26},{... | collective-permute-start | bytes 18440 | tf_op jit(solution)/shard_map/ppermute | solution.py:17
  97.8 3.2 %collective-permute-start.22 = (f32[2,32,48]{2,1,0:T(8,128)S(1)}, f32[2,32,48]{2,1,0:T(8,128)S(1)}, u32[]{:S(2)}, u32[]{:S(2)}) collective-permute-start(f32[2,32,48]{2,1,0:T(8,128)S(1)} %pad_maximum_fusion.17), channel_id=1, source_target_pairs={{0,1},{1,2},{2,3},{3,4},{4,5},{5,6},{6,7},{8,9},{9,10},{10,11},{11... | collective-permute-start | bytes 36872 | tf_op jit(solution)/shard_map/ppermute | solution.py:17
  101.4 6.0 %collective-permute-start.24 = (f32[8,768]{1,0:T(8,128)S(1)}, f32[8,768]{1,0:T(8,128)S(1)}, u32[]{:S(2)}, u32[]{:S(2)}) collective-permute-start(f32[8,768]{1,0:T(8,128)S(1)} %get-tuple-element.66), channel_id=1, source_target_pairs={{0,8},{8,16},{16,24},{1,9},{9,17},{17,25},{2,10},{10,18},{18,26},{... | collective-permute-start | bytes 73736 | tf_op jit(solution)/shard_map/ppermute | solution.py:25
  103.4 5.5 %collective-permute-start.25 = (f32[8,768]{1,0:T(8,128)S(1)}, f32[8,768]{1,0:T(8,128)S(1)}, u32[]{:S(2)}, u32[]{:S(2)}) collective-permute-start(f32[8,768]{1,0:T(8,128)S(1)} %get-tuple-element.67), channel_id=1, source_target_pairs={{8,0},{16,8},{24,16},{9,1},{17,9},{25,17},{10,2},{18,10},{26,18},{... | collective-permute-start | bytes 73736 | tf_op jit(solution)/shard_map/ppermute | solution.py:28
  109.1 8.0 %collective-permute-start.26 = (f32[32,384]{1,0:T(8,128)S(1)}, f32[32,384]{1,0:T(8,128)S(1)}, u32[]{:S(2)}, u32[]{:S(2)}) collective-permute-start(f32[32,384]{1,0:T(8,128)S(1)} %get-tuple-element.64), channel_id=1, source_target_pairs={{0,1},{1,2},{2,3},{3,4},{4,5},{5,6},{6,7},{8,9},{9,10},{10,11},{11... | collective-permute-start | bytes 147464 | tf_op jit(solution)/shard_map/ppermute | solution.py:25
  114.4 5.4 %collective-permute-start.27 = (f32[32,384]{1,0:T(8,128)S(1)}, f32[32,384]{1,0:T(8,128)S(1)}, u32[]{:S(2)}, u32[]{:S(2)}) collective-permute-start(f32[32,384]{1,0:T(8,128)S(1)} %get-tuple-element.65), channel_id=1, source_target_pairs={{1,0},{2,1},{3,2},{4,3},{5,4},{6,5},{7,6},{9,8},{10,9},{11,10},{12... | collective-permute-start | bytes 147464 | tf_op jit(solution)/shard_map/ppermute | solution.py:28
where the time goes:
time: 123 us; the launch traced here: 121 us
  starting transfers between devices  82.5 us (67%)
  waiting for transfers between devices  26.1 us (21%)
  other arithmetic  7.06 us (6%)
  local copies, waits for them, and re-layouts  3.43 us (3%)
  between operations  1.85 us (2%)
    ppermute x24, starting transfers between devices, passed_along(): return lax.ppermute(block, axis, route)  70.1 us
    ppermute x24, waiting for transfers between devices, passed_along(): return lax.ppermute(block, axis, route)  21.9 us
    ppermute x2, starting transfers between devices, with_halo(): lax.ppermute(lax.slice_in_dim(block, block.shape[dim] - width, None, axis...  7.3 us
    ppermute x2, starting transfers between devices, with_halo(): lax.ppermute(lax.slice_in_dim(block, 0, width, axis=dim), axis, backward)  5.18 us
    ppermute x2, waiting for transfers between devices, with_halo(): lax.ppermute(lax.slice_in_dim(block, 0, width, axis=dim), axis, backward)  4.21 us
    add x11, other arithmetic, leapfrog(): mats[col] * fields_e[0] + mats[3 + col] * fields_e[1]  2.72 us
  transfers between devices with their start and end apart: 28, of which 14 were waited for; matrix products, arithmetic and copies ran while one was open for 4% of the time, Pallas kernels for 0%

commit v1 on v0

v1 whole, which is shorter than its diff:
```python
import jax
import jax.numpy as jnp
from jax import lax
from jax.sharding import PartitionSpec as P

NZ = 48
STEPS = 6
RADIUS = 8


courant = 0.45


def swap_pairs(count, first):
    pairs = []
    for i in range(first, count - 1, 2):
        pairs += [(i, i + 1), (i + 1, i)]
    return pairs


def swap(first, last, axis):
    count = lax.axis_size(axis)
    even = lax.axis_index(axis) % 2 == 0
    from_a = lax.ppermute(jnp.where(even, last, first), axis, swap_pairs(count, 0))
    from_b = lax.ppermute(jnp.where(even, first, last), axis, swap_pairs(count, 1))
    return jnp.where(even, from_b, from_a), jnp.where(even, from_a, from_b)


def tent(offset):
    return (RADIUS + 1.0 - abs(offset)) / (RADIUS + 1.0)


def coverage(places, length):
    total = jnp.zeros(places.shape, jnp.float32)
    for offset in range(-RADIUS, RADIUS + 1):
        inside = ((places + offset >= 0) & (places + offset < length)).astype(jnp.float32)
        total = total + tent(offset) * inside
    return total


def filter_rows(extended, tile_rows):
    result = tent(-RADIUS) * extended[0:tile_rows]
    for offset in range(-RADIUS + 1, RADIUS + 1):
        result = result + tent(offset) * extended[RADIUS + offset : RADIUS + offset + tile_rows]
    return result


def filter_columns(extended, tile_width):
    result = tent(-RADIUS) * extended[:, 0:tile_width]
    for offset in range(-RADIUS + 1, RADIUS + 1):
        begin = (RADIUS + offset) * NZ
        result = result + tent(offset) * extended[:, begin : begin + tile_width]
    return result


def leapfrog(fields_e, fields_h, mats, upper_mask, lower_mask, inside):
    rows, width = fields_e[0].shape
    zero_row = jnp.zeros((1, width), jnp.float32)
    zero_y = jnp.zeros((rows, NZ), jnp.float32)
    zero_z = jnp.zeros((rows, 1), jnp.float32)

    def next_x(field):
        return jnp.concatenate([field[1:], zero_row], axis=0) - field

    def next_y(field):
        return jnp.concatenate([field[:, NZ:], zero_y], axis=1) - field

    def next_z(field):
        return jnp.concatenate([field[:, 1:], zero_z], axis=1) * upper_mask - field

    def prev_x(field):
        return field - jnp.concatenate([zero_row, field[:-1]], axis=0)

    def prev_y(field):
        return field - jnp.concatenate([zero_y, field[:, :-NZ]], axis=1)

    def prev_z(field):
        return field - jnp.concatenate([zero_z, field[:, :-1]], axis=1) * lower_mask

    g = [
        mats[col] * fields_e[0] + mats[3 + col] * fields_e[1] + mats[6 + col] * fields_e[2]
        for col in range(3)
    ]
    fields_h = [
        (fields_h[0] - courant * (next_y(g[2]) - next_z(g[1]))) * inside,
        (fields_h[1] - courant * (next_z(g[0]) - next_x(g[2]))) * inside,
        (fields_h[2] - courant * (next_x(g[1]) - next_y(g[0]))) * inside,
    ]
    h = fields_h
    fields_e = [
        fields_e[0] + courant * (prev_y(h[2]) - prev_z(h[1])),
        fields_e[1] + courant * (prev_z(h[0]) - prev_x(h[2])),
        fields_e[2] + courant * (prev_x(h[1]) - prev_y(h[0])),
    ]
    return fields_e, fields_h


def shards(electric, magnetic, tensor, saved):
    tile_rows, tile_width = electric.shape[1:]
    tile_cols = tile_width // NZ
    halo = STEPS
    side = halo * NZ
    parts = [*electric, *magnetic, *tensor]
    n = len(parts)

    def stack_rows(begin):
        return jnp.concatenate([p[begin : begin + halo] for p in parts], axis=0)

    def stack_lanes(begin):
        return jnp.concatenate([p[:, begin : begin + side] for p in parts], axis=1)

    low_x, high_x = swap(stack_rows(0), stack_rows(tile_rows - halo), "gx")
    low_y, high_y = swap(stack_lanes(0), stack_lanes(tile_width - side), "gy")
    both_x = [low_x, high_x]

    def corners(begin):
        return jnp.concatenate([b[:, begin : begin + side] for b in both_x], axis=1)

    low_c, high_c = swap(corners(0), corners(tile_width - side), "gy")

    def extend(k):
        rows = slice(k * halo, (k + 1) * halo)
        lanes = slice(k * side, (k + 1) * side)
        mid = jnp.concatenate([low_x[rows], parts[k], high_x[rows]], axis=0)
        low = jnp.concatenate([low_c[rows, :side], low_y[:, lanes], low_c[rows, side:]], axis=0)
        high = jnp.concatenate([high_c[rows, :side], high_y[:, lanes], high_c[rows, side:]], axis=0)
        return jnp.concatenate([low, mid, high], axis=1)

    ext = [extend(k) for k in range(n)]
    fields_e, fields_h, mats = ext[0:3], ext[3:6], ext[6:15]
    shape = ext[0].shape
    lane = lax.broadcasted_iota(jnp.int32, shape, 1)
    row = lax.broadcasted_iota(jnp.int32, shape, 0)
    depth = lane % NZ
    upper_mask = (depth != NZ - 1).astype(jnp.float32)
    lower_mask = (depth != 0).astype(jnp.float32)
    inside = (
        (row + lax.axis_index("gx") * tile_rows >= halo)
        & (lane + lax.axis_index("gy") * tile_width >= side)
    ).astype(jnp.float32)

    def own(x):
        return x[halo : halo + tile_rows, side : side + tile_width]

    corr = jnp.zeros((tile_rows, tile_width), jnp.float32)
    for section in range(STEPS):
        fields_e, fields_h = leapfrog(fields_e, fields_h, mats, upper_mask, lower_mask, inside)
        frame = saved[section].astype(jnp.float32)
        corr = corr + (own(fields_e[0]) * frame[0] + own(fields_e[1]) * frame[1] + own(fields_e[2]) * frame[2])

    row_places = lax.axis_index("gx") * tile_rows + jnp.arange(tile_rows, dtype=jnp.int32)
    col_places = lax.axis_index("gy") * tile_cols + jnp.arange(tile_cols, dtype=jnp.int32)
    cover_rows = coverage(row_places, lax.axis_size("gx") * tile_rows)
    cover_cols = jnp.repeat(coverage(col_places, lax.axis_size("gy") * tile_cols), NZ)
    cover = cover_rows[:, None] * cover_cols[None, :]
    scaled = corr / cover
    low, high = swap(scaled[:RADIUS], scaled[-RADIUS:], "gx")
    across = filter_rows(jnp.concatenate([low, scaled, high], axis=0), tile_rows)
    reach = RADIUS * NZ
    low, high = swap(across[:, :reach], across[:, -reach:], "gy")
    gradient = filter_columns(jnp.concatenate([low, across, high], axis=1), tile_width)
    return (jnp.stack([own(x) for x in fields_e]), jnp.stack([own(x) for x in fields_h]), gradient)


def solution(mesh):
    in_specs = (
        P(None, "gx", "gy"),
        P(None, "gx", "gy"),
        P(None, "gx", "gy"),
        P(None, None, "gx", "gy"),
    )
    out_specs = (P(None, "gx", "gy"), P(None, "gx", "gy"), P("gx", "gy"))
    return jax.shard_map(shards, mesh=mesh, in_specs=in_specs, out_specs=out_specs, check_vma=False)
```

time: 123 us -> 105 us (0.85)
  starting transfers between devices: 82.5 us -> 19.8 us
  local copies, waits for them, and re-layouts: 3.43 us -> 41 us
  other arithmetic: 7.06 us -> 28 us
  waiting for transfers between devices: 26.1 us -> 12.9 us
    ppermute x28 -> x10, starting transfers between devices: 82.5 us -> 19.8 us  [the longest x5 19.4 us: swap(): lax.ppermute(jnp.where(even, first, last), axis, swap_pairs(count, 1))]
    slice x38 -> x56, local copies, waits for them, and re-layouts: 2.17 us -> 16.2 us  [the longest x8 3.86 us: stack_lanes(): return jnp.concatenate([p[:, begin:begin + side] for p in parts], axis=1)]
    ppermute x28 -> x10, waiting for transfers between devices: 26.1 us -> 12.9 us  [the longest x5 8.12 us: swap(): lax.ppermute(jnp.where(even, first, last), axis, swap_pairs(count, 1))]
    concatenate x0 -> x19, local copies, waits for them, and re-layouts: none -> 12.8 us  [the longest x15 8.65 us: extend(): return jnp.concatenate([low, mid, high], axis=1)]
    unnamed x8 -> x112, local copies, waits for them, and re-layouts: 0.02 us -> 9.63 us
    concatenate x0 -> x45, other arithmetic: none -> 8.86 us  [the longest x15 3.78 us: extend(): jnp.concatenate([high_c[rows, :side], high_y[:, lanes], high_c[rows, side...]
    select_n x0 -> x10, other arithmetic: none -> 4.37 us  [the longest x5 2.35 us: swap(): return (jnp.where(even, from_b, from_a), jnp.where(even, from_a, from_b))]
    mul x0 -> x6, other arithmetic: none -> 3.47 us  [leapfrog(): (fields_h[0] - courant * (next_y(g[2]) - next_z(g[1]))) * inside]
  transfers between devices with their start and end apart: 28 -> 10, of which waited for: 14 -> 6; matrix products, arithmetic and copies ran while one was open for 4% -> 14% of each run, Pallas kernels for 0% -> 0%
where the time goes in v1:
time: 105 us; the launch traced here: 104 us
  local copies, waits for them, and re-layouts  41 us (39%)
  other arithmetic  28 us (27%)
  starting transfers between devices  19.8 us (19%)
  waiting for transfers between devices  12.9 us (12%)
  between operations  1.83 us (2%)
    ppermute x5, starting transfers between devices, swap(): lax.ppermute(jnp.where(even, first, last), axis, swap_pairs(count, 1))  19.4 us
    unnamed x112, local copies, waits for them, and re-layouts  9.63 us
    concatenate x15, local copies, waits for them, and re-layouts, extend(): return jnp.concatenate([low, mid, high], axis=1)  8.65 us
    ppermute x5, waiting for transfers between devices, swap(): lax.ppermute(jnp.where(even, first, last), axis, swap_pairs(count, 1))  8.12 us
    ppermute x5, waiting for transfers between devices, swap(): lax.ppermute(jnp.where(even, last, first), axis, swap_pairs(count, 0))  4.78 us
    add x11, other arithmetic, leapfrog(): mats[col] * fields_e[0] + mats[3 + col] * fields_e[1]  4.42 us
    slice x8, local copies, waits for them, and re-layouts, stack_lanes(): return jnp.concatenate([p[:, begin:begin + side] for p in parts], axis=1)  3.86 us
    concatenate x15, other arithmetic, extend(): jnp.concatenate([high_c[rows, :side], high_y[:, lanes], high_c[rows, side...  3.78 us
  transfers between devices with their start and end apart: 10, of which 6 were waited for; matrix products, arithmetic and copies ran while one was open for 14% of the time, Pallas kernels for 0%

profile of v1, /device:TPU:11, one launch (start us, length us, event | category | flops | bytes accessed | tf_op | source)
XLA Modules:
  0.0 103.6 jit_solution(5573127457815845644)
XLA Ops:
  0.6 1.4 %slice_bitcast_fusion.18 = (f32[32,768]{1,0:T(8,128)S(1)}, f32[32,768]{1,0:T(8,128)S(1)}, f32[32,768]{1,0:T(8,128)S(1)}, f32[32,768]{1,0:T(8,128)S(1)}, f32[32,7...) fusion(f32[9,32,768]{2,1,0:T(8,128)} %param.6), kind=kLoop, calls=%fused_computation.373 | loop fusion | bytes 1769472 | tf_op jit(solution)/shard_map/unstack | solution.py:103
  2.1 0.9 copy-done.11
  3.0 0.7 fusion.264
  4.0 0.7 fusion.256
  4.7 0.7 fusion.258
  5.4 0.7 fusion.259
  6.2 0.7 fusion.262
  6.9 1.1 %concatenate.460 = f32[32,4320]{1,0:T(8,128)S(1)} concatenate(f32[32,288]{1,0:T(8,128)} %get-tuple-element.280, f32[32,288]{1,0:T(8,128)} %get-tuple-element.289, f32[32,288]{1,0:T(8,128)} %get-tuple-element.276, f32[32,288]{1,0:T(8,128)S(1)} %get-tuple-element.301, f32[32,288]{1,0:T(8,128)} %get-tuple-element.291, f32[32,288]{1,0:T(8,128)S(1)} %get-tuple-element.270, ...), dimensions={1} | concatenate | bytes 1105920 | tf_op jit(solution)/shard_map/concatenate | solution.py:110
  8.0 1.2 %concatenate.461 = f32[32,4320]{1,0:T(8,128)S(1)} concatenate(f32[32,288]{1,0:T(8,128)} %get-tuple-element.279, f32[32,288]{1,0:T(8,128)} %get-tuple-element.290, f32[32,288]{1,0:T(8,128)} %get-tuple-element.275, f32[32,288]{1,0:T(8,128)} %get-tuple-element.302, f32[32,288]{1,0:T(8,128)} %get-tuple-element.292, f32[32,288]{1,0:T(8,128)} %get-tuple-element.269, ...), dimensions={1} | concatenate | bytes 1105920 | tf_op jit(solution)/shard_map/concatenate | solution.py:110
  9.3 1.1 %broadcast_select_fusion.2 = (f32[32,4320]{1,0:T(8,128)}, f32[32,4320]{1,0:T(8,128)}) fusion(f32[32,4320]{1,0:T(8,128)S(1)} %concatenate.461, f32[32,4320]{1,0:T(8,128)S(1)} %concatenate.460, pred[]{:T(512)S(6)} %eq.17), kind=kLoop, calls=%fused_computation.64 | loop fusion | flops 276480 | bytes 2211841 | tf_op jit(solution)/shard_map/jit(_where)/select_n | solution.py:24
  10.4 3.8 %collective-permute-start.4 = (f32[32,4320]{1,0:T(8,128)}, f32[32,4320]{1,0:T(8,128)}, u32[]{:S(2)}, u32[]{:S(2)}) collective-permute-start(f32[32,4320]{1,0:T(8,128)} %get-tuple-element.30), channel_id=1, source_target_pairs={{1,2},{2,1},{3,4},{4,3},{5,6},{6,5},{9,10},{10,9},{11,12},{12,11},... | collective-permute-start | bytes 1658888 | tf_op jit(solution)/shard_map/ppermute | solution.py:25
  14.3 0.9 concatenate.457
  15.2 0.9 concatenate.456
  16.1 0.8 broadcast_select_fusion.7
  16.9 3.1 %collective-permute-start = (f32[90,768]{1,0:T(8,128)}, f32[90,768]{1,0:T(8,128)S(1)}, u32[]{:S(2)}, u32[]{:S(2)}) collective-permute-start(f32[90,768]{1,0:T(8,128)} %get-tuple-element.81), channel_id=1, source_target_pairs={{8,16},{16,8},{9,17},{17,9},{10,18},{18,10},{11,19},{19,11},{12,20... | collective-permute-start | bytes 829448 | tf_op jit(solution)/shard_map/ppermute | solution.py:25
  21.4 0.7 mul.853
  22.0 1.2 %slice_convert_fusion.5 = (f32[1,3,32,768]{3,2,1,0:T(8,128)}, f32[1,3,32,768]{3,2,1,0:T(8,128)}, f32[1,3,32,768]{3,2,1,0:T(8,128)}, f32[1,3,32,768]{3,2,1,0:T(8,...) fusion(bf16[6,3,32,768]{3,2,1,0:T(8,128)(2,1)S(1)} %copy-done.9), kind=kLoop, calls=%fused_computation.199 | loop fusion | flops 442368 | bytes 2654208 | tf_op jit(solution)/shard_map/convert_element_type | solution.py:148
  23.3 4.7 %collective-permute-done = f32[90,768]{1,0:T(8,128)S(1)} collective-permute-done((f32[90,768]{1,0:T(8,128)}, f32[90,768]{1,0:T(8,128)S(1)}, u32[]{:S(2)}, u32[]{:S(2)}) %collective-permute-start) | collective-permute-done | bytes 276512 | tf_op jit(solution)/shard_map/ppermute | solution.py:25
  28.0 4.4 %collective-permute-done.1 = f32[90,768]{1,0:T(8,128)} collective-permute-done((f32[90,768]{1,0:T(8,128)S(1)}, f32[90,768]{1,0:T(8,128)}, u32[]{:S(2)}, u32[]{:S(2)}) %collective-permute-start.1) | collective-permute-done | bytes 276512 | tf_op jit(solution)/shard_map/ppermute | solution.py:24
  32.4 1.0 broadcast_select_fusion.5
  33.8 4.6 %collective-permute-start.2 = (f32[90,576]{1,0:T(8,128)S(1)}, f32[90,576]{1,0:T(8,128)S(1)}, u32[]{:S(2)}, u32[]{:S(2)}) collective-permute-start(f32[90,576]{1,0:T(8,128)S(1)} %get-tuple-element.78), channel_id=1, source_target_pairs={{1,2},{2,1},{3,4},{4,3},{5,6},{6,5},{9,10},{10,9},{11,12},{12,11},... | collective-permute-start | bytes 622088 | tf_op jit(solution)/shard_map/ppermute | solution.py:25
  38.5 0.7 pad_maximum_fusion.5
  39.2 0.7 pad_maximum_fusion.14
  40.0 0.7 pad_maximum_fusion.8
  40.9 0.7 pad_maximum_fusion.18
  41.5 0.7 collective-permute-done.2
  42.9 0.7 fusion.249
  43.6 0.7 fusion.246
  44.4 0.7 fusion.247
  45.1 1.3 %broadcast_select_fusion = (f32[32,4320]{1,0:T(8,128)S(1)}, f32[32,4320]{1,0:T(8,128)S(1)}) fusion(f32[32,4320]{1,0:T(8,128)} %collective-permute-done.5, f32[32,4320]{1,0:T(8,128)} %collective-permute-done.4, pred[]{:T(512)S(6)} %eq.17), kind=kLoop, calls=%fused_computation.62 | loop fusion | flops 276480 | bytes 2211841 | tf_op jit(solution)/shard_map/jit(_where)/select_n | solution.py:26
  46.4 0.8 fusion.240
  47.2 0.8 fusion.241
  50.0 0.7 copy-done.26
  51.4 0.7 copy-done.52
  52.2 0.9 concatenate.489
  53.0 0.7 copy-done.51
  53.9 0.7 copy-done.24
  54.7 0.8 concatenate.465
  55.5 0.7 copy-done.46
  57.0 0.8 copy-done.19
  58.6 0.8 copy-done.18
  59.6 1.3 %multiply_add_fusion.32 = (f32[44,1344]{1,0:T(8,128)S(1)}, f32[44,1344]{1,0:T(8,128)S(1)}, f32[44,1344]{1,0:T(8,128)S(1)}) fusion(f32[44,1344]{1,0:T(8,128)S(1)} %concatenate.485, f32[44,1344]{1,0:T(8,128)} %concatenate.489, f32[44,1344]{1,0:T(8,128)S(1)} %concatenate.477, f32[44,1344]{1,0:T(8,128)S(1)} %concatenate.481, f32[44,1344]{1,0:T(8,128)S(1)} %concatenate.473, ...), kind=kLoop, calls=%fused_computation.146 | loop fusion | flops 887040 | bytes 3548160 | tf_op jit(solution)/shard_map/add | solution.py:81
  60.8 0.8 slice.1666
  61.7 0.8 slice.1676
  62.5 0.7 slice.1701
  63.2 0.9 slice.1711
  64.1 0.7 slice.1641
  64.8 0.8 slice.1712
  66.5 0.6 pad_maximum_fusion.25
  67.1 1.8 %concatenate.469 = f32[44,1344]{1,0:T(8,128)} concatenate(f32[44,288]{1,0:T(8,128)} %pad_maximum_fusion.25, f32[44,768]{1,0:T(8,128)} %pad_maximum_fusion.5, f32[44,288]{1,0:T(8,128)} %pad_maximum_fusion.26), dimensions={1} | concatenate | bytes 473088 | tf_op jit(solution)/shard_map/concatenate | solution.py:127
  69.0 1.5 %pad_maximum_fusion.44 = f32[44,288]{1,0:T(8,128)} fusion(f32[6,288]{1,0:T(8,128)S(1)} %copy-done.31, f32[32,288]{1,0:T(8,128)} %get-tuple-element.87, f32[6,288]{1,0:T(8,128)} %get-tuple-element.194), kind=kLoop, calls=%fused_computation.412 | loop fusion | flops 25344 | bytes 101376 | tf_op jit(solution)/shard_map/concatenate | solution.py:126
  70.5 0.6 pad_maximum_fusion.43
  71.1 1.8 %concatenate.508 = f32[44,1344]{1,0:T(8,128)} concatenate(f32[44,288]{1,0:T(8,128)} %pad_maximum_fusion.43, f32[44,768]{1,0:T(8,128)} %pad_maximum_fusion.14, f32[44,288]{1,0:T(8,128)} %pad_maximum_fusion.44), dimensions={1} | concatenate | bytes 473088 | tf_op jit(solution)/shard_map/concatenate | solution.py:127
  73.0 1.5 %pad_maximum_fusion.52 = f32[44,288]{1,0:T(8,128)} fusion(f32[6,288]{1,0:T(8,128)} %get-tuple-element.186, f32[32,288]{1,0:T(8,128)} %get-tuple-element.83, f32[6,288]{1,0:T(8,128)S(1)} %copy-done.30), kind=kLoop, calls=%fused_computation.420 | loop fusion | flops 25344 | bytes 101376 | tf_op jit(solution)/shard_map/concatenate | solution.py:126
  75.1 1.8 %concatenate.527 = f32[44,1344]{1,0:T(8,128)} concatenate(f32[44,288]{1,0:T(8,128)} %pad_maximum_fusion.51, f32[44,768]{1,0:T(8,128)} %pad_maximum_fusion.18, f32[44,288]{1,0:T(8,128)} %pad_maximum_fusion.52), dimensions={1} | concatenate | bytes 473088 | tf_op jit(solution)/shard_map/concatenate | solution.py:127
  76.9 1.9 %and_select_fusion.15 = (f32[44,1344]{1,0:T(8,128)S(1)}, f32[44,1344]{1,0:T(8,128)S(1)}, f32[44,1344]{1,0:T(8,128)S(1)}) fusion(f32[44,1344]{1,0:T(8,128)} %concatenate.527, f32[44,1344]{1,0:T(8,128)S(1)} %get-tuple-element.74, f32[44,1343]{1,0:T(8,128)} %slice.1712, f32[44,1344]{1,0:T(8,128)S(1)} %get-tuple-element.75, f32[44,1296]{1,0:T(8,128)} %slice.1711, ...), kind=kLoop, calls=%fused_computation.15 | loop fusion | flops 1360128 | bytes 3533644 | tf_op jit(solution)/shard_map/mul | solution.py:85
  87.9 1.7 %fusion.157 = (f32[32,768]{1,0:T(8,128)S(1)}, f32[32,768]{1,0:T(8,128)S(1)}, f32[32,768]{1,0:T(8,128)S(1)}, f32[32,768]{1,0:T(8,128)S(1)}) fusion(f32[1,3,32,768]{3,2,1,0:T(8,128)S(1)} %copy-done.7, f32[1,3,32,768]{3,2,1,0:T(8,128)S(1)} %copy-done.8, f32[1,3,32,768]{3,2,1,0:T(8,128)S(1)} %copy-done.4, f32[44,1344]{1,0:T(8,128)S(1)} %get-tuple-element.14, ...), kind=kLoop, calls=%fused_computation.306 | loop fusion | flops 1327104 | bytes 5351200 | tf_op jit(solution)/shard_map/div | solution.py:156
  89.6 3.1 %collective-permute-start.6 = (f32[8,768]{1,0:T(8,128)S(1)}, f32[8,768]{1,0:T(8,128)S(1)}, u32[]{:S(2)}, u32[]{:S(2)}) collective-permute-start(f32[8,768]{1,0:T(8,128)S(1)} %get-tuple-element.249), channel_id=1, source_target_pairs={{8,16},{16,8},{9,17},{17,9},{10,18},{18,10},{11,19},{19,11},{12,20... | collective-permute-start | bytes 73736 | tf_op jit(solution)/shard_map/ppermute | solution.py:25
  92.7 0.7 pad_maximum_fusion.1
  93.5 1.6 %collective-permute-done.6 = f32[8,768]{1,0:T(8,128)S(1)} collective-permute-done((f32[8,768]{1,0:T(8,128)S(1)}, f32[8,768]{1,0:T(8,128)S(1)}, u32[]{:S(2)}, u32[]{:S(2)}) %collective-permute-start.6) | collective-permute-done | bytes 24608 | tf_op jit(solution)/shard_map/ppermute | solution.py:25
  95.6 4.9 %collective-permute-start.8 = (f32[32,384]{1,0:T(8,128)S(1)}, f32[32,384]{1,0:T(8,128)S(1)}, u32[]{:S(2)}, u32[]{:S(2)}) collective-permute-start(f32[32,384]{1,0:T(8,128)S(1)} %get-tuple-element.247), channel_id=1, source_target_pairs={{1,2},{2,1},{3,4},{4,3},{5,6},{6,5},{9,10},{10,9},{11,12},{12,11},... | collective-permute-start | bytes 147464 | tf_op jit(solution)/shard_map/ppermute | solution.py:25
  100.6 0.7 pad_maximum_fusion
  101.3 1.1 %collective-permute-done.8 = f32[32,384]{1,0:T(8,128)S(1)} collective-permute-done((f32[32,384]{1,0:T(8,128)S(1)}, f32[32,384]{1,0:T(8,128)S(1)}, u32[]{:S(2)}, u32[]{:S(2)}) %collective-permute-start.8) | collective-permute-done | bytes 49184 | tf_op jit(solution)/shard_map/ppermute | solution.py:25
  102.5 1.1 %fusion.109 = f32[32,768]{1,0:T(8,128)} fusion(f32[32,768]{1,0:T(8,128)S(1)} %fusion.65, f32[32,384]{1,0:T(8,128)S(1)} %get-tuple-element.246, f32[32,384]{1,0:T(8,128)S(1)} %get-tuple-element.245), kind=kLoop, calls=%fused_computation.253 | loop fusion | flops 1179648 | bytes 294912 | tf_op jit(solution)/shard_map/add | solution.py:52
  (235 shorter events, 18.6 us)
Async XLA Ops:
  0.6 1.4 %copy-start.10 = (f32[3,32,768]{2,1,0:T(8,128)S(1)}, f32[3,32,768]{2,1,0:T(8,128)}, u32[]{:S(2)}) copy-start(f32[3,32,768]{2,1,0:T(8,128)} %param.5) | copy-start | bytes 884740
  2.0 1.0 copy-start.11
  9.3 5.0 %copy-start.2 = (f32[9,32,768]{2,1,0:T(8,128)S(1)}, f32[9,32,768]{2,1,0:T(8,128)}, u32[]{:S(2)}) copy-start(f32[9,32,768]{2,1,0:T(8,128)} %param.6) | copy-start | bytes 2654212
  10.4 34.7 %collective-permute-start.4 = (f32[32,4320]{1,0:T(8,128)}, f32[32,4320]{1,0:T(8,128)}, u32[]{:S(2)}, u32[]{:S(2)}) collective-permute-start(f32[32,4320]{1,0:T(8,128)} %get-tuple-element.30), channel_id=1, source_target_pairs={{1,2},{2,1},{3,4},{4,3},{5,6},{6,5},{9,10},{10,9},{11,12},{12,11},... | collective-permute-start | bytes 1658888 | tf_op jit(solution)/shard_map/ppermute | solution.py:25
  14.1 31.0 %collective-permute-start.5 = (f32[32,4320]{1,0:T(8,128)}, f32[32,4320]{1,0:T(8,128)}, u32[]{:S(2)}, u32[]{:S(2)}) collective-permute-start(f32[32,4320]{1,0:T(8,128)} %get-tuple-element.29), channel_id=1, source_target_pairs={{0,1},{1,0},{2,3},{3,2},{4,5},{5,4},{6,7},{7,6},{8,9},{9,8},{10,11... | collective-permute-start | bytes 1658888 | tf_op jit(solution)/shard_map/ppermute | solution.py:24
  15.2 6.8 %copy-start.9 = (bf16[6,3,32,768]{3,2,1,0:T(8,128)(2,1)S(1)}, bf16[6,3,32,768]{3,2,1,0:T(8,128)(2,1)}, u32[]{:S(2)}) copy-start(bf16[6,3,32,768]{3,2,1,0:T(8,128)(2,1)} %param.7) | copy-start | bytes 2654212
  16.9 11.1 %collective-permute-start = (f32[90,768]{1,0:T(8,128)}, f32[90,768]{1,0:T(8,128)S(1)}, u32[]{:S(2)}, u32[]{:S(2)}) collective-permute-start(f32[90,768]{1,0:T(8,128)} %get-tuple-element.81), channel_id=1, source_target_pairs={{8,16},{16,8},{9,17},{17,9},{10,18},{18,10},{11,19},{19,11},{12,20... | collective-permute-start | bytes 829448 | tf_op jit(solution)/shard_map/ppermute | solution.py:25
  20.0 12.4 %collective-permute-start.1 = (f32[90,768]{1,0:T(8,128)S(1)}, f32[90,768]{1,0:T(8,128)}, u32[]{:S(2)}, u32[]{:S(2)}) collective-permute-start(f32[90,768]{1,0:T(8,128)S(1)} %get-tuple-element.82), channel_id=1, source_target_pairs={{0,8},{8,0},{16,24},{24,16},{1,9},{9,1},{17,25},{25,17},{2,10},{10... | collective-permute-start | bytes 829448 | tf_op jit(solution)/shard_map/ppermute | solution.py:24
  33.8 8.5 %collective-permute-start.2 = (f32[90,576]{1,0:T(8,128)S(1)}, f32[90,576]{1,0:T(8,128)S(1)}, u32[]{:S(2)}, u32[]{:S(2)}) collective-permute-start(f32[90,576]{1,0:T(8,128)S(1)} %get-tuple-element.78), channel_id=1, source_target_pairs={{1,2},{2,1},{3,4},{4,3},{5,6},{6,5},{9,10},{10,9},{11,12},{12,11},... | collective-permute-start | bytes 622088 | tf_op jit(solution)/shard_map/ppermute | solution.py:25
  38.4 3.8 %collective-permute-start.3 = (f32[90,576]{1,0:T(8,128)S(1)}, f32[90,576]{1,0:T(8,128)S(1)}, u32[]{:S(2)}, u32[]{:S(2)}) collective-permute-start(f32[90,576]{1,0:T(8,128)S(1)} %get-tuple-element.77), channel_id=1, source_target_pairs={{0,1},{1,0},{2,3},{3,2},{4,5},{5,4},{6,7},{7,6},{8,9},{9,8},{10,11... | collective-permute-start | bytes 622088 | tf_op jit(solution)/shard_map/ppermute | solution.py:24
  48.7 0.8 copy-start.20
  48.7 0.8 copy-start.28
  48.7 0.8 copy-start.29
  48.9 0.9 copy-start.12
  50.0 0.7 copy-start.26
  50.0 0.7 copy-start.27
  50.7 0.7 copy-start.49
  50.7 0.7 copy-start.50
  51.4 0.7 copy-start.53
  52.2 0.9 copy-start.48
  53.9 0.7 copy-start.24
  53.9 0.7 copy-start.25
  54.6 0.8 copy-start.42
  54.7 0.8 copy-start.43
  55.5 0.7 copy-start.46
  55.5 0.7 copy-start.47
  56.2 0.7 copy-start.38
  56.2 0.7 copy-start.39
  57.0 0.8 copy-start.19
  57.0 0.8 copy-start.44
  57.0 0.8 copy-start.45
  57.8 0.8 copy-start.17
  57.8 0.8 copy-start.36
  57.8 0.8 copy-start.37
  58.6 0.8 copy-start.18
  58.6 0.8 copy-start.40
  58.6 0.8 copy-start.41
  64.8 0.9 copy-start.14
  64.8 0.9 copy-start.21
  65.7 0.8 copy-start.16
  65.7 0.8 copy-start.22
  65.7 0.8 copy-start.23
  67.1 1.8 %copy-start.31 = (f32[6,288]{1,0:T(8,128)S(1)}, f32[6,288]{1,0:T(8,128)}, u32[]{:S(2)}) copy-start(f32[6,288]{1,0:T(8,128)} %get-tuple-element.193) | copy-start | bytes 20740
  69.0 1.5 %copy-start.15 = (f32[32,288]{1,0:T(8,128)S(1)}, f32[32,288]{1,0:T(8,128)}, u32[]{:S(2)}) copy-start(f32[32,288]{1,0:T(8,128)} %get-tuple-element.102) | copy-start | bytes 110596
  69.0 1.5 %copy-start.34 = (f32[6,288]{1,0:T(8,128)S(1)}, f32[6,288]{1,0:T(8,128)}, u32[]{:S(2)}) copy-start(f32[6,288]{1,0:T(8,128)} %get-tuple-element.212) | copy-start | bytes 20740
  69.0 1.5 %copy-start.35 = (f32[6,288]{1,0:T(8,128)S(1)}, f32[6,288]{1,0:T(8,128)}, u32[]{:S(2)}) copy-start(f32[6,288]{1,0:T(8,128)} %get-tuple-element.213) | copy-start | bytes 20740
  71.1 1.8 %copy-start.30 = (f32[6,288]{1,0:T(8,128)S(1)}, f32[6,288]{1,0:T(8,128)}, u32[]{:S(2)}) copy-start(f32[6,288]{1,0:T(8,128)} %get-tuple-element.185) | copy-start | bytes 20740
  72.9 1.5 %copy-start.13 = (f32[32,288]{1,0:T(8,128)S(1)}, f32[32,288]{1,0:T(8,128)}, u32[]{:S(2)}) copy-start(f32[32,288]{1,0:T(8,128)} %get-tuple-element.98) | copy-start | bytes 110596
  72.9 1.5 %copy-start.32 = (f32[6,288]{1,0:T(8,128)S(1)}, f32[6,288]{1,0:T(8,128)}, u32[]{:S(2)}) copy-start(f32[6,288]{1,0:T(8,128)} %get-tuple-element.204) | copy-start | bytes 20740
  73.0 1.5 %copy-start.33 = (f32[6,288]{1,0:T(8,128)S(1)}, f32[6,288]{1,0:T(8,128)}, u32[]{:S(2)}) copy-start(f32[6,288]{1,0:T(8,128)} %get-tuple-element.205) | copy-start | bytes 20740
  76.9 1.9 %copy-start = (f32[44,1344]{1,0:T(8,128)S(1)}, f32[44,1344]{1,0:T(8,128)}, u32[]{:S(2)}) copy-start(f32[44,1344]{1,0:T(8,128)} %concatenate.489) | copy-start | bytes 709636
  76.9 1.9 %copy-start.1 = (f32[44,1344]{1,0:T(8,128)S(1)}, f32[44,1344]{1,0:T(8,128)}, u32[]{:S(2)}) copy-start(f32[44,1344]{1,0:T(8,128)} %concatenate.465) | copy-start | bytes 709636
  86.4 1.0 copy-start.5
  86.4 1.0 %copy-start.6 = (f32[1,3,32,768]{3,2,1,0:T(8,128)S(1)}, f32[1,3,32,768]{3,2,1,0:T(8,128)}, u32[]{:S(2)}) copy-start(f32[1,3,32,768]{3,2,1,0:T(8,128)} %get-tuple-element.34) | copy-start | bytes 884740
  86.4 1.1 %copy-start.7 = (f32[1,3,32,768]{3,2,1,0:T(8,128)S(1)}, f32[1,3,32,768]{3,2,1,0:T(8,128)}, u32[]{:S(2)}) copy-start(f32[1,3,32,768]{3,2,1,0:T(8,128)} %get-tuple-element.35) | copy-start | bytes 884740
  86.4 1.2 %copy-start.8 = (f32[1,3,32,768]{3,2,1,0:T(8,128)S(1)}, f32[1,3,32,768]{3,2,1,0:T(8,128)}, u32[]{:S(2)}) copy-start(f32[1,3,32,768]{3,2,1,0:T(8,128)} %get-tuple-element.36) | copy-start | bytes 884740
  86.7 1.1 %copy-start.3 = (f32[1,3,32,768]{3,2,1,0:T(8,128)S(1)}, f32[1,3,32,768]{3,2,1,0:T(8,128)}, u32[]{:S(2)}) copy-start(f32[1,3,32,768]{3,2,1,0:T(8,128)} %get-tuple-element.31) | copy-start | bytes 884740
  86.7 1.1 %copy-start.4 = (f32[1,3,32,768]{3,2,1,0:T(8,128)S(1)}, f32[1,3,32,768]{3,2,1,0:T(8,128)}, u32[]{:S(2)}) copy-start(f32[1,3,32,768]{3,2,1,0:T(8,128)} %get-tuple-element.32) | copy-start | bytes 884740
  87.0 0.8 copy-start.54
  87.0 0.8 copy-start.55
  89.6 5.5 %collective-permute-start.6 = (f32[8,768]{1,0:T(8,128)S(1)}, f32[8,768]{1,0:T(8,128)S(1)}, u32[]{:S(2)}, u32[]{:S(2)}) collective-permute-start(f32[8,768]{1,0:T(8,128)S(1)} %get-tuple-element.249), channel_id=1, source_target_pairs={{8,16},{16,8},{9,17},{17,9},{10,18},{18,10},{11,19},{19,11},{12,20... | collective-permute-start | bytes 73736 | tf_op jit(solution)/shard_map/ppermute | solution.py:25
  92.6 2.7 %collective-permute-start.7 = (f32[8,768]{1,0:T(8,128)S(1)}, f32[8,768]{1,0:T(8,128)S(1)}, u32[]{:S(2)}, u32[]{:S(2)}) collective-permute-start(f32[8,768]{1,0:T(8,128)S(1)} %get-tuple-element.250), channel_id=1, source_target_pairs={{0,8},{8,0},{16,24},{24,16},{1,9},{9,1},{17,25},{25,17},{2,10},{10... | collective-permute-start | bytes 73736 | tf_op jit(solution)/shard_map/ppermute | solution.py:24
  95.6 6.8 %collective-permute-start.8 = (f32[32,384]{1,0:T(8,128)S(1)}, f32[32,384]{1,0:T(8,128)S(1)}, u32[]{:S(2)}, u32[]{:S(2)}) collective-permute-start(f32[32,384]{1,0:T(8,128)S(1)} %get-tuple-element.247), channel_id=1, source_target_pairs={{1,2},{2,1},{3,4},{4,3},{5,6},{6,5},{9,10},{10,9},{11,12},{12,11},... | collective-permute-start | bytes 147464 | tf_op jit(solution)/shard_map/ppermute | solution.py:25
  100.5 1.9 %collective-permute-start.9 = (f32[32,384]{1,0:T(8,128)S(1)}, f32[32,384]{1,0:T(8,128)S(1)}, u32[]{:S(2)}, u32[]{:S(2)}) collective-permute-start(f32[32,384]{1,0:T(8,128)S(1)} %get-tuple-element.248), channel_id=1, source_target_pairs={{0,1},{1,0},{2,3},{3,2},{4,5},{5,4},{6,7},{7,6},{8,9},{9,8},{10,11... | collective-permute-start | bytes 147464 | tf_op jit(solution)/shard_map/ppermute | solution.py:24
  (2 other events, 1.4 us)

commit v2 on v1

v2 whole, which is shorter than its diff:
```python
import functools

import jax
import jax.numpy as jnp
from jax import lax
from jax.experimental import pallas as pl
from jax.experimental.pallas import tpu as pltpu
from jax.sharding import PartitionSpec as P

NZ = 48
STEPS = 6
RADIUS = 8
SUB = 8
LANE = 128

courant = 0.45


def up_to(size, unit):
    return -(-size // unit) * unit


HALO = STEPS
SIDE = up_to(HALO * NZ, LANE)
REACH = RADIUS * NZ


def swap_pairs(count, first):
    pairs = []
    for i in range(first, count - 1, 2):
        pairs += [(i, i + 1), (i + 1, i)]
    return pairs


def swap(to_a, to_b, axis):
    count = lax.axis_size(axis)
    from_b = lax.ppermute(to_b, axis, swap_pairs(count, 1))
    from_a = lax.ppermute(to_a, axis, swap_pairs(count, 0))
    return from_a, from_b


def is_even(axis):
    return lax.rem(lax.axis_index(axis), 2) == 0


def call(body, outs, ins, scratch=(), limit=16):
    vmem = pl.BlockSpec(memory_space=pltpu.VMEM)
    return pl.pallas_call(
        body,
        out_shape=[jax.ShapeDtypeStruct(s, jnp.float32) for s in outs],
        in_specs=[vmem] * len(ins),
        out_specs=[vmem] * len(outs),
        scratch_shapes=list(scratch),
        compiler_params=pltpu.CompilerParams(vmem_limit_bytes=limit * 2**20),
    )(*ins)


def pack_rows(first_e, last_e, first_h, last_h, first_t, last_t, to_a, to_b):
    even = is_even("gx")
    at = 0
    for first, last in ((first_e, last_e), (first_h, last_h), (first_t, last_t)):
        for c in range(first.shape[0]):
            head = first[c, 0:HALO, :]
            tail = last[c, SUB - HALO : SUB, :]
            to_a[at : at + HALO, :] = jnp.where(even, tail, head)
            to_b[at : at + HALO, :] = jnp.where(even, head, tail)
            at += HALO


def pack_x(electric, magnetic, tensor):
    rows, width = electric.shape[1:]
    parts = (electric, magnetic, tensor)
    ins, specs = [], []
    for part in parts:
        for block in (0, rows // SUB - 1):
            ins.append(part)
            specs.append(pl.BlockSpec((part.shape[0], SUB, width), lambda i, block=block: (0, block, 0)))
    packed = HALO * sum(part.shape[0] for part in parts)
    out = jax.ShapeDtypeStruct((packed, width), jnp.float32)
    return pl.pallas_call(
        pack_rows,
        grid=(1,),
        out_shape=[out, out],
        in_specs=specs,
        out_specs=[pl.BlockSpec((packed, width), lambda i: (0, 0))] * 2,
        compiler_params=pltpu.CompilerParams(vmem_limit_bytes=8 * 2**20),
    )(*ins)


def pack_lanes(size, *refs):
    ins, (to_a, to_b) = refs[:-2], refs[-2:]
    even = is_even("gy")
    at = 0
    for ref in ins:
        width = ref.shape[2]
        for c in range(ref.shape[0]):
            head = ref[c, :, 0:size]
            tail = ref[c, :, width - size : width]
            to_a[at] = jnp.where(even, tail, head)
            to_b[at] = jnp.where(even, head, tail)
            at += 1


def pack_y(size, *ins):
    out = (sum(x.shape[0] for x in ins), ins[0].shape[1], size)
    return call(functools.partial(pack_lanes, size), [out, out], ins)


def main_body(
    e_in, h_in, t_in, saved, xa, xb, ya, yb, ca, cb, inverse, e_out, h_out, scaled, to_a, to_b, fe, fh, ft
):
    rows, width = e_in.shape[1:]
    total_rows, total = fe.shape[1:]
    tiles = total_rows // SUB
    even_x, even_y = is_even("gx"), is_even("gy")
    inner = slice(SUB, SUB + rows)
    middle = slice(SIDE, SIDE + width)
    left, right = slice(0, SIDE), slice(SIDE + width, total)
    top, bottom = slice(0, SUB), slice(SUB + rows, total_rows)
    top_in = slice(SUB - HALO, SUB)
    bottom_in = slice(SUB + rows, SUB + rows + HALO)

    k = 0
    for own, full, factor in ((e_in, fe, None), (h_in, fh, courant), (t_in, ft, courant * courant)):
        for c in range(own.shape[0]):

            def put(where_rows, where_lanes, value, full=full, c=c, factor=factor):
                full[c, where_rows, where_lanes] = value if factor is None else value * factor

            packed = slice(k * HALO, (k + 1) * HALO)
            full[c, top, :] = jnp.zeros((SUB, total), jnp.float32)
            full[c, bottom, :] = jnp.zeros((SUB, total), jnp.float32)
            put(inner, middle, own[c])
            a, b = ya[k], yb[k]
            put(inner, left, jnp.where(even_y, b, a))
            put(inner, right, jnp.where(even_y, a, b))
            a, b = xa[packed], xb[packed]
            put(top_in, middle, jnp.where(even_x, b, a))
            put(bottom_in, middle, jnp.where(even_x, a, b))
            aa, ab, ba, bb = ca[0, packed], cb[0, packed], ca[1, packed], cb[1, packed]
            left_a, left_b = jnp.where(even_y, ab, aa), jnp.where(even_y, bb, ba)
            put(top_in, left, jnp.where(even_x, left_b, left_a))
            put(bottom_in, left, jnp.where(even_x, left_a, left_b))
            right_a, right_b = jnp.where(even_y, aa, ab), jnp.where(even_y, ba, bb)
            put(top_in, right, jnp.where(even_x, right_b, right_a))
            put(bottom_in, right, jnp.where(even_x, right_a, right_b))
            k += 1

    inside_x = jnp.where(lax.axis_index("gx") > 0, 1.0, 0.0).astype(jnp.float32)
    inside_y = jnp.where(lax.axis_index("gy") > 0, 1.0, 0.0).astype(jnp.float32)

    for step in range(STEPS):
        left_over = STEPS - step
        begin = (SIDE - left_over * NZ) // LANE * LANE
        end = up_to(SIDE + width + left_over * NZ, LANE)
        span = end - begin
        lanes = slice(begin, end)
        sub = lax.broadcasted_iota(jnp.int32, (SUB, span), 0)
        depth = lax.rem(lax.broadcasted_iota(jnp.int32, (SUB, span), 1) + (begin % NZ), NZ)
        upper = (depth != NZ - 1).astype(jnp.float32)
        lower = (depth != 0).astype(jnp.float32)
        low = SIDE - begin
        last = step == STEPS - 1

        def tile(ref, c, r):
            return ref[c, r * SUB : (r + 1) * SUB, lanes]

        def to_tile(ref, c, r, value):
            ref[c, r * SUB : (r + 1) * SUB, lanes] = value

        def from_next_y(f):
            return pltpu.roll(f, span - NZ, 1)

        def from_next_z(f):
            return pltpu.roll(f, span - 1, 1) * upper

        def from_prev_y(f):
            return pltpu.roll(f, NZ, 1)

        def from_prev_z(f):
            return pltpu.roll(f, 1, 1) * lower

        after = None
        for r in reversed(range(tiles)):
            e = [tile(fe, c, r) for c in range(3)]
            g = [
                (tile(ft, c, r) * e[0] + tile(ft, 3 + c, r) * e[1]) + tile(ft, 6 + c, r) * e[2]
                for c in range(3)
            ]
            turned = [None] + [pltpu.roll(g[c], SUB - 1, 0) for c in (1, 2)]
            if after is None:
                after = turned
            if not (last and r == tiles - 1):
                next_x = [None] + [jnp.where(sub == SUB - 1, after[c], turned[c]) for c in (1, 2)]
                curl = [
                    (from_next_y(g[2]) - g[2]) - (from_next_z(g[1]) - g[1]),
                    (from_next_z(g[0]) - g[0]) - (next_x[2] - g[2]),
                    (next_x[1] - g[1]) - (from_next_y(g[0]) - g[0]),
                ]
                for c in range(3):
                    h = tile(fh, c, r) - curl[c]
                    if r == 0:
                        h = h * inside_x
                    h = jnp.concatenate([h[:, :low] * inside_y, h[:, low:]], axis=1)
                    to_tile(fh, c, r, h)
            after = turned

        before = None
        for r in range(tiles):
            if last and r == tiles - 1:
                continue
            h = [tile(fh, c, r) for c in range(3)]
            turned = [None] + [pltpu.roll(h[c], 1, 0) for c in (1, 2)]
            if before is None:
                before = turned
            if not (last and r == 0):
                prev_x = [None] + [jnp.where(sub == 0, before[c], turned[c]) for c in (1, 2)]
                curl = [
                    (h[2] - from_prev_y(h[2])) - (h[1] - from_prev_z(h[1])),
                    (h[0] - from_prev_z(h[0])) - (h[2] - prev_x[2]),
                    (h[1] - prev_x[1]) - (h[0] - from_prev_y(h[0])),
                ]
                for c in range(3):
                    to_tile(fe, c, r, tile(fe, c, r) + curl[c])
            before = turned

        pair = 2 * SUB
        for r in range(rows // pair):
            at = slice(r * pair, (r + 1) * pair)
            at_full = slice(SUB + r * pair, SUB + (r + 1) * pair)
            s = [saved[step, c, at].astype(jnp.float32) for c in range(3)]
            e = [fe[c, at_full, middle] for c in range(3)]
            term = (e[0] * s[0] + e[1] * s[1]) + e[2] * s[2]
            scaled[at] = term if step == 0 else scaled[at] + term

    for c in range(3):
        e_out[c] = fe[c, inner, middle]
        h_out[c] = fh[c, inner, middle] * (1.0 / courant)
    scaled[...] = scaled[...] * inverse[...]
    head, tail = scaled[:RADIUS], scaled[rows - RADIUS :]
    to_a[...] = jnp.where(even_x, tail, head)
    to_b[...] = jnp.where(even_x, head, tail)


def run_steps(electric, magnetic, tensor, saved, xa, xb, ya, yb, ca, cb, inverse):
    rows, width = electric.shape[1:]
    full = (rows + 2 * SUB, width + 2 * SIDE)
    edge = (RADIUS, width)
    return call(
        main_body,
        [electric.shape, magnetic.shape, (rows, width), edge, edge],
        (electric, magnetic, tensor, saved, xa, xb, ya, yb, ca, cb, inverse),
        [pltpu.VMEM((n, *full), jnp.float32) for n in (3, 3, 9)],
        limit=28,
    )


def box(values, unit, axis):
    size = values.shape[axis]

    def ahead(v, places):
        return pltpu.roll(v, size - places * unit, axis)

    two = values + ahead(values, 1)
    four = two + ahead(two, 2)
    eight = four + ahead(four, 4)
    return eight + ahead(values, 8)


def filter_rows(scaled, xa, xb, across, to_a, to_b):
    rows, width = scaled.shape
    even_x, even_y = is_even("gx"), is_even("gy")
    a, b = xa[...], xb[...]
    low, high = jnp.where(even_x, b, a), jnp.where(even_x, a, b)
    extended = jnp.concatenate([low, scaled[...], high], axis=0)
    result = box(box(extended, 1, 0), 1, 0)[:rows] * (1.0 / (RADIUS + 1.0))
    across[...] = result
    head, tail = result[:, :REACH], result[:, width - REACH :]
    to_a[...] = jnp.where(even_y, tail, head)
    to_b[...] = jnp.where(even_y, head, tail)


def filter_columns(across, ya, yb, gradient):
    width = across.shape[1]
    even_y = is_even("gy")
    for r in range(across.shape[0] // SUB):
        at = slice(r * SUB, (r + 1) * SUB)
        a, b = ya[at], yb[at]
        low, high = jnp.where(even_y, b, a), jnp.where(even_y, a, b)
        extended = jnp.concatenate([low, across[at], high], axis=1)
        gradient[at] = box(box(extended, NZ, 1), NZ, 1)[:, :width] * (1.0 / (RADIUS + 1.0))


def tent(offset):
    return (RADIUS + 1.0 - abs(offset)) / (RADIUS + 1.0)


def coverage(places, length):
    total = jnp.zeros(places.shape, jnp.float32)
    for offset in range(-RADIUS, RADIUS + 1):
        inside = ((places + offset >= 0) & (places + offset < length)).astype(jnp.float32)
        total = total + tent(offset) * inside
    return total


def shards(electric, magnetic, tensor, saved):
    rows, width = electric.shape[1:]
    cols = width // NZ
    edge = (RADIUS, width)

    xa, xb = swap(*pack_x(electric, magnetic, tensor), "gx")
    ya, yb = swap(*pack_y(SIDE, electric, magnetic, tensor), "gy")
    ca, cb = swap(*pack_y(SIDE, xa[None], xb[None]), "gy")

    row_places = lax.axis_index("gx") * rows + lax.broadcasted_iota(jnp.int32, (rows, width), 0)
    col_places = lax.axis_index("gy") * cols + lax.broadcasted_iota(jnp.int32, (rows, width), 1) // NZ
    cover = coverage(row_places, lax.axis_size("gx") * rows) * coverage(col_places, lax.axis_size("gy") * cols)

    e, h, scaled, to_a, to_b = run_steps(
        electric, magnetic, tensor, saved, xa, xb, ya, yb, ca, cb, 1.0 / cover
    )
    xa, xb = swap(to_a, to_b, "gx")
    side = (rows, REACH)
    across, to_a, to_b = call(filter_rows, [(rows, width), side, side], (scaled, xa, xb))
    ya, yb = swap(to_a, to_b, "gy")
    (gradient,) = call(filter_columns, [(rows, width)], (across, ya, yb))
    return e, h, gradient


def solution(mesh):
    in_specs = (
        P(None, "gx", "gy"),
        P(None, "gx", "gy"),
        P(None, "gx", "gy"),
        P(None, None, "gx", "gy"),
    )
    out_specs = (P(None, "gx", "gy"), P(None, "gx", "gy"), P("gx", "gy"))
    return jax.shard_map(shards, mesh=mesh, in_specs=in_specs, out_specs=out_specs, check_vma=False)
```

time: 105 us -> 55.1 us (0.52)
  local copies, waits for them, and re-layouts: 41 us -> 3.1 us
  other arithmetic: 28 us -> 0.15 us
  Pallas kernels: 0 us -> 10.3 us
  waiting for transfers between devices: 12.9 us -> 22.3 us
  starting transfers between devices: 19.8 us -> 18.1 us
    slice x56 -> x0, local copies, waits for them, and re-layouts: 16.2 us -> none  [the longest x8 3.86 us: stack_lanes(): return jnp.concatenate([p[:, begin:begin + side] for p in parts], axis=1)]
    concatenate x19 -> x0, local copies, waits for them, and re-layouts: 12.8 us -> none  [the longest x15 8.65 us: extend(): return jnp.concatenate([low, mid, high], axis=1)]
    pallas_call x0 -> x6, Pallas kernels: none -> 10.3 us  [the longest x5 10.1 us: call(): pl.pallas_call(body, out_shape=[jax.ShapeDtypeStruct(s, jnp.float32) for...]
    ppermute x10, waiting for transfers between devices: 12.9 us -> 22.3 us  [the longest x5 17 us: swap(): from_b = lax.ppermute(to_b, axis, swap_pairs(count, 1))]
    concatenate x45 -> x0, other arithmetic: 8.86 us -> none  [the longest x15 3.78 us: extend(): jnp.concatenate([high_c[rows, :side], high_y[:, lanes], high_c[rows, side...]
    unnamed x112 -> x14, local copies, waits for them, and re-layouts: 9.63 us -> 3.1 us
    add x13 -> x0, other arithmetic: 5.74 us -> none  [the longest x11 4.42 us: leapfrog(): mats[col] * fields_e[0] + mats[3 + col] * fields_e[1]]
    select_n x10 -> x0, other arithmetic: 4.37 us -> none  [the longest x5 2.35 us: swap(): return (jnp.where(even, from_b, from_a), jnp.where(even, from_a, from_b))]
  transfers between devices with their start and end apart: 10 -> 10, of which waited for: 6 -> 6; matrix products, arithmetic and copies ran while one was open for 14% -> 0% of each run, Pallas kernels for 0% -> 2%
where the time goes in v2:
time: 55.1 us; the launch traced here: 54.7 us
  waiting for transfers between devices  22.3 us (40%)
  starting transfers between devices  18.1 us (33%)
  Pallas kernels  10.3 us (19%)
  local copies, waits for them, and re-layouts  3.1 us (6%)
  between operations  0.79 us (1%)
    ppermute x5, waiting for transfers between devices, swap(): from_b = lax.ppermute(to_b, axis, swap_pairs(count, 1))  17 us
    ppermute x5, starting transfers between devices, swap(): from_b = lax.ppermute(to_b, axis, swap_pairs(count, 1))  15.4 us
    pallas_call x5, Pallas kernels, call(): pl.pallas_call(body, out_shape=[jax.ShapeDtypeStruct(s, jnp.float32) for...  10.1 us
    ppermute x5, waiting for transfers between devices, swap(): from_a = lax.ppermute(to_a, axis, swap_pairs(count, 0))  5.38 us
    unnamed x14, local copies, waits for them, and re-layouts  3.1 us
    ppermute x5, starting transfers between devices, swap(): from_a = lax.ppermute(to_a, axis, swap_pairs(count, 0))  2.72 us
  transfers between devices with their start and end apart: 10, of which 6 were waited for; matrix products, arithmetic and copies ran while one was open for 0% of the time, Pallas kernels for 2%

profile of v2, /device:TPU:11, one launch (start us, length us, event | category | flops | bytes accessed | tf_op | source)
XLA Modules:
  0.0 54.7 jit_solution(380995985965124964)
XLA Ops:
  0.6 0.0 copy-start
  0.6 1.2 %copy-done = f32[9,32,768]{2,1,0:T(8,128)S(1)} copy-done((f32[9,32,768]{2,1,0:T(8,128)S(1)}, f32[9,32,768]{2,1,0:T(8,128)}, u32[]{:S(2)}) %copy-start) | copy-done | bytes 884760
  1.8 0.0 copy-start.2
  1.8 1.0 %copy-done.2 = f32[3,32,768]{2,1,0:T(8,128)S(1)} copy-done((f32[3,32,768]{2,1,0:T(8,128)S(1)}, f32[3,32,768]{2,1,0:T(8,128)}, u32[]{:S(2)}) %copy-start.2) | copy-done | bytes 294936
  2.8 0.0 copy-start.4
  2.8 1.0 %copy-done.4 = f32[3,32,768]{2,1,0:T(8,128)S(1)} copy-done((f32[3,32,768]{2,1,0:T(8,128)S(1)}, f32[3,32,768]{2,1,0:T(8,128)}, u32[]{:S(2)}) %copy-start.4) | copy-done | bytes 294936
  3.7 1.2 %shard_map.68 = (f32[15,32,384]{2,1,0:T(8,128)}, f32[15,32,384]{2,1,0:T(8,128)}) custom-call(f32[3,32,768]{2,1,0:T(8,128)S(1)} %copy-done.2, f32[3,32,768]{2,1,0:T(8,128)S(1)} %copy-done.4, f32[9,32,768]{2,1,0:T(8,128)S(1)} %copy-done), custom_call_target="tpu_custom_call" | custom-call | tf_op jit(solution)/shard_map/pallas_call | solution.py:48
  5.0 0.7 %collective-permute-start.2 = (f32[15,32,384]{2,1,0:T(8,128)}, f32[15,32,384]{2,1,0:T(8,128)}, u32[]{:S(2)}, u32[]{:S(2)}) collective-permute-start(f32[15,32,384]{2,1,0:T(8,128)} %get-tuple-element.19), channel_id=1, source_target_pairs={{0,1},{1,0},{2,3},{3,2},{4,5},{5,4},{6,7},{7,6},{8,9},{9,8},{10,11... | collective-permute-start | bytes 2211848 | tf_op jit(solution)/shard_map/ppermute | solution.py:38
  5.6 3.1 %collective-permute-start.3 = (f32[15,32,384]{2,1,0:T(8,128)}, f32[15,32,384]{2,1,0:T(8,128)}, u32[]{:S(2)}, u32[]{:S(2)}) collective-permute-start(f32[15,32,384]{2,1,0:T(8,128)} %get-tuple-element.20), channel_id=1, source_target_pairs={{1,2},{2,1},{3,4},{4,3},{5,6},{6,5},{9,10},{10,9},{11,12},{12,11},... | collective-permute-start | bytes 2211848 | tf_op jit(solution)/shard_map/ppermute | solution.py:37
  8.7 0.0 copy-start.1
  8.7 0.0 copy-start.6
  8.8 0.2 shard_map.67
  8.9 0.3 collective-permute-start
  9.2 4.1 %collective-permute-start.1 = (f32[90,768]{1,0:T(8,128)S(1)}, f32[90,768]{1,0:T(8,128)S(1)}, u32[]{:S(2)}, u32[]{:S(2)}) collective-permute-start(f32[90,768]{1,0:T(8,128)S(1)} %get-tuple-element.18), channel_id=1, source_target_pairs={{8,16},{16,8},{9,17},{17,9},{10,18},{18,10},{11,19},{19,11},{12,20... | collective-permute-start | bytes 829448 | tf_op jit(solution)/shard_map/ppermute | solution.py:37
  13.3 4.6 %collective-permute-done.xa = f32[90,768]{1,0:T(8,128)S(1)} collective-permute-done((f32[90,768]{1,0:T(8,128)S(1)}, f32[90,768]{1,0:T(8,128)S(1)}, u32[]{:S(2)}, u32[]{:S(2)}) %collective-permute-start) | collective-permute-done | bytes 276512 | tf_op jit(solution)/shard_map/ppermute | solution.py:38
  18.0 7.0 %collective-permute-done.1.xb = f32[90,768]{1,0:T(8,128)S(1)} collective-permute-done((f32[90,768]{1,0:T(8,128)S(1)}, f32[90,768]{1,0:T(8,128)S(1)}, u32[]{:S(2)}, u32[]{:S(2)}) %collective-permute-start.1) | collective-permute-done | bytes 276512 | tf_op jit(solution)/shard_map/ppermute | solution.py:37
  25.0 0.0 copy-start.3
  25.0 0.0 copy-start.5
  25.0 0.9 %shard_map.69 = (f32[2,90,384]{2,1,0:T(8,128)}, f32[2,90,384]{2,1,0:T(8,128)}) custom-call(f32[1,90,768]{2,1,0:T(8,128)S(1)} %bitcast.2, f32[1,90,768]{2,1,0:T(8,128)S(1)} %bitcast.3), custom_call_target="tpu_custom_call" | custom-call | tf_op jit(solution)/shard_map/pallas_call | solution.py:48
  25.8 0.4 collective-permute-start.4
  26.2 3.2 %collective-permute-start.5 = (f32[2,90,384]{2,1,0:T(8,128)}, f32[2,90,384]{2,1,0:T(8,128)S(1)}, u32[]{:S(2)}, u32[]{:S(2)}) collective-permute-start(f32[2,90,384]{2,1,0:T(8,128)} %get-tuple-element.22), channel_id=1, source_target_pairs={{1,2},{2,1},{3,4},{4,3},{5,6},{6,5},{9,10},{10,9},{11,12},{12,11},... | collective-permute-start | bytes 829448 | tf_op jit(solution)/shard_map/ppermute | solution.py:37
  29.5 0.1 multiply_divide_fusion.inverse
  29.6 0.0 collective-permute-done.4.ca
  29.6 4.9 %collective-permute-done.5.cb = f32[2,90,384]{2,1,0:T(8,128)S(1)} collective-permute-done((f32[2,90,384]{2,1,0:T(8,128)}, f32[2,90,384]{2,1,0:T(8,128)S(1)}, u32[]{:S(2)}, u32[]{:S(2)}) %collective-permute-start.5) | collective-permute-done | bytes 276512 | tf_op jit(solution)/shard_map/ppermute | solution.py:37
  34.5 0.0 collective-permute-done.2.ya
  34.5 0.0 collective-permute-done.3.yb
  34.5 0.0 copy-done.1
  34.5 0.0 copy-done.6
  34.5 0.0 copy-done.3
  34.5 0.0 copy-done.5
  34.5 6.8 %shard_map.70 = (f32[3,32,768]{2,1,0:T(8,128)}, f32[3,32,768]{2,1,0:T(8,128)}, f32[32,768]{1,0:T(8,128)S(1)}, f32[8,768]{1,0:T(8,128)S(1)}, f32[8,768]{1,0:T(8,128)S(1)}) custom-call(f32[3,32,768]{2,1,0:T(8,128)S(1)} %copy-done.3, f32[3,32,768]{2,1,0:T(8,128)S(1)} %copy-done.5, f32[9,32,768]{2,1,0:T(8,128)S(1)} %copy-done.1, ...), custom_call_target="tpu_custom_call" | custom-call | tf_op jit(solution)/shard_map/pallas_call | solution.py:48
  41.3 0.0 collective-permute-start.6
  41.3 1.9 %collective-permute-start.7 = (f32[8,768]{1,0:T(8,128)S(1)}, f32[8,768]{1,0:T(8,128)S(1)}, u32[]{:S(2)}, u32[]{:S(2)}) collective-permute-start(f32[8,768]{1,0:T(8,128)S(1)} %get-tuple-element.27), channel_id=1, source_target_pairs={{8,16},{16,8},{9,17},{17,9},{10,18},{18,10},{11,19},{19,11},{12,20... | collective-permute-start | bytes 73736 | tf_op jit(solution)/shard_map/ppermute | solution.py:37
  43.2 0.8 %collective-permute-done.6.xa = f32[8,768]{1,0:T(8,128)S(1)} collective-permute-done((f32[8,768]{1,0:T(8,128)S(1)}, f32[8,768]{1,0:T(8,128)S(1)}, u32[]{:S(2)}, u32[]{:S(2)}) %collective-permute-start.6) | collective-permute-done | bytes 24608 | tf_op jit(solution)/shard_map/ppermute | solution.py:38
  43.9 2.8 %collective-permute-done.7.xb = f32[8,768]{1,0:T(8,128)S(1)} collective-permute-done((f32[8,768]{1,0:T(8,128)S(1)}, f32[8,768]{1,0:T(8,128)S(1)}, u32[]{:S(2)}, u32[]{:S(2)}) %collective-permute-start.7) | collective-permute-done | bytes 24608 | tf_op jit(solution)/shard_map/ppermute | solution.py:37
  46.7 0.1 shard_map.71
  46.8 1.3 %collective-permute-start.8 = (f32[32,384]{1,0:T(8,128)S(1)}, f32[32,384]{1,0:T(8,128)S(1)}, u32[]{:S(2)}, u32[]{:S(2)}) collective-permute-start(f32[32,384]{1,0:T(8,128)S(1)} %get-tuple-element.29), channel_id=1, source_target_pairs={{0,1},{1,0},{2,3},{3,2},{4,5},{5,4},{6,7},{7,6},{8,9},{9,8},{10,11... | collective-permute-start | bytes 147464 | tf_op jit(solution)/shard_map/ppermute | solution.py:38
  48.2 3.1 %collective-permute-start.9 = (f32[32,384]{1,0:T(8,128)S(1)}, f32[32,384]{1,0:T(8,128)S(1)}, u32[]{:S(2)}, u32[]{:S(2)}) collective-permute-start(f32[32,384]{1,0:T(8,128)S(1)} %get-tuple-element.30), channel_id=1, source_target_pairs={{1,2},{2,1},{3,4},{4,3},{5,6},{6,5},{9,10},{10,9},{11,12},{12,11},... | collective-permute-start | bytes 147464 | tf_op jit(solution)/shard_map/ppermute | solution.py:37
  51.3 0.0 collective-permute-done.8.ya
  51.3 2.3 %collective-permute-done.9.yb = f32[32,384]{1,0:T(8,128)S(1)} collective-permute-done((f32[32,384]{1,0:T(8,128)S(1)}, f32[32,384]{1,0:T(8,128)S(1)}, u32[]{:S(2)}, u32[]{:S(2)}) %collective-permute-start.9) | collective-permute-done | bytes 49184 | tf_op jit(solution)/shard_map/ppermute | solution.py:37
  53.6 1.2 %shard_map.72 = f32[32,768]{1,0:T(8,128)} custom-call(f32[32,768]{1,0:T(8,128)S(1)} %get-tuple-element.28.across, f32[32,384]{1,0:T(8,128)S(1)} %collective-permute-done.8.ya, f32[32,384]{1,0:T(8,128)S(1)} %collective-permute-done.9.yb), custom_call_target="tpu_custom_call" | custom-call | tf_op jit(solution)/shard_map/pallas_call | solution.py:48
  (3 shorter events, 0.0 us)
Async XLA Ops:
  0.6 1.2 %copy-start = (f32[9,32,768]{2,1,0:T(8,128)S(1)}, f32[9,32,768]{2,1,0:T(8,128)}, u32[]{:S(2)}) copy-start(f32[9,32,768]{2,1,0:T(8,128)} %t_in.1) | copy-start | bytes 2654212
  1.8 1.0 %copy-start.2 = (f32[3,32,768]{2,1,0:T(8,128)S(1)}, f32[3,32,768]{2,1,0:T(8,128)}, u32[]{:S(2)}) copy-start(f32[3,32,768]{2,1,0:T(8,128)} %e_in.1) | copy-start | bytes 884740
  2.8 1.0 %copy-start.4 = (f32[3,32,768]{2,1,0:T(8,128)S(1)}, f32[3,32,768]{2,1,0:T(8,128)}, u32[]{:S(2)}) copy-start(f32[3,32,768]{2,1,0:T(8,128)} %h_in.1) | copy-start | bytes 884740
  5.0 29.5 %collective-permute-start.2 = (f32[15,32,384]{2,1,0:T(8,128)}, f32[15,32,384]{2,1,0:T(8,128)}, u32[]{:S(2)}, u32[]{:S(2)}) collective-permute-start(f32[15,32,384]{2,1,0:T(8,128)} %get-tuple-element.19), channel_id=1, source_target_pairs={{0,1},{1,0},{2,3},{3,2},{4,5},{5,4},{6,7},{7,6},{8,9},{9,8},{10,11... | collective-permute-start | bytes 2211848 | tf_op jit(solution)/shard_map/ppermute | solution.py:38
  5.6 28.8 %collective-permute-start.3 = (f32[15,32,384]{2,1,0:T(8,128)}, f32[15,32,384]{2,1,0:T(8,128)}, u32[]{:S(2)}, u32[]{:S(2)}) collective-permute-start(f32[15,32,384]{2,1,0:T(8,128)} %get-tuple-element.20), channel_id=1, source_target_pairs={{1,2},{2,1},{3,4},{4,3},{5,6},{6,5},{9,10},{10,9},{11,12},{12,11},... | collective-permute-start | bytes 2211848 | tf_op jit(solution)/shard_map/ppermute | solution.py:37
  8.7 25.7 %copy-start.1 = (f32[9,32,768]{2,1,0:T(8,128)S(1)}, f32[9,32,768]{2,1,0:T(8,128)}, u32[]{:S(2)}) copy-start(f32[9,32,768]{2,1,0:T(8,128)} %t_in.1) | copy-start | bytes 2654212
  8.7 25.7 %copy-start.6 = (bf16[6,3,32,768]{3,2,1,0:T(8,128)(2,1)S(1)}, bf16[6,3,32,768]{3,2,1,0:T(8,128)(2,1)}, u32[]{:S(2)}) copy-start(bf16[6,3,32,768]{3,2,1,0:T(8,128)(2,1)} %saved.1) | copy-start | bytes 2654212
  8.9 9.0 %collective-permute-start = (f32[90,768]{1,0:T(8,128)S(1)}, f32[90,768]{1,0:T(8,128)S(1)}, u32[]{:S(2)}, u32[]{:S(2)}) collective-permute-start(f32[90,768]{1,0:T(8,128)S(1)} %get-tuple-element.17), channel_id=1, source_target_pairs={{0,8},{8,0},{16,24},{24,16},{1,9},{9,1},{17,25},{25,17},{2,10},{10... | collective-permute-start | bytes 829448 | tf_op jit(solution)/shard_map/ppermute | solution.py:38
  9.2 15.7 %collective-permute-start.1 = (f32[90,768]{1,0:T(8,128)S(1)}, f32[90,768]{1,0:T(8,128)S(1)}, u32[]{:S(2)}, u32[]{:S(2)}) collective-permute-start(f32[90,768]{1,0:T(8,128)S(1)} %get-tuple-element.18), channel_id=1, source_target_pairs={{8,16},{16,8},{9,17},{17,9},{10,18},{18,10},{11,19},{19,11},{12,20... | collective-permute-start | bytes 829448 | tf_op jit(solution)/shard_map/ppermute | solution.py:37
  25.0 9.5 %copy-start.3 = (f32[3,32,768]{2,1,0:T(8,128)S(1)}, f32[3,32,768]{2,1,0:T(8,128)}, u32[]{:S(2)}) copy-start(f32[3,32,768]{2,1,0:T(8,128)} %e_in.1) | copy-start | bytes 884740
  25.0 9.5 %copy-start.5 = (f32[3,32,768]{2,1,0:T(8,128)S(1)}, f32[3,32,768]{2,1,0:T(8,128)}, u32[]{:S(2)}) copy-start(f32[3,32,768]{2,1,0:T(8,128)} %h_in.1) | copy-start | bytes 884740
  25.8 3.7 %collective-permute-start.4 = (f32[2,90,384]{2,1,0:T(8,128)}, f32[2,90,384]{2,1,0:T(8,128)S(1)}, u32[]{:S(2)}, u32[]{:S(2)}) collective-permute-start(f32[2,90,384]{2,1,0:T(8,128)} %get-tuple-element.21), channel_id=1, source_target_pairs={{0,1},{1,0},{2,3},{3,2},{4,5},{5,4},{6,7},{7,6},{8,9},{9,8},{10,11... | collective-permute-start | bytes 829448 | tf_op jit(solution)/shard_map/ppermute | solution.py:38
  26.2 8.2 %collective-permute-start.5 = (f32[2,90,384]{2,1,0:T(8,128)}, f32[2,90,384]{2,1,0:T(8,128)S(1)}, u32[]{:S(2)}, u32[]{:S(2)}) collective-permute-start(f32[2,90,384]{2,1,0:T(8,128)} %get-tuple-element.22), channel_id=1, source_target_pairs={{1,2},{2,1},{3,4},{4,3},{5,6},{6,5},{9,10},{10,9},{11,12},{12,11},... | collective-permute-start | bytes 829448 | tf_op jit(solution)/shard_map/ppermute | solution.py:37
  41.3 2.7 %collective-permute-start.6 = (f32[8,768]{1,0:T(8,128)S(1)}, f32[8,768]{1,0:T(8,128)S(1)}, u32[]{:S(2)}, u32[]{:S(2)}) collective-permute-start(f32[8,768]{1,0:T(8,128)S(1)} %get-tuple-element.26), channel_id=1, source_target_pairs={{0,8},{8,0},{16,24},{24,16},{1,9},{9,1},{17,25},{25,17},{2,10},{10... | collective-permute-start | bytes 73736 | tf_op jit(solution)/shard_map/ppermute | solution.py:38
  41.3 5.5 %collective-permute-start.7 = (f32[8,768]{1,0:T(8,128)S(1)}, f32[8,768]{1,0:T(8,128)S(1)}, u32[]{:S(2)}, u32[]{:S(2)}) collective-permute-start(f32[8,768]{1,0:T(8,128)S(1)} %get-tuple-element.27), channel_id=1, source_target_pairs={{8,16},{16,8},{9,17},{17,9},{10,18},{18,10},{11,19},{19,11},{12,20... | collective-permute-start | bytes 73736 | tf_op jit(solution)/shard_map/ppermute | solution.py:37
  46.8 4.4 %collective-permute-start.8 = (f32[32,384]{1,0:T(8,128)S(1)}, f32[32,384]{1,0:T(8,128)S(1)}, u32[]{:S(2)}, u32[]{:S(2)}) collective-permute-start(f32[32,384]{1,0:T(8,128)S(1)} %get-tuple-element.29), channel_id=1, source_target_pairs={{0,1},{1,0},{2,3},{3,2},{4,5},{5,4},{6,7},{7,6},{8,9},{9,8},{10,11... | collective-permute-start | bytes 147464 | tf_op jit(solution)/shard_map/ppermute | solution.py:38
  48.2 5.4 %collective-permute-start.9 = (f32[32,384]{1,0:T(8,128)S(1)}, f32[32,384]{1,0:T(8,128)S(1)}, u32[]{:S(2)}, u32[]{:S(2)}) collective-permute-start(f32[32,384]{1,0:T(8,128)S(1)} %get-tuple-element.30), channel_id=1, source_target_pairs={{1,2},{2,1},{3,4},{4,3},{5,6},{6,5},{9,10},{10,9},{11,12},{12,11},... | collective-permute-start | bytes 147464 | tf_op jit(solution)/shard_map/ppermute | solution.py:37

commit v3 on v2

--- a/solution.py
+++ b/solution.py
@@ -7,6 +7,7 @@
 from jax.experimental.pallas import tpu as pltpu
 from jax.sharding import PartitionSpec as P
 
+
 NZ = 48
 STEPS = 6
 RADIUS = 8
@@ -23,19 +24,27 @@
 HALO = STEPS
 SIDE = up_to(HALO * NZ, LANE)
 REACH = RADIUS * NZ
-
-
-def swap_pairs(count, first):
-    pairs = []
-    for i in range(first, count - 1, 2):
-        pairs += [(i, i + 1), (i + 1, i)]
-    return pairs
-
-
-def swap(to_a, to_b, axis):
-    count = lax.axis_size(axis)
-    from_b = lax.ppermute(to_b, axis, swap_pairs(count, 1))
-    from_a = lax.ppermute(to_a, axis, swap_pairs(count, 0))
+AXES = ("gx", "gy")
+PACK_LIMIT = 58
+
+
+def neighbours(axis, other, first, fill):
+    count, wide = lax.axis_size(axis), lax.axis_size(other)
+    pairs = [((i, j), (i + 1, j)) for i in range(first, count - 1, 2) for j in range(wide)]
+    if fill and wide % 2 == 0:
+        paired = {i for i, _ in (p for pair in pairs for p in pair)}
+        idle = [i for i in range(count) if i not in paired]
+        pairs += [((i, j), (i, j + 1)) for i in idle for j in range(0, wide, 2)]
+    route = []
+    for (i, j), (k, m) in pairs:
+        one, two = (i * wide + j, k * wide + m) if axis == AXES[0] else (j * count + i, m * count + k)
+        route += [(one, two), (two, one)]
+    return route
+
+
+def swap(to_a, to_b, axis, other, fill=True):
+    from_b = lax.ppermute(to_b, AXES, neighbours(axis, other, 1, fill))
+    from_a = lax.ppermute(to_a, AXES, neighbours(axis, other, 0, fill))
     return from_a, from_b
 
 
@@ -43,7 +52,21 @@
     return lax.rem(lax.axis_index(axis), 2) == 0
 
 
-def call(body, outs, ins, scratch=(), limit=16):
+def sorter(axis):
+    index = lax.axis_index(axis)
+    even = lax.rem(index, 2) == 0
+    starts, ends = index == 0, index == lax.axis_size(axis) - 1
+
+    def low(a, b):
+        return jnp.where(starts, 0.0, jnp.where(even, b, a))
+
+    def high(a, b):
+        return jnp.where(ends, 0.0, jnp.where(even, a, b))
+
+    return low, high
+
+
+def call(body, outs, ins, scratch=(), limit=16, aliases=None, cost=2**20):
     vmem = pl.BlockSpec(memory_space=pltpu.VMEM)
     return pl.pallas_call(
         body,
@@ -51,20 +74,43 @@
         in_specs=[vmem] * len(ins),
         out_specs=[vmem] * len(outs),
         scratch_shapes=list(scratch),
+        input_output_aliases=aliases or {},
+        cost_estimate=pl.CostEstimate(flops=cost, bytes_accessed=cost, transcendentals=0),
         compiler_params=pltpu.CompilerParams(vmem_limit_bytes=limit * 2**20),
     )(*ins)
+
+
+FULL = HALO - 1
+EXTRA = 3
+
+
+def columns_of(t, e, row):
+    rows = slice(row, row + 1)
+    return [
+        (t[c, rows] * e[0, rows] + t[3 + c, rows] * e[1, rows]) + t[6 + c, rows] * e[2, rows] for c in range(3)
+    ]
 
 
 def pack_rows(first_e, last_e, first_h, last_h, first_t, last_t, to_a, to_b):
     even = is_even("gx")
     at = 0
+
+    def put(head, tail):
+        nonlocal at
+        size = head.shape[0]
+        to_a[at : at + size, :] = jnp.where(even, tail, head)
+        to_b[at : at + size, :] = jnp.where(even, head, tail)
+        at += size
+
     for first, last in ((first_e, last_e), (first_h, last_h), (first_t, last_t)):
         for c in range(first.shape[0]):
-            head = first[c, 0:HALO, :]
-            tail = last[c, SUB - HALO : SUB, :]
-            to_a[at : at + HALO, :] = jnp.where(even, tail, head)
-            to_b[at : at + HALO, :] = jnp.where(even, head, tail)
-            at += HALO
+            put(first[c, 0:FULL, :], last[c, SUB - FULL : SUB, :])
+    ahead = columns_of(first_t, first_e, FULL)
+    row = SUB - HALO
+    g = columns_of(last_t, last_e, row)
+    put(ahead[1], g[0])
+    put(ahead[2], last_h[1, row : row + 1] - courant * g[2])
+    put(jnp.zeros_like(g[0]), last_h[2, row : row + 1] + courant * g[1])
 
 
 def pack_x(electric, magnetic, tensor):
@@ -75,15 +121,16 @@
         for block in (0, rows // SUB - 1):
             ins.append(part)
             specs.append(pl.BlockSpec((part.shape[0], SUB, width), lambda i, block=block: (0, block, 0)))
-    packed = HALO * sum(part.shape[0] for part in parts)
+    packed = FULL * sum(part.shape[0] for part in parts) + EXTRA
     out = jax.ShapeDtypeStruct((packed, width), jnp.float32)
     return pl.pallas_call(
         pack_rows,
+        name="pack_x",
         grid=(1,),
         out_shape=[out, out],
         in_specs=specs,
         out_specs=[pl.BlockSpec((packed, width), lambda i: (0, 0))] * 2,
-        compiler_params=pltpu.CompilerParams(vmem_limit_bytes=8 * 2**20),
+        compiler_params=pltpu.CompilerParams(vmem_limit_bytes=PACK_LIMIT * 2**20),
     )(*ins)
 
 
@@ -106,45 +153,68 @@
     return call(functools.partial(pack_lanes, size), [out, out], ins)
 
 
-def main_body(
-    e_in, h_in, t_in, saved, xa, xb, ya, yb, ca, cb, inverse, e_out, h_out, scaled, to_a, to_b, fe, fh, ft
-):
+def place_rows(full_e, full_h, full_t, rows, lanes, low, high):
+    fields = [(full_e, c, None) for c in range(3)] + [(full_h, c, courant) for c in range(3)]
+    fields += [(full_t, c, courant * courant) for c in range(9)]
+    top, bottom = slice(SUB - FULL, SUB), slice(SUB + rows, SUB + rows + FULL)
+    for k, (full, c, factor) in enumerate(fields):
+        packet = slice(k * FULL, (k + 1) * FULL)
+        for at, get in ((top, low), (bottom, high)):
+            value = get(packet)
+            full[c, at, lanes] = value if factor is None else value * factor
+    base = len(fields) * FULL
+    extra = [slice(base + i, base + i + 1) for i in range(EXTRA)]
+    top, bottom = slice(SUB - HALO, SUB - FULL), slice(SUB + rows + FULL, SUB + rows + HALO)
+    full_t[0, top, lanes] = low(extra[0]) * (courant * courant)
+    full_h[1, top, lanes] = low(extra[1]) * courant
+    full_h[2, top, lanes] = low(extra[2]) * courant
+    full_t[1, bottom, lanes] = high(extra[0]) * (courant * courant)
+    full_t[2, bottom, lanes] = high(extra[1]) * (courant * courant)
+    one = jnp.ones_like(low(extra[0]))
+    full_e[0, top, lanes] = one
+    full_e[0, bottom, lanes] = one
+
+
+def assemble_body(e_in, h_in, t_in, xa, xb, ya, yb, fe, fh, ft):
     rows, width = e_in.shape[1:]
     total_rows, total = fe.shape[1:]
-    tiles = total_rows // SUB
-    even_x, even_y = is_even("gx"), is_even("gy")
+    low_x, high_x = sorter("gx")
+    low_y, high_y = sorter("gy")
     inner = slice(SUB, SUB + rows)
     middle = slice(SIDE, SIDE + width)
     left, right = slice(0, SIDE), slice(SIDE + width, total)
     top, bottom = slice(0, SUB), slice(SUB + rows, total_rows)
-    top_in = slice(SUB - HALO, SUB)
-    bottom_in = slice(SUB + rows, SUB + rows + HALO)
-
     k = 0
     for own, full, factor in ((e_in, fe, None), (h_in, fh, courant), (t_in, ft, courant * courant)):
         for c in range(own.shape[0]):
-
-            def put(where_rows, where_lanes, value, full=full, c=c, factor=factor):
-                full[c, where_rows, where_lanes] = value if factor is None else value * factor
-
-            packed = slice(k * HALO, (k + 1) * HALO)
             full[c, top, :] = jnp.zeros((SUB, total), jnp.float32)
             full[c, bottom, :] = jnp.zeros((SUB, total), jnp.float32)
-            put(inner, middle, own[c])
-            a, b = ya[k], yb[k]
-            put(inner, left, jnp.where(even_y, b, a))
-            put(inner, right, jnp.where(even_y, a, b))
-            a, b = xa[packed], xb[packed]
-            put(top_in, middle, jnp.where(even_x, b, a))
-            put(bottom_in, middle, jnp.where(even_x, a, b))
-            aa, ab, ba, bb = ca[0, packed], cb[0, packed], ca[1, packed], cb[1, packed]
-            left_a, left_b = jnp.where(even_y, ab, aa), jnp.where(even_y, bb, ba)
-            put(top_in, left, jnp.where(even_x, left_b, left_a))
-            put(bottom_in, left, jnp.where(even_x, left_a, left_b))
-            right_a, right_b = jnp.where(even_y, aa, ab), jnp.where(even_y, ba, bb)
-            put(top_in, right, jnp.where(even_x, right_b, right_a))
-            put(bottom_in, right, jnp.where(even_x, right_a, right_b))
+            for lanes, value in (
+                (middle, own[c]),
+                (left, low_y(ya[k], yb[k])),
+                (right, high_y(ya[k], yb[k])),
+            ):
+                full[c, inner, lanes] = value if factor is None else value * factor
             k += 1
+    place_rows(fe, fh, ft, rows, middle, lambda s: low_x(xa[s], xb[s]), lambda s: high_x(xa[s], xb[s]))
+
+
+def main_body(fe_in, fh_in, ft_in, saved, ca, cb, inverse, fe, fh, ft, scaled, to_a, to_b):
+    del fe_in, fh_in, ft_in
+    rows, width = scaled.shape
+    total_rows, total = fe.shape[1:]
+    tiles = total_rows // SUB
+    middle = slice(SIDE, SIDE + width)
+    low_x, high_x = sorter("gx")
+    low_y, high_y = sorter("gy")
+    even_x = is_even("gx")
+
+    for lanes, side in ((slice(0, SIDE), low_y), (slice(SIDE + width, total), high_y)):
+
+        def of(s, pick, side=side):
+            return pick(side(ca[0, s], cb[0, s]), side(ca[1, s], cb[1, s]))
+
+        place_rows(fe, fh, ft, rows, lanes, lambda s, of=of: of(s, low_x), lambda s, of=of: of(s, high_x))
 
     inside_x = jnp.where(lax.axis_index("gx") > 0, 1.0, 0.0).astype(jnp.float32)
     inside_y = jnp.where(lax.axis_index("gy") > 0, 1.0, 0.0).astype(jnp.float32)
@@ -233,26 +303,17 @@
             term = (e[0] * s[0] + e[1] * s[1]) + e[2] * s[2]
             scaled[at] = term if step == 0 else scaled[at] + term
 
-    for c in range(3):
-        e_out[c] = fe[c, inner, middle]
-        h_out[c] = fh[c, inner, middle] * (1.0 / courant)
     scaled[...] = scaled[...] * inverse[...]
     head, tail = scaled[:RADIUS], scaled[rows - RADIUS :]
     to_a[...] = jnp.where(even_x, tail, head)
     to_b[...] = jnp.where(even_x, head, tail)
 
 
-def run_steps(electric, magnetic, tensor, saved, xa, xb, ya, yb, ca, cb, inverse):
-    rows, width = electric.shape[1:]
-    full = (rows + 2 * SUB, width + 2 * SIDE)
-    edge = (RADIUS, width)
-    return call(
-        main_body,
-        [electric.shape, magnetic.shape, (rows, width), edge, edge],
-        (electric, magnetic, tensor, saved, xa, xb, ya, yb, ca, cb, inverse),
-        [pltpu.VMEM((n, *full), jnp.float32) for n in (3, 3, 9)],
-        limit=28,
-    )
+def emit_body(fe, fh, e_out, h_out):
+    rows, width = e_out.shape[1:]
+    for c in range(3):
+        e_out[c] = fe[c, SUB : SUB + rows, SIDE : SIDE + width]
+        h_out[c] = fh[c, SUB : SUB + rows, SIDE : SIDE + width] * (1.0 / courant)
 
 
 def box(values, unit, axis):
@@ -269,10 +330,10 @@
 
 def filter_rows(scaled, xa, xb, across, to_a, to_b):
     rows, width = scaled.shape
-    even_x, even_y = is_even("gx"), is_even("gy")
+    even_y = is_even("gy")
+    low, high = sorter("gx")
     a, b = xa[...], xb[...]
-    low, high = jnp.where(even_x, b, a), jnp.where(even_x, a, b)
-    extended = jnp.concatenate([low, scaled[...], high], axis=0)
+    extended = jnp.concatenate([low(a, b), scaled[...], high(a, b)], axis=0)
     result = box(box(extended, 1, 0), 1, 0)[:rows] * (1.0 / (RADIUS + 1.0))
     across[...] = result
     head, tail = result[:, :REACH], result[:, width - REACH :]
@@ -282,12 +343,11 @@
 
 def filter_columns(across, ya, yb, gradient):
     width = across.shape[1]
-    even_y = is_even("gy")
+    low, high = sorter("gy")
     for r in range(across.shape[0] // SUB):
         at = slice(r * SUB, (r + 1) * SUB)
         a, b = ya[at], yb[at]
-        low, high = jnp.where(even_y, b, a), jnp.where(even_y, a, b)
-        extended = jnp.concatenate([low, across[at], high], axis=1)
+        extended = jnp.concatenate([low(a, b), across[at], high(a, b)], axis=1)
         gradient[at] = box(box(extended, NZ, 1), NZ, 1)[:, :width] * (1.0 / (RADIUS + 1.0))
 
 
@@ -307,22 +367,31 @@
     rows, width = electric.shape[1:]
     cols = width // NZ
     edge = (RADIUS, width)
-
-    xa, xb = swap(*pack_x(electric, magnetic, tensor), "gx")
-    ya, yb = swap(*pack_y(SIDE, electric, magnetic, tensor), "gy")
-    ca, cb = swap(*pack_y(SIDE, xa[None], xb[None]), "gy")
+    full = (rows + 2 * SUB, width + 2 * SIDE)
+    fulls = [(n, *full) for n in (3, 3, 9)]
+
+    xa, xb = swap(*pack_x(electric, magnetic, tensor), "gx", "gy")
+    ya, yb = swap(*pack_y(SIDE, electric, magnetic, tensor), "gy", "gx", fill=False)
+    ca, cb = swap(*pack_y(SIDE, xa[None], xb[None]), "gy", "gx")
 
     row_places = lax.axis_index("gx") * rows + lax.broadcasted_iota(jnp.int32, (rows, width), 0)
     col_places = lax.axis_index("gy") * cols + lax.broadcasted_iota(jnp.int32, (rows, width), 1) // NZ
     cover = coverage(row_places, lax.axis_size("gx") * rows) * coverage(col_places, lax.axis_size("gy") * cols)
 
-    e, h, scaled, to_a, to_b = run_steps(
-        electric, magnetic, tensor, saved, xa, xb, ya, yb, ca, cb, 1.0 / cover
+    fields = call(assemble_body, fulls, (electric, magnetic, tensor, xa, xb, ya, yb), cost=2**22)
+    fe, fh, _, scaled, to_a, to_b = call(
+        main_body,
+        [*fulls, (rows, width), edge, edge],
+        (*fields, saved, ca, cb, 1.0 / cover),
+        limit=20,
+        aliases={0: 0, 1: 1, 2: 2},
+        cost=2**23,
     )
-    xa, xb = swap(to_a, to_b, "gx")
+    xa, xb = swap(to_a, to_b, "gx", "gy")
+    e, h = call(emit_body, [electric.shape, magnetic.shape], (fe, fh))
     side = (rows, REACH)
     across, to_a, to_b = call(filter_rows, [(rows, width), side, side], (scaled, xa, xb))
-    ya, yb = swap(to_a, to_b, "gy")
+    ya, yb = swap(to_a, to_b, "gy", "gx")
     (gradient,) = call(filter_columns, [(rows, width)], (across, ya, yb))
     return e, h, gradient
 

time: 55.1 us -> 47 us (0.85)
  starting transfers between devices: 18.1 us -> 10.6 us
  waiting for transfers between devices: 22.3 us -> 19.1 us
  Pallas kernels: 10.3 us -> 12.6 us
    ppermute x10, starting transfers between devices: 18.1 us -> 10.6 us  [the longest x5 7.88 us: swap(): from_b = lax.ppermute(to_b, AXES, neighbours(axis, other, 1, fill))]
    ppermute x10, waiting for transfers between devices: 22.3 us -> 19.1 us  [the longest x5 11.1 us: swap(): from_b = lax.ppermute(to_b, AXES, neighbours(axis, other, 1, fill))]
    pallas_call x1, Pallas kernels: 0.15 us -> 2.1 us  [pack_x(): pl.pallas_call(pack_rows, name='pack_x', grid=(1,), out_shape=[out, out],...]
    pallas_call x5 -> x7, Pallas kernels: 10.1 us -> 10.5 us  [call(): pl.pallas_call(body, out_shape=[jax.ShapeDtypeStruct(s, jnp.float32) for...]
  transfers between devices with their start and end apart: 10 -> 10, of which waited for: 6 -> 6; matrix products, arithmetic and copies ran while one was open for 0% -> 0% of each run, Pallas kernels for 2% -> 12%
where the time goes in v3:
time: 47 us; the launch traced here: 46.3 us
  waiting for transfers between devices  19.1 us (41%)
  Pallas kernels  12.6 us (27%)
  starting transfers between devices  10.6 us (23%)
  local copies, waits for them, and re-layouts  3.1 us (7%)
  between operations  0.75 us (2%)
    ppermute x5, waiting for transfers between devices, swap(): from_b = lax.ppermute(to_b, AXES, neighbours(axis, other, 1, fill))  11.1 us
    pallas_call x7, Pallas kernels, call(): pl.pallas_call(body, out_shape=[jax.ShapeDtypeStruct(s, jnp.float32) for...  10.5 us
    ppermute x5, waiting for transfers between devices, swap(): from_a = lax.ppermute(to_a, AXES, neighbours(axis, other, 0, fill))  8.01 us
    ppermute x5, starting transfers between devices, swap(): from_b = lax.ppermute(to_b, AXES, neighbours(axis, other, 1, fill))  7.88 us
    unnamed x14, local copies, waits for them, and re-layouts  3.1 us
    ppermute x5, starting transfers between devices, swap(): from_a = lax.ppermute(to_a, AXES, neighbours(axis, other, 0, fill))  2.73 us
    pallas_call x1, Pallas kernels, pack_x(): pl.pallas_call(pack_rows, name='pack_x', grid=(1,), out_shape=[out, out],...  2.1 us
  transfers between devices with their start and end apart: 10, of which 6 were waited for; matrix products, arithmetic and copies ran while one was open for 0% of the time, Pallas kernels for 12%

profile of v3, /device:TPU:11, one launch (start us, length us, event | category | flops | bytes accessed | tf_op | source)
XLA Modules:
  0.0 46.3 jit_solution(480502622041147425)
XLA Ops:
  0.6 0.0 copy-start
  0.6 1.2 %copy-done = f32[9,32,768]{2,1,0:T(8,128)S(1)} copy-done((f32[9,32,768]{2,1,0:T(8,128)S(1)}, f32[9,32,768]{2,1,0:T(8,128)}, u32[]{:S(2)}) %copy-start) | copy-done | bytes 884760
  1.8 0.0 copy-start.2
  1.8 1.0 %copy-done.2 = f32[3,32,768]{2,1,0:T(8,128)S(1)} copy-done((f32[3,32,768]{2,1,0:T(8,128)S(1)}, f32[3,32,768]{2,1,0:T(8,128)}, u32[]{:S(2)}) %copy-start.2) | copy-done | bytes 294936
  2.8 0.0 copy-start.4
  2.8 1.0 %copy-done.4 = f32[3,32,768]{2,1,0:T(8,128)S(1)} copy-done((f32[3,32,768]{2,1,0:T(8,128)S(1)}, f32[3,32,768]{2,1,0:T(8,128)}, u32[]{:S(2)}) %copy-start.4) | copy-done | bytes 294936
  3.7 0.0 copy-start.1
  3.7 0.0 copy-start.3
  3.7 0.0 copy-start.5
  3.7 1.2 %shard_map.67 = (f32[15,32,384]{2,1,0:T(8,128)}, f32[15,32,384]{2,1,0:T(8,128)}) custom-call(f32[3,32,768]{2,1,0:T(8,128)S(1)} %copy-done.2, f32[3,32,768]{2,1,0:T(8,128)S(1)} %copy-done.4, f32[9,32,768]{2,1,0:T(8,128)S(1)} %copy-done), custom_call_target="tpu_custom_call" | custom-call | flops 1048576 | bytes 1048576 | tf_op jit(solution)/shard_map/pallas_call | solution.py:71
  5.0 0.7 %collective-permute-start.2 = (f32[15,32,384]{2,1,0:T(8,128)}, f32[15,32,384]{2,1,0:T(8,128)}, u32[]{:S(2)}, u32[]{:S(2)}) collective-permute-start(f32[15,32,384]{2,1,0:T(8,128)} %get-tuple-element.24), channel_id=1, source_target_pairs={{0,1},{1,0},{8,9},{9,8},{16,17},{17,16},{24,25},{25,24},{2,3},{3,2... | collective-permute-start | bytes 2211848 | tf_op jit(solution)/shard_map/ppermute | solution.py:47
  5.6 3.1 %collective-permute-start.3 = (f32[15,32,384]{2,1,0:T(8,128)}, f32[15,32,384]{2,1,0:T(8,128)}, u32[]{:S(2)}, u32[]{:S(2)}) collective-permute-start(f32[15,32,384]{2,1,0:T(8,128)} %get-tuple-element.25), channel_id=1, source_target_pairs={{1,2},{2,1},{9,10},{10,9},{17,18},{18,17},{25,26},{26,25},{3,4},{4... | collective-permute-start | bytes 2211848 | tf_op jit(solution)/shard_map/ppermute | solution.py:46
  8.7 2.1 %pack_x.1 = (f32[78,768]{1,0:T(8,128)}, f32[78,768]{1,0:T(8,128)}) custom-call(f32[3,32,768]{2,1,0:T(8,128)} %e_in.1, f32[3,32,768]{2,1,0:T(8,128)} %e_in.1, f32[3,32,768]{2,1,0:T(8,128)} %h_in.1, f32[3,32,768]{2,1,0:T(8,128)} %h_in.1, f32[9,32,768]{2,1,0:T(8,128)} %t_in.1, f32[9,32,768]{2,1,0:T(8,128)} %t_in.1), custom_call_target="tpu_custom_call" | custom-call | tf_op jit(solution)/shard_map/pack_x/pallas_call | solution.py:126
  10.8 0.0 copy-start.6
  10.8 0.3 collective-permute-start
  11.1 2.2 %collective-permute-start.1 = (f32[78,768]{1,0:T(8,128)}, f32[78,768]{1,0:T(8,128)S(1)}, u32[]{:S(2)}, u32[]{:S(2)}) collective-permute-start(f32[78,768]{1,0:T(8,128)} %get-tuple-element.23), channel_id=1, source_target_pairs={{8,16},{16,8},{9,17},{17,9},{10,18},{18,10},{11,19},{19,11},{12,20... | collective-permute-start | bytes 718856 | tf_op jit(solution)/shard_map/ppermute | solution.py:46
  13.3 5.4 %collective-permute-done.xa = f32[78,768]{1,0:T(8,128)S(1)} collective-permute-done((f32[78,768]{1,0:T(8,128)}, f32[78,768]{1,0:T(8,128)S(1)}, u32[]{:S(2)}, u32[]{:S(2)}) %collective-permute-start) | collective-permute-done | bytes 239648 | tf_op jit(solution)/shard_map/ppermute | solution.py:47
  18.7 6.2 %collective-permute-done.1.xb = f32[78,768]{1,0:T(8,128)S(1)} collective-permute-done((f32[78,768]{1,0:T(8,128)}, f32[78,768]{1,0:T(8,128)S(1)}, u32[]{:S(2)}, u32[]{:S(2)}) %collective-permute-start.1) | collective-permute-done | bytes 239648 | tf_op jit(solution)/shard_map/ppermute | solution.py:46
  24.9 0.8 %shard_map.69 = (f32[2,78,384]{2,1,0:T(8,128)}, f32[2,78,384]{2,1,0:T(8,128)}) custom-call(f32[1,78,768]{2,1,0:T(8,128)S(1)} %bitcast.2, f32[1,78,768]{2,1,0:T(8,128)S(1)} %bitcast.3), custom_call_target="tpu_custom_call" | custom-call | flops 1048576 | bytes 1048576 | tf_op jit(solution)/shard_map/pallas_call | solution.py:71
  25.7 0.4 collective-permute-start.4
  26.1 1.3 %collective-permute-start.5 = (f32[2,78,384]{2,1,0:T(8,128)}, f32[2,78,384]{2,1,0:T(8,128)S(1)}, u32[]{:S(2)}, u32[]{:S(2)}) collective-permute-start(f32[2,78,384]{2,1,0:T(8,128)} %get-tuple-element.30), channel_id=1, source_target_pairs={{1,2},{2,1},{9,10},{10,9},{17,18},{18,17},{25,26},{26,25},{3,4},{4... | collective-permute-start | bytes 718856 | tf_op jit(solution)/shard_map/ppermute | solution.py:46
  27.5 0.1 multiply_divide_fusion.inverse
  27.6 0.0 collective-permute-done.2.ya
  27.6 0.0 collective-permute-done.3.yb
  27.6 0.0 copy-done.1
  27.6 0.0 copy-done.3
  27.6 0.0 copy-done.5
  27.6 1.9 %shard_map.68 = (f32[3,48,1536]{2,1,0:T(8,128)S(1)}, f32[3,48,1536]{2,1,0:T(8,128)S(1)}, f32[9,48,1536]{2,1,0:T(8,128)S(1)}) custom-call(f32[3,32,768]{2,1,0:T(8,128)S(1)} %copy-done.3, f32[3,32,768]{2,1,0:T(8,128)S(1)} %copy-done.5, f32[9,32,768]{2,1,0:T(8,128)S(1)} %copy-done.1, f32[78,768]{1,0:T(8,128)S(1)} %collective-permute-done.xa, ...), custom_call_target="tpu_custom_call" | custom-call | flops 4194304 | bytes 4194304 | tf_op jit(solution)/shard_map/pallas_call | solution.py:71
  29.5 0.0 collective-permute-done.4.ca
  29.5 2.5 %collective-permute-done.5.cb = f32[2,78,384]{2,1,0:T(8,128)S(1)} collective-permute-done((f32[2,78,384]{2,1,0:T(8,128)}, f32[2,78,384]{2,1,0:T(8,128)S(1)}, u32[]{:S(2)}, u32[]{:S(2)}) %collective-permute-start.5) | collective-permute-done | bytes 239648 | tf_op jit(solution)/shard_map/ppermute | solution.py:46
  32.0 0.0 copy-done.6
  32.0 4.5 %shard_map.70 = (f32[3,48,1536]{2,1,0:T(8,128)S(1)}, f32[3,48,1536]{2,1,0:T(8,128)S(1)}, f32[9,48,1536]{2,1,0:T(8,128)S(1)}, f32[32,768]{1,0:T(8,128)S(1)}, f32[8,768]{1,0:T(8,128)S(1)}, /*index=5*/f32[8,768]{1,0:T(8,128)S(1)}) custom-call(f32[3,48,1536]{2,1,0:T(8,128)S(1)} %get-tuple-element.26.fe_in, ...), custom_call_target="tpu_custom_call", output_to_operand_aliasing={{0}: (0, {}), {1}: (1, {}), {2}: (2, {})} | custom-call | flops 8388608 | bytes 8388608 | tf_op jit(solution)/shard_map/pallas_call | solution.py:71
  36.5 0.1 collective-permute-start.6
  36.5 0.1 collective-permute-start.7
  36.6 2.6 %collective-permute-done.6.xa = f32[8,768]{1,0:T(8,128)S(1)} collective-permute-done((f32[8,768]{1,0:T(8,128)S(1)}, f32[8,768]{1,0:T(8,128)S(1)}, u32[]{:S(2)}, u32[]{:S(2)}) %collective-permute-start.6) | collective-permute-done | bytes 24608 | tf_op jit(solution)/shard_map/ppermute | solution.py:47
  39.2 1.0 %collective-permute-done.7.xb = f32[8,768]{1,0:T(8,128)S(1)} collective-permute-done((f32[8,768]{1,0:T(8,128)S(1)}, f32[8,768]{1,0:T(8,128)S(1)}, u32[]{:S(2)}, u32[]{:S(2)}) %collective-permute-start.7) | collective-permute-done | bytes 24608 | tf_op jit(solution)/shard_map/ppermute | solution.py:46
  40.2 0.1 shard_map.72
  40.3 1.3 %collective-permute-start.8 = (f32[32,384]{1,0:T(8,128)S(1)}, f32[32,384]{1,0:T(8,128)S(1)}, u32[]{:S(2)}, u32[]{:S(2)}) collective-permute-start(f32[32,384]{1,0:T(8,128)S(1)} %get-tuple-element.39), channel_id=1, source_target_pairs={{0,1},{1,0},{8,9},{9,8},{16,17},{17,16},{24,25},{25,24},{2,3},{3,2... | collective-permute-start | bytes 147464 | tf_op jit(solution)/shard_map/ppermute | solution.py:47
  41.6 1.3 %collective-permute-start.9 = (f32[32,384]{1,0:T(8,128)S(1)}, f32[32,384]{1,0:T(8,128)S(1)}, u32[]{:S(2)}, u32[]{:S(2)}) collective-permute-start(f32[32,384]{1,0:T(8,128)S(1)} %get-tuple-element.40), channel_id=1, source_target_pairs={{1,2},{2,1},{9,10},{10,9},{17,18},{18,17},{25,26},{26,25},{3,4},{4... | collective-permute-start | bytes 147464 | tf_op jit(solution)/shard_map/ppermute | solution.py:46
  42.9 0.9 %shard_map.71 = (f32[3,32,768]{2,1,0:T(8,128)}, f32[3,32,768]{2,1,0:T(8,128)}) custom-call(f32[3,48,1536]{2,1,0:T(8,128)S(1)} %get-tuple-element.31.fe, f32[3,48,1536]{2,1,0:T(8,128)S(1)} %get-tuple-element.32.fh), custom_call_target="tpu_custom_call" | custom-call | flops 1048576 | bytes 1048576 | tf_op jit(solution)/shard_map/pallas_call | solution.py:71
  43.7 0.0 collective-permute-done.8.ya
  43.7 1.4 %collective-permute-done.9.yb = f32[32,384]{1,0:T(8,128)S(1)} collective-permute-done((f32[32,384]{1,0:T(8,128)S(1)}, f32[32,384]{1,0:T(8,128)S(1)}, u32[]{:S(2)}, u32[]{:S(2)}) %collective-permute-start.9) | collective-permute-done | bytes 49184 | tf_op jit(solution)/shard_map/ppermute | solution.py:46
  45.1 1.2 %shard_map.73 = f32[32,768]{1,0:T(8,128)} custom-call(f32[32,768]{1,0:T(8,128)S(1)} %get-tuple-element.38.across, f32[32,384]{1,0:T(8,128)S(1)} %collective-permute-done.8.ya, f32[32,384]{1,0:T(8,128)S(1)} %collective-permute-done.9.yb), custom_call_target="tpu_custom_call" | custom-call | flops 1048576 | bytes 1048576 | tf_op jit(solution)/shard_map/pallas_call | solution.py:71
  (3 shorter events, 0.0 us)
Async XLA Ops:
  0.6 1.2 %copy-start = (f32[9,32,768]{2,1,0:T(8,128)S(1)}, f32[9,32,768]{2,1,0:T(8,128)}, u32[]{:S(2)}) copy-start(f32[9,32,768]{2,1,0:T(8,128)} %t_in.1) | copy-start | bytes 2654212
  1.8 1.0 %copy-start.2 = (f32[3,32,768]{2,1,0:T(8,128)S(1)}, f32[3,32,768]{2,1,0:T(8,128)}, u32[]{:S(2)}) copy-start(f32[3,32,768]{2,1,0:T(8,128)} %e_in.1) | copy-start | bytes 884740
  2.8 1.0 %copy-start.4 = (f32[3,32,768]{2,1,0:T(8,128)S(1)}, f32[3,32,768]{2,1,0:T(8,128)}, u32[]{:S(2)}) copy-start(f32[3,32,768]{2,1,0:T(8,128)} %h_in.1) | copy-start | bytes 884740
  3.7 23.9 %copy-start.1 = (f32[9,32,768]{2,1,0:T(8,128)S(1)}, f32[9,32,768]{2,1,0:T(8,128)}, u32[]{:S(2)}) copy-start(f32[9,32,768]{2,1,0:T(8,128)} %t_in.1) | copy-start | bytes 2654212
  3.7 23.9 %copy-start.3 = (f32[3,32,768]{2,1,0:T(8,128)S(1)}, f32[3,32,768]{2,1,0:T(8,128)}, u32[]{:S(2)}) copy-start(f32[3,32,768]{2,1,0:T(8,128)} %e_in.1) | copy-start | bytes 884740
  3.7 23.9 %copy-start.5 = (f32[3,32,768]{2,1,0:T(8,128)S(1)}, f32[3,32,768]{2,1,0:T(8,128)}, u32[]{:S(2)}) copy-start(f32[3,32,768]{2,1,0:T(8,128)} %h_in.1) | copy-start | bytes 884740
  5.0 22.6 %collective-permute-start.2 = (f32[15,32,384]{2,1,0:T(8,128)}, f32[15,32,384]{2,1,0:T(8,128)}, u32[]{:S(2)}, u32[]{:S(2)}) collective-permute-start(f32[15,32,384]{2,1,0:T(8,128)} %get-tuple-element.24), channel_id=1, source_target_pairs={{0,1},{1,0},{8,9},{9,8},{16,17},{17,16},{24,25},{25,24},{2,3},{3,2... | collective-permute-start | bytes 2211848 | tf_op jit(solution)/shard_map/ppermute | solution.py:47
  5.6 21.9 %collective-permute-start.3 = (f32[15,32,384]{2,1,0:T(8,128)}, f32[15,32,384]{2,1,0:T(8,128)}, u32[]{:S(2)}, u32[]{:S(2)}) collective-permute-start(f32[15,32,384]{2,1,0:T(8,128)} %get-tuple-element.25), channel_id=1, source_target_pairs={{1,2},{2,1},{9,10},{10,9},{17,18},{18,17},{25,26},{26,25},{3,4},{4... | collective-permute-start | bytes 2211848 | tf_op jit(solution)/shard_map/ppermute | solution.py:46
  10.8 21.1 %copy-start.6 = (bf16[6,3,32,768]{3,2,1,0:T(8,128)(2,1)S(1)}, bf16[6,3,32,768]{3,2,1,0:T(8,128)(2,1)}, u32[]{:S(2)}) copy-start(bf16[6,3,32,768]{3,2,1,0:T(8,128)(2,1)} %saved.1) | copy-start | bytes 2654212
  10.8 7.9 %collective-permute-start = (f32[78,768]{1,0:T(8,128)}, f32[78,768]{1,0:T(8,128)S(1)}, u32[]{:S(2)}, u32[]{:S(2)}) collective-permute-start(f32[78,768]{1,0:T(8,128)} %get-tuple-element.22), channel_id=1, source_target_pairs={{0,8},{8,0},{1,9},{9,1},{2,10},{10,2},{3,11},{11,3},{4,12},{12,4},... | collective-permute-start | bytes 718856 | tf_op jit(solution)/shard_map/ppermute | solution.py:47
  11.1 13.8 %collective-permute-start.1 = (f32[78,768]{1,0:T(8,128)}, f32[78,768]{1,0:T(8,128)S(1)}, u32[]{:S(2)}, u32[]{:S(2)}) collective-permute-start(f32[78,768]{1,0:T(8,128)} %get-tuple-element.23), channel_id=1, source_target_pairs={{8,16},{16,8},{9,17},{17,9},{10,18},{18,10},{11,19},{19,11},{12,20... | collective-permute-start | bytes 718856 | tf_op jit(solution)/shard_map/ppermute | solution.py:46
  25.7 3.8 %collective-permute-start.4 = (f32[2,78,384]{2,1,0:T(8,128)}, f32[2,78,384]{2,1,0:T(8,128)S(1)}, u32[]{:S(2)}, u32[]{:S(2)}) collective-permute-start(f32[2,78,384]{2,1,0:T(8,128)} %get-tuple-element.29), channel_id=1, source_target_pairs={{0,1},{1,0},{8,9},{9,8},{16,17},{17,16},{24,25},{25,24},{2,3},{3,2... | collective-permute-start | bytes 718856 | tf_op jit(solution)/shard_map/ppermute | solution.py:47
  26.1 5.8 %collective-permute-start.5 = (f32[2,78,384]{2,1,0:T(8,128)}, f32[2,78,384]{2,1,0:T(8,128)S(1)}, u32[]{:S(2)}, u32[]{:S(2)}) collective-permute-start(f32[2,78,384]{2,1,0:T(8,128)} %get-tuple-element.30), channel_id=1, source_target_pairs={{1,2},{2,1},{9,10},{10,9},{17,18},{18,17},{25,26},{26,25},{3,4},{4... | collective-permute-start | bytes 718856 | tf_op jit(solution)/shard_map/ppermute | solution.py:46
  36.5 2.7 %collective-permute-start.6 = (f32[8,768]{1,0:T(8,128)S(1)}, f32[8,768]{1,0:T(8,128)S(1)}, u32[]{:S(2)}, u32[]{:S(2)}) collective-permute-start(f32[8,768]{1,0:T(8,128)S(1)} %get-tuple-element.36), channel_id=1, source_target_pairs={{0,8},{8,0},{1,9},{9,1},{2,10},{10,2},{3,11},{11,3},{4,12},{12,4},... | collective-permute-start | bytes 73736 | tf_op jit(solution)/shard_map/ppermute | solution.py:47
  36.5 3.6 %collective-permute-start.7 = (f32[8,768]{1,0:T(8,128)S(1)}, f32[8,768]{1,0:T(8,128)S(1)}, u32[]{:S(2)}, u32[]{:S(2)}) collective-permute-start(f32[8,768]{1,0:T(8,128)S(1)} %get-tuple-element.37), channel_id=1, source_target_pairs={{8,16},{16,8},{9,17},{17,9},{10,18},{18,10},{11,19},{19,11},{12,20... | collective-permute-start | bytes 73736 | tf_op jit(solution)/shard_map/ppermute | solution.py:46
  40.3 3.4 %collective-permute-start.8 = (f32[32,384]{1,0:T(8,128)S(1)}, f32[32,384]{1,0:T(8,128)S(1)}, u32[]{:S(2)}, u32[]{:S(2)}) collective-permute-start(f32[32,384]{1,0:T(8,128)S(1)} %get-tuple-element.39), channel_id=1, source_target_pairs={{0,1},{1,0},{8,9},{9,8},{16,17},{17,16},{24,25},{25,24},{2,3},{3,2... | collective-permute-start | bytes 147464 | tf_op jit(solution)/shard_map/ppermute | solution.py:47
  41.6 3.5 %collective-permute-start.9 = (f32[32,384]{1,0:T(8,128)S(1)}, f32[32,384]{1,0:T(8,128)S(1)}, u32[]{:S(2)}, u32[]{:S(2)}) collective-permute-start(f32[32,384]{1,0:T(8,128)S(1)} %get-tuple-element.40), channel_id=1, source_target_pairs={{1,2},{2,1},{9,10},{10,9},{17,18},{18,17},{25,26},{26,25},{3,4},{4... | collective-permute-start | bytes 147464 | tf_op jit(solution)/shard_map/ppermute | solution.py:46

commit v4 on v3

--- a/solution.py
+++ b/solution.py
@@ -1,5 +1,3 @@
-import functools
-
 import jax
 import jax.numpy as jnp
 from jax import lax
@@ -23,9 +21,12 @@
 
 HALO = STEPS
 SIDE = up_to(HALO * NZ, LANE)
+WHOLE = HALO * NZ // LANE * LANE
+REST = HALO * NZ - WHOLE
+PER_TILE = LANE // REST
 REACH = RADIUS * NZ
 AXES = ("gx", "gy")
-PACK_LIMIT = 58
+PACK_LIMIT = 8
 
 
 def neighbours(axis, other, first, fill):
@@ -91,7 +92,17 @@
     ]
 
 
-def pack_rows(first_e, last_e, first_h, last_h, first_t, last_t, to_a, to_b):
+def pack_rows(e_hbm, h_hbm, t_hbm, to_a, to_b, e_rows, h_rows, t_rows, sems):
+    rows = e_hbm.shape[1]
+    copies = []
+    for n, (source, target) in enumerate(((e_hbm, e_rows), (h_hbm, h_rows), (t_hbm, t_rows))):
+        for side, begin in enumerate((0, rows - SUB)):
+            copies.append(
+                pltpu.make_async_copy(source.at[:, begin : begin + SUB, :], target.at[side], sems.at[n, side])
+            )
+            copies[-1].start()
+    for copy in copies:
+        copy.wait()
     even = is_even("gx")
     at = 0
 
@@ -102,55 +113,124 @@
         to_b[at : at + size, :] = jnp.where(even, head, tail)
         at += size
 
-    for first, last in ((first_e, last_e), (first_h, last_h), (first_t, last_t)):
-        for c in range(first.shape[0]):
-            put(first[c, 0:FULL, :], last[c, SUB - FULL : SUB, :])
-    ahead = columns_of(first_t, first_e, FULL)
+    for part in (e_rows, h_rows, t_rows):
+        for c in range(part.shape[1]):
+            put(part[0, c, 0:FULL, :], part[1, c, SUB - FULL : SUB, :])
+    ahead = columns_of(t_rows.at[0], e_rows.at[0], FULL)
     row = SUB - HALO
-    g = columns_of(last_t, last_e, row)
+    g = columns_of(t_rows.at[1], e_rows.at[1], row)
     put(ahead[1], g[0])
-    put(ahead[2], last_h[1, row : row + 1] - courant * g[2])
-    put(jnp.zeros_like(g[0]), last_h[2, row : row + 1] + courant * g[1])
+    put(ahead[2], h_rows[1, 1, row : row + 1] - courant * g[2])
+    put(jnp.zeros_like(g[0]), h_rows[1, 2, row : row + 1] + courant * g[1])
+    spare = to_a.shape[0] - at
+    nothing = jnp.zeros((spare, to_a.shape[1]), jnp.float32)
+    put(nothing, nothing)
 
 
 def pack_x(electric, magnetic, tensor):
-    rows, width = electric.shape[1:]
+    width = electric.shape[2]
     parts = (electric, magnetic, tensor)
-    ins, specs = [], []
-    for part in parts:
-        for block in (0, rows // SUB - 1):
-            ins.append(part)
-            specs.append(pl.BlockSpec((part.shape[0], SUB, width), lambda i, block=block: (0, block, 0)))
-    packed = FULL * sum(part.shape[0] for part in parts) + EXTRA
+    packed = up_to(FULL * sum(part.shape[0] for part in parts) + EXTRA, 2 * SUB)
     out = jax.ShapeDtypeStruct((packed, width), jnp.float32)
     return pl.pallas_call(
         pack_rows,
         name="pack_x",
-        grid=(1,),
         out_shape=[out, out],
-        in_specs=specs,
-        out_specs=[pl.BlockSpec((packed, width), lambda i: (0, 0))] * 2,
+        in_specs=[pl.BlockSpec(memory_space=pltpu.HBM)] * 3,
+        out_specs=[pl.BlockSpec(memory_space=pltpu.VMEM)] * 2,
+        scratch_shapes=[pltpu.VMEM((2, part.shape[0], SUB, width), jnp.float32) for part in parts]
+        + [pltpu.SemaphoreType.DMA((3, 2))],
         compiler_params=pltpu.CompilerParams(vmem_limit_bytes=PACK_LIMIT * 2**20),
-    )(*ins)
-
-
-def pack_lanes(size, *refs):
-    ins, (to_a, to_b) = refs[:-2], refs[-2:]
+    )(*parts)
+
+
+def quarters(parts):
+    slot = lax.broadcasted_iota(jnp.int32, parts[0][0].shape, 1) // REST
+    result = None
+    for n, (part, first) in enumerate(parts):
+        turn = (n * REST - first) % LANE
+        turned = pltpu.roll(part, turn, 1) if turn else part
+        result = turned if result is None else jnp.where(slot == n, turned, result)
+    return result
+
+
+def whole_and_rest(width, tail):
+    if tail:
+        return width - WHOLE, width - WHOLE - LANE, LANE - REST
+    return 0, WHOLE, 0
+
+
+def pack_lanes(e_in, h_in, t_in, to_a, to_b):
     even = is_even("gy")
-    at = 0
-    for ref in ins:
-        width = ref.shape[2]
-        for c in range(ref.shape[0]):
-            head = ref[c, :, 0:size]
-            tail = ref[c, :, width - size : width]
-            to_a[at] = jnp.where(even, tail, head)
-            to_b[at] = jnp.where(even, head, tail)
-            at += 1
-
-
-def pack_y(size, *ins):
-    out = (sum(x.shape[0] for x in ins), ins[0].shape[1], size)
-    return call(functools.partial(pack_lanes, size), [out, out], ins)
+    width = e_in.shape[2]
+    fields = [ref.at[c] for ref in (e_in, h_in, t_in) for c in range(ref.shape[0])]
+    made = []
+    for tail in (False, True):
+        whole, rest, first = whole_and_rest(width, tail)
+        blocks = [f[:, whole : whole + WHOLE] for f in fields]
+        for n in range(0, len(fields), PER_TILE):
+            blocks.append(quarters([(f[:, rest : rest + LANE], first) for f in fields[n : n + PER_TILE]]))
+        made.append(blocks)
+    count = len(fields)
+    for k, (head, tail) in enumerate(zip(*made)):
+        if k < count:
+            at, lanes = k, slice(0, WHOLE)
+        else:
+            at, half = count + (k - count) // 2, (k - count) % 2
+            lanes = slice(half * LANE, (half + 1) * LANE)
+        to_a[at, :, lanes] = jnp.where(even, tail, head)
+        to_b[at, :, lanes] = jnp.where(even, head, tail)
+
+
+def from_lanes(ref, k, count, tail):
+    group, slot = k // PER_TILE, k % PER_TILE
+    at, half = count + group // 2, group % 2
+    first = LANE - REST if tail else 0
+    turn = (first - slot * REST) % LANE
+    rest = ref[at, :, half * LANE : (half + 1) * LANE]
+    rest = pltpu.roll(rest, turn, 1) if turn else rest
+    whole = ref[k]
+    return jnp.concatenate([rest, whole] if tail else [whole, rest], axis=1)
+
+
+def pack_corners(xa, xb, to_a, to_b):
+    even = is_even("gy")
+    height, width = xa.shape
+    half = height // 2
+    made = []
+    for tail in (False, True):
+        whole, rest, first = whole_and_rest(width, tail)
+        pieces = [
+            (x[at : at + half, rest : rest + LANE], first) for x in (xa, xb) for at in (0, half)
+        ]
+        made.append((xa[:, whole : whole + WHOLE], xb[:, whole : whole + WHOLE], quarters(pieces)))
+    upper = up_to(half // 2, SUB)
+    for out, (blocks_even, blocks_odd) in ((to_a, (made[1], made[0])), (to_b, (made[0], made[1]))):
+        one, two, rest = (jnp.where(even, p, q) for p, q in zip(blocks_even, blocks_odd))
+        out[0:height] = one
+        out[height : 2 * height] = two
+        out[2 * height : 2 * height + upper, 0:LANE] = rest[:upper]
+        out[2 * height : 2 * height + half - upper, LANE:] = rest[upper:]
+        if 2 * upper > half:
+            out[2 * height + half - upper :, LANE:] = jnp.zeros((2 * upper - half, LANE), jnp.float32)
+
+
+def from_corners(ref, height, tail):
+    half = height // 2
+    upper = up_to(half // 2, SUB)
+    base = 2 * height
+    rest = jnp.concatenate([ref[base : base + upper, 0:LANE], ref[base : base + half - upper, LANE:]], axis=0)
+    first = LANE - REST if tail else 0
+    result = []
+    for n in range(2):
+        turned = []
+        for m in range(2):
+            turn = (first - (2 * n + m) * REST) % LANE
+            turned.append(pltpu.roll(rest, turn, 1) if turn else rest)
+        rest_n = jnp.concatenate(turned, axis=0)
+        whole = ref[n * height : (n + 1) * height]
+        result.append(jnp.concatenate([rest_n, whole] if tail else [whole, rest_n], axis=1))
+    return result
 
 
 def place_rows(full_e, full_h, full_t, rows, lanes, low, high):
@@ -175,7 +255,7 @@
     full_e[0, bottom, lanes] = one
 
 
-def assemble_body(e_in, h_in, t_in, xa, xb, ya, yb, fe, fh, ft):
+def assemble_body(e_in, h_in, t_in, xa, xb, ya, yb, fe, fh, ft, masks):
     rows, width = e_in.shape[1:]
     total_rows, total = fe.shape[1:]
     low_x, high_x = sorter("gx")
@@ -184,6 +264,7 @@
     middle = slice(SIDE, SIDE + width)
     left, right = slice(0, SIDE), slice(SIDE + width, total)
     top, bottom = slice(0, SUB), slice(SUB + rows, total_rows)
+    count = e_in.shape[0] + h_in.shape[0] + t_in.shape[0]
     k = 0
     for own, full, factor in ((e_in, fe, None), (h_in, fh, courant), (t_in, ft, courant * courant)):
         for c in range(own.shape[0]):
@@ -191,15 +272,18 @@
             full[c, bottom, :] = jnp.zeros((SUB, total), jnp.float32)
             for lanes, value in (
                 (middle, own[c]),
-                (left, low_y(ya[k], yb[k])),
-                (right, high_y(ya[k], yb[k])),
+                (left, low_y(from_lanes(ya, k, count, True), from_lanes(yb, k, count, True))),
+                (right, high_y(from_lanes(ya, k, count, False), from_lanes(yb, k, count, False))),
             ):
                 full[c, inner, lanes] = value if factor is None else value * factor
             k += 1
+    depth = lax.rem(lax.broadcasted_iota(jnp.int32, (SUB, total), 1) + (NZ - SIDE % NZ), NZ)
+    masks[0] = (depth != NZ - 1).astype(jnp.float32)
+    masks[1] = (depth != 0).astype(jnp.float32)
     place_rows(fe, fh, ft, rows, middle, lambda s: low_x(xa[s], xb[s]), lambda s: high_x(xa[s], xb[s]))
 
 
-def main_body(fe_in, fh_in, ft_in, saved, ca, cb, inverse, fe, fh, ft, scaled, to_a, to_b):
+def main_body(fe_in, fh_in, ft_in, masks, saved, ca, cb, inverse, fe, fh, ft, scaled, to_a, to_b):
     del fe_in, fh_in, ft_in
     rows, width = scaled.shape
     total_rows, total = fe.shape[1:]
@@ -209,12 +293,13 @@
     low_y, high_y = sorter("gy")
     even_x = is_even("gx")
 
-    for lanes, side in ((slice(0, SIDE), low_y), (slice(SIDE + width, total), high_y)):
-
-        def of(s, pick, side=side):
-            return pick(side(ca[0, s], cb[0, s]), side(ca[1, s], cb[1, s]))
-
-        place_rows(fe, fh, ft, rows, lanes, lambda s, of=of: of(s, low_x), lambda s, of=of: of(s, high_x))
+    height = up_to(FULL * 15 + EXTRA, 2 * SUB)
+    for lanes, side, tail in ((slice(0, SIDE), low_y, True), (slice(SIDE + width, total), high_y, False)):
+        packets = [
+            side(a, b) for a, b in zip(from_corners(ca, height, tail), from_corners(cb, height, tail))
+        ]
+        low, high = low_x(*packets), high_x(*packets)
+        place_rows(fe, fh, ft, rows, lanes, lambda s, low=low: low[s], lambda s, high=high: high[s])
 
     inside_x = jnp.where(lax.axis_index("gx") > 0, 1.0, 0.0).astype(jnp.float32)
     inside_y = jnp.where(lax.axis_index("gy") > 0, 1.0, 0.0).astype(jnp.float32)
@@ -226,9 +311,7 @@
         span = end - begin
         lanes = slice(begin, end)
         sub = lax.broadcasted_iota(jnp.int32, (SUB, span), 0)
-        depth = lax.rem(lax.broadcasted_iota(jnp.int32, (SUB, span), 1) + (begin % NZ), NZ)
-        upper = (depth != NZ - 1).astype(jnp.float32)
-        lower = (depth != 0).astype(jnp.float32)
+        upper, lower = masks[0, :, lanes], masks[1, :, lanes]
         low = SIDE - begin
         last = step == STEPS - 1
 
@@ -371,14 +454,19 @@
     fulls = [(n, *full) for n in (3, 3, 9)]
 
     xa, xb = swap(*pack_x(electric, magnetic, tensor), "gx", "gy")
-    ya, yb = swap(*pack_y(SIDE, electric, magnetic, tensor), "gy", "gx", fill=False)
-    ca, cb = swap(*pack_y(SIDE, xa[None], xb[None]), "gy", "gx")
+    count = electric.shape[0] + magnetic.shape[0] + tensor.shape[0]
+    packet = (count + -(-count // (2 * PER_TILE)), rows, WHOLE)
+    ya, yb = swap(*call(pack_lanes, [packet, packet], (electric, magnetic, tensor), limit=8), "gy", "gx", fill=False)
+    height = xa.shape[0]
+    packet = (2 * height + up_to(height // 4, SUB), WHOLE)
+    ca, cb = swap(*call(pack_corners, [packet, packet], (xa, xb), limit=8), "gy", "gx")
 
     row_places = lax.axis_index("gx") * rows + lax.broadcasted_iota(jnp.int32, (rows, width), 0)
     col_places = lax.axis_index("gy") * cols + lax.broadcasted_iota(jnp.int32, (rows, width), 1) // NZ
     cover = coverage(row_places, lax.axis_size("gx") * rows) * coverage(col_places, lax.axis_size("gy") * cols)
 
-    fields = call(assemble_body, fulls, (electric, magnetic, tensor, xa, xb, ya, yb), cost=2**22)
+    masks = (2, SUB, full[1])
+    fields = call(assemble_body, [*fulls, masks], (electric, magnetic, tensor, xa, xb, ya, yb), cost=2**22)
     fe, fh, _, scaled, to_a, to_b = call(
         main_body,
         [*fulls, (rows, width), edge, edge],

time: 47 us -> 40.8 us (0.87)
  the two profiles are of different devices: /device:TPU:11 before, /device:TPU:0 now
where the time goes in v4:
time: 40.8 us; the launch traced here: 40.5 us
  starting transfers between devices  17.5 us (43%)
  Pallas kernels  10.6 us (26%)
  waiting for transfers between devices  8.41 us (21%)
  local copies, waits for them, and re-layouts  3.1 us (8%)
  between operations  0.77 us (2%)
    ppermute x5, starting transfers between devices, swap(): from_b = lax.ppermute(to_b, AXES, neighbours(axis, other, 1, fill))  11.7 us
    pallas_call x7, Pallas kernels, call(): pl.pallas_call(body, out_shape=[jax.ShapeDtypeStruct(s, jnp.float32) for...  9.46 us
    ppermute x5, starting transfers between devices, swap(): from_a = lax.ppermute(to_a, AXES, neighbours(axis, other, 0, fill))  5.77 us
    ppermute x5, waiting for transfers between devices, swap(): from_a = lax.ppermute(to_a, AXES, neighbours(axis, other, 0, fill))  5.56 us
    unnamed x14, local copies, waits for them, and re-layouts  3.1 us
    ppermute x5, waiting for transfers between devices, swap(): from_b = lax.ppermute(to_b, AXES, neighbours(axis, other, 1, fill))  2.85 us
    pallas_call x1, Pallas kernels, pack_x(): pl.pallas_call(pack_rows, name='pack_x', out_shape=[out, out], in_specs=[...  1.15 us
  transfers between devices with their start and end apart: 10, of which 4 were waited for; matrix products, arithmetic and copies ran while one was open for 0% of the time, Pallas kernels for 10%

profile of v4, /device:TPU:0, one launch (start us, length us, event | category | flops | bytes accessed | tf_op | source)
XLA Modules:
  0.0 40.5 jit_solution(2827544315343220245)
XLA Ops:
  0.6 0.0 copy-start
  0.6 1.2 %copy-done = f32[9,32,768]{2,1,0:T(8,128)S(1)} copy-done((f32[9,32,768]{2,1,0:T(8,128)S(1)}, f32[9,32,768]{2,1,0:T(8,128)}, u32[]{:S(2)}) %copy-start) | copy-done | bytes 884760
  1.8 0.0 copy-start.2
  1.8 1.0 %copy-done.2 = f32[3,32,768]{2,1,0:T(8,128)S(1)} copy-done((f32[3,32,768]{2,1,0:T(8,128)S(1)}, f32[3,32,768]{2,1,0:T(8,128)}, u32[]{:S(2)}) %copy-start.2) | copy-done | bytes 294936
  2.8 0.0 copy-start.4
  2.8 1.0 %copy-done.4 = f32[3,32,768]{2,1,0:T(8,128)S(1)} copy-done((f32[3,32,768]{2,1,0:T(8,128)S(1)}, f32[3,32,768]{2,1,0:T(8,128)}, u32[]{:S(2)}) %copy-start.4) | copy-done | bytes 294936
  3.7 0.0 copy-start.1
  3.7 0.0 copy-start.3
  3.7 0.0 copy-start.5
  3.7 1.2 %pack_x.1 = (f32[80,768]{1,0:T(8,128)}, f32[80,768]{1,0:T(8,128)}) custom-call(f32[3,32,768]{2,1,0:T(8,128)S(1)} %copy-done.2, f32[3,32,768]{2,1,0:T(8,128)S(1)} %copy-done.4, f32[9,32,768]{2,1,0:T(8,128)S(1)} %copy-done), custom_call_target="tpu_custom_call" | custom-call | tf_op jit(solution)/shard_map/pack_x/pallas_call | solution.py:135
  4.9 0.0 copy-start.6
  4.9 3.0 %collective-permute-start = (f32[80,768]{1,0:T(8,128)}, f32[80,768]{1,0:T(8,128)S(1)}, u32[]{:S(2)}, u32[]{:S(2)}) collective-permute-start(f32[80,768]{1,0:T(8,128)} %get-tuple-element.23), channel_id=1, source_target_pairs={{0,8},{8,0},{1,9},{9,1},{2,10},{10,2},{3,11},{11,3},{4,12},{12,4},... | collective-permute-start | bytes 737288 | tf_op jit(solution)/shard_map/ppermute | solution.py:48
  7.9 0.0 collective-permute-start.1
  7.9 1.2 %shard_map.67 = (f32[17,32,256]{2,1,0:T(8,128)}, f32[17,32,256]{2,1,0:T(8,128)}) custom-call(f32[3,32,768]{2,1,0:T(8,128)S(1)} %copy-done.2, f32[3,32,768]{2,1,0:T(8,128)S(1)} %copy-done.4, f32[9,32,768]{2,1,0:T(8,128)S(1)} %copy-done), custom_call_target="tpu_custom_call" | custom-call | flops 1048576 | bytes 1048576 | tf_op jit(solution)/shard_map/pallas_call | solution.py:72
  9.2 0.5 %collective-permute-start.2 = (f32[17,32,256]{2,1,0:T(8,128)}, f32[17,32,256]{2,1,0:T(8,128)S(1)}, u32[]{:S(2)}, u32[]{:S(2)}) collective-permute-start(f32[17,32,256]{2,1,0:T(8,128)} %get-tuple-element.25), channel_id=1, source_target_pairs={{0,1},{1,0},{8,9},{9,8},{16,17},{17,16},{24,25},{25,24},{2,3},{3,2... | collective-permute-start | bytes 1671176 | tf_op jit(solution)/shard_map/ppermute | solution.py:48
  9.7 1.5 %collective-permute-start.3 = (f32[17,32,256]{2,1,0:T(8,128)}, f32[17,32,256]{2,1,0:T(8,128)}, u32[]{:S(2)}, u32[]{:S(2)}) collective-permute-start(f32[17,32,256]{2,1,0:T(8,128)} %get-tuple-element.26), channel_id=1, source_target_pairs={{1,2},{2,1},{9,10},{10,9},{17,18},{18,17},{25,26},{26,25},{3,4},{4... | collective-permute-start | bytes 1671176 | tf_op jit(solution)/shard_map/ppermute | solution.py:47
  11.2 3.8 %collective-permute-done.xa = f32[80,768]{1,0:T(8,128)S(1)} collective-permute-done((f32[80,768]{1,0:T(8,128)}, f32[80,768]{1,0:T(8,128)S(1)}, u32[]{:S(2)}, u32[]{:S(2)}) %collective-permute-start) | collective-permute-done | bytes 245792 | tf_op jit(solution)/shard_map/ppermute | solution.py:48
  15.0 0.0 collective-permute-done.1.xb
  15.0 0.1 shard_map.69
  15.1 0.1 collective-permute-start.4
  15.1 7.2 %collective-permute-start.5 = (f32[184,256]{1,0:T(8,128)S(1)}, f32[184,256]{1,0:T(8,128)S(1)}, u32[]{:S(2)}, u32[]{:S(2)}) collective-permute-start(f32[184,256]{1,0:T(8,128)S(1)} %get-tuple-element.32), channel_id=1, source_target_pairs={{1,2},{2,1},{9,10},{10,9},{17,18},{18,17},{25,26},{26,25},{3,4},{4... | collective-permute-start | bytes 565256 | tf_op jit(solution)/shard_map/ppermute | solution.py:47
  22.3 0.1 multiply_divide_fusion.inverse
  22.4 0.0 collective-permute-done.2.ya
  22.4 0.0 collective-permute-done.3.yb
  22.4 0.0 copy-done.1
  22.4 0.0 copy-done.3
  22.5 0.0 copy-done.5
  22.5 1.8 %shard_map.68 = (f32[3,48,1536]{2,1,0:T(8,128)S(1)}, f32[3,48,1536]{2,1,0:T(8,128)S(1)}, f32[9,48,1536]{2,1,0:T(8,128)S(1)}, f32[2,8,1536]{2,1,0:T(8,128)S(1)}) custom-call(f32[3,32,768]{2,1,0:T(8,128)S(1)} %copy-done.3, f32[3,32,768]{2,1,0:T(8,128)S(1)} %copy-done.5, f32[9,32,768]{2,1,0:T(8,128)S(1)} %copy-done.1, f32[80,768]{1,0:T(8,128)S(1)} %collective-permute-done.xa, ...), custom_call_target="tpu_custom_call" | custom-call | flops 4194304 | bytes 4194304 | tf_op jit(solution)/shard_map/pallas_call | solution.py:72
  24.2 0.0 collective-permute-done.4.ca
  24.2 1.6 %collective-permute-done.5.cb = f32[184,256]{1,0:T(8,128)S(1)} collective-permute-done((f32[184,256]{1,0:T(8,128)S(1)}, f32[184,256]{1,0:T(8,128)S(1)}, u32[]{:S(2)}, u32[]{:S(2)}) %collective-permute-start.5) | collective-permute-done | bytes 188448 | tf_op jit(solution)/shard_map/ppermute | solution.py:47
  25.9 0.0 copy-done.6
  25.9 4.3 %shard_map.70 = (f32[3,48,1536]{2,1,0:T(8,128)S(1)}, f32[3,48,1536]{2,1,0:T(8,128)S(1)}, f32[9,48,1536]{2,1,0:T(8,128)S(1)}, f32[32,768]{1,0:T(8,128)S(1)}, f32[8,768]{1,0:T(8,128)S(1)}, /*index=5*/f32[8,768]{1,0:T(8,128)S(1)}) custom-call(f32[3,48,1536]{2,1,0:T(8,128)S(1)} %get-tuple-element.27.fe_in, ...), custom_call_target="tpu_custom_call", output_to_operand_aliasing={{0}: (0, {}), {1}: (1, {}), {2}: (2, {})} | custom-call | flops 8388608 | bytes 8388608 | tf_op jit(solution)/shard_map/pallas_call | solution.py:72
  30.2 2.1 %collective-permute-start.6 = (f32[8,768]{1,0:T(8,128)S(1)}, f32[8,768]{1,0:T(8,128)S(1)}, u32[]{:S(2)}, u32[]{:S(2)}) collective-permute-start(f32[8,768]{1,0:T(8,128)S(1)} %get-tuple-element.38), channel_id=1, source_target_pairs={{0,8},{8,0},{1,9},{9,1},{2,10},{10,2},{3,11},{11,3},{4,12},{12,4},... | collective-permute-start | bytes 73736 | tf_op jit(solution)/shard_map/ppermute | solution.py:48
  32.2 0.0 collective-permute-start.7
  32.2 1.8 %collective-permute-done.6.xa = f32[8,768]{1,0:T(8,128)S(1)} collective-permute-done((f32[8,768]{1,0:T(8,128)S(1)}, f32[8,768]{1,0:T(8,128)S(1)}, u32[]{:S(2)}, u32[]{:S(2)}) %collective-permute-start.6) | collective-permute-done | bytes 24608 | tf_op jit(solution)/shard_map/ppermute | solution.py:48
  34.0 0.0 collective-permute-done.7.xb
  34.0 0.1 shard_map.72
  34.2 0.1 collective-permute-start.8
  34.2 3.1 %collective-permute-start.9 = (f32[32,384]{1,0:T(8,128)S(1)}, f32[32,384]{1,0:T(8,128)S(1)}, u32[]{:S(2)}, u32[]{:S(2)}) collective-permute-start(f32[32,384]{1,0:T(8,128)S(1)} %get-tuple-element.42), channel_id=1, source_target_pairs={{1,2},{2,1},{9,10},{10,9},{17,18},{18,17},{25,26},{26,25},{3,4},{4... | collective-permute-start | bytes 147464 | tf_op jit(solution)/shard_map/ppermute | solution.py:47
  37.3 0.9 %shard_map.71 = (f32[3,32,768]{2,1,0:T(8,128)}, f32[3,32,768]{2,1,0:T(8,128)}) custom-call(f32[3,48,1536]{2,1,0:T(8,128)S(1)} %get-tuple-element.33.fe, f32[3,48,1536]{2,1,0:T(8,128)S(1)} %get-tuple-element.34.fh), custom_call_target="tpu_custom_call" | custom-call | flops 1048576 | bytes 1048576 | tf_op jit(solution)/shard_map/pallas_call | solution.py:72
  38.2 0.0 collective-permute-done.8.ya
  38.2 1.2 %collective-permute-done.9.yb = f32[32,384]{1,0:T(8,128)S(1)} collective-permute-done((f32[32,384]{1,0:T(8,128)S(1)}, f32[32,384]{1,0:T(8,128)S(1)}, u32[]{:S(2)}, u32[]{:S(2)}) %collective-permute-start.9) | collective-permute-done | bytes 49184 | tf_op jit(solution)/shard_map/ppermute | solution.py:47
  39.4 1.2 %shard_map.73 = f32[32,768]{1,0:T(8,128)} custom-call(f32[32,768]{1,0:T(8,128)S(1)} %get-tuple-element.40.across, f32[32,384]{1,0:T(8,128)S(1)} %collective-permute-done.8.ya, f32[32,384]{1,0:T(8,128)S(1)} %collective-permute-done.9.yb), custom_call_target="tpu_custom_call" | custom-call | flops 1048576 | bytes 1048576 | tf_op jit(solution)/shard_map/pallas_call | solution.py:72
  (3 shorter events, 0.0 us)
Async XLA Ops:
  0.6 1.2 %copy-start = (f32[9,32,768]{2,1,0:T(8,128)S(1)}, f32[9,32,768]{2,1,0:T(8,128)}, u32[]{:S(2)}) copy-start(f32[9,32,768]{2,1,0:T(8,128)} %t_in.3) | copy-start | bytes 2654212
  1.8 1.0 %copy-start.2 = (f32[3,32,768]{2,1,0:T(8,128)S(1)}, f32[3,32,768]{2,1,0:T(8,128)}, u32[]{:S(2)}) copy-start(f32[3,32,768]{2,1,0:T(8,128)} %e_in.3) | copy-start | bytes 884740
  2.8 1.0 %copy-start.4 = (f32[3,32,768]{2,1,0:T(8,128)S(1)}, f32[3,32,768]{2,1,0:T(8,128)}, u32[]{:S(2)}) copy-start(f32[3,32,768]{2,1,0:T(8,128)} %h_in.3) | copy-start | bytes 884740
  3.7 18.7 %copy-start.1 = (f32[9,32,768]{2,1,0:T(8,128)S(1)}, f32[9,32,768]{2,1,0:T(8,128)}, u32[]{:S(2)}) copy-start(f32[9,32,768]{2,1,0:T(8,128)} %t_in.3) | copy-start | bytes 2654212
  3.7 18.7 %copy-start.3 = (f32[3,32,768]{2,1,0:T(8,128)S(1)}, f32[3,32,768]{2,1,0:T(8,128)}, u32[]{:S(2)}) copy-start(f32[3,32,768]{2,1,0:T(8,128)} %e_in.3) | copy-start | bytes 884740
  3.7 18.7 %copy-start.5 = (f32[3,32,768]{2,1,0:T(8,128)S(1)}, f32[3,32,768]{2,1,0:T(8,128)}, u32[]{:S(2)}) copy-start(f32[3,32,768]{2,1,0:T(8,128)} %h_in.3) | copy-start | bytes 884740
  4.9 21.0 %copy-start.6 = (bf16[6,3,32,768]{3,2,1,0:T(8,128)(2,1)S(1)}, bf16[6,3,32,768]{3,2,1,0:T(8,128)(2,1)}, u32[]{:S(2)}) copy-start(bf16[6,3,32,768]{3,2,1,0:T(8,128)(2,1)} %saved.1) | copy-start | bytes 2654212
  4.9 10.0 %collective-permute-start = (f32[80,768]{1,0:T(8,128)}, f32[80,768]{1,0:T(8,128)S(1)}, u32[]{:S(2)}, u32[]{:S(2)}) collective-permute-start(f32[80,768]{1,0:T(8,128)} %get-tuple-element.23), channel_id=1, source_target_pairs={{0,8},{8,0},{1,9},{9,1},{2,10},{10,2},{3,11},{11,3},{4,12},{12,4},... | collective-permute-start | bytes 737288 | tf_op jit(solution)/shard_map/ppermute | solution.py:48
  7.9 7.0 %collective-permute-start.1 = (f32[80,768]{1,0:T(8,128)}, f32[80,768]{1,0:T(8,128)S(1)}, u32[]{:S(2)}, u32[]{:S(2)}) collective-permute-start(f32[80,768]{1,0:T(8,128)} %get-tuple-element.24), channel_id=1, source_target_pairs={{8,16},{16,8},{9,17},{17,9},{10,18},{18,10},{11,19},{19,11},{12,20... | collective-permute-start | bytes 737288 | tf_op jit(solution)/shard_map/ppermute | solution.py:47
  9.2 13.3 %collective-permute-start.2 = (f32[17,32,256]{2,1,0:T(8,128)}, f32[17,32,256]{2,1,0:T(8,128)S(1)}, u32[]{:S(2)}, u32[]{:S(2)}) collective-permute-start(f32[17,32,256]{2,1,0:T(8,128)} %get-tuple-element.25), channel_id=1, source_target_pairs={{0,1},{1,0},{8,9},{9,8},{16,17},{17,16},{24,25},{25,24},{2,3},{3,2... | collective-permute-start | bytes 1671176 | tf_op jit(solution)/shard_map/ppermute | solution.py:48
  9.7 12.8 %collective-permute-start.3 = (f32[17,32,256]{2,1,0:T(8,128)}, f32[17,32,256]{2,1,0:T(8,128)}, u32[]{:S(2)}, u32[]{:S(2)}) collective-permute-start(f32[17,32,256]{2,1,0:T(8,128)} %get-tuple-element.26), channel_id=1, source_target_pairs={{1,2},{2,1},{9,10},{10,9},{17,18},{18,17},{25,26},{26,25},{3,4},{4... | collective-permute-start | bytes 1671176 | tf_op jit(solution)/shard_map/ppermute | solution.py:47
  15.1 9.2 %collective-permute-start.4 = (f32[184,256]{1,0:T(8,128)S(1)}, f32[184,256]{1,0:T(8,128)S(1)}, u32[]{:S(2)}, u32[]{:S(2)}) collective-permute-start(f32[184,256]{1,0:T(8,128)S(1)} %get-tuple-element.31), channel_id=1, source_target_pairs={{0,1},{1,0},{8,9},{9,8},{16,17},{17,16},{24,25},{25,24},{2,3},{3,2... | collective-permute-start | bytes 565256 | tf_op jit(solution)/shard_map/ppermute | solution.py:48
  15.1 10.7 %collective-permute-start.5 = (f32[184,256]{1,0:T(8,128)S(1)}, f32[184,256]{1,0:T(8,128)S(1)}, u32[]{:S(2)}, u32[]{:S(2)}) collective-permute-start(f32[184,256]{1,0:T(8,128)S(1)} %get-tuple-element.32), channel_id=1, source_target_pairs={{1,2},{2,1},{9,10},{10,9},{17,18},{18,17},{25,26},{26,25},{3,4},{4... | collective-permute-start | bytes 565256 | tf_op jit(solution)/shard_map/ppermute | solution.py:47
  30.2 3.9 %collective-permute-start.6 = (f32[8,768]{1,0:T(8,128)S(1)}, f32[8,768]{1,0:T(8,128)S(1)}, u32[]{:S(2)}, u32[]{:S(2)}) collective-permute-start(f32[8,768]{1,0:T(8,128)S(1)} %get-tuple-element.38), channel_id=1, source_target_pairs={{0,8},{8,0},{1,9},{9,1},{2,10},{10,2},{3,11},{11,3},{4,12},{12,4},... | collective-permute-start | bytes 73736 | tf_op jit(solution)/shard_map/ppermute | solution.py:48
  32.2 1.8 %collective-permute-start.7 = (f32[8,768]{1,0:T(8,128)S(1)}, f32[8,768]{1,0:T(8,128)S(1)}, u32[]{:S(2)}, u32[]{:S(2)}) collective-permute-start(f32[8,768]{1,0:T(8,128)S(1)} %get-tuple-element.39), channel_id=1, source_target_pairs={{8,16},{16,8},{9,17},{17,9},{10,18},{18,10},{11,19},{19,11},{12,20... | collective-permute-start | bytes 73736 | tf_op jit(solution)/shard_map/ppermute | solution.py:47
  34.2 4.0 %collective-permute-start.8 = (f32[32,384]{1,0:T(8,128)S(1)}, f32[32,384]{1,0:T(8,128)S(1)}, u32[]{:S(2)}, u32[]{:S(2)}) collective-permute-start(f32[32,384]{1,0:T(8,128)S(1)} %get-tuple-element.41), channel_id=1, source_target_pairs={{0,1},{1,0},{8,9},{9,8},{16,17},{17,16},{24,25},{25,24},{2,3},{3,2... | collective-permute-start | bytes 147464 | tf_op jit(solution)/shard_map/ppermute | solution.py:48
  34.2 5.1 %collective-permute-start.9 = (f32[32,384]{1,0:T(8,128)S(1)}, f32[32,384]{1,0:T(8,128)S(1)}, u32[]{:S(2)}, u32[]{:S(2)}) collective-permute-start(f32[32,384]{1,0:T(8,128)S(1)} %get-tuple-element.42), channel_id=1, source_target_pairs={{1,2},{2,1},{9,10},{10,9},{17,18},{18,17},{25,26},{26,25},{3,4},{4... | collective-permute-start | bytes 147464 | tf_op jit(solution)/shard_map/ppermute | solution.py:47

commit v5 on v4

--- a/solution.py
+++ b/solution.py
@@ -67,12 +67,15 @@
     return low, high
 
 
-def call(body, outs, ins, scratch=(), limit=16, aliases=None, cost=2**20):
+def call(body, outs, ins, scratch=(), limit=16, aliases=None, cost=2**20, far=()):
     vmem = pl.BlockSpec(memory_space=pltpu.VMEM)
+    hbm = pl.BlockSpec(memory_space=pltpu.HBM)
+    specs = [hbm if n in far else vmem for n in range(len(ins))]
+    ins = [pltpu.with_memory_space_constraint(x, pltpu.HBM) if n in far else x for n, x in enumerate(ins)]
     return pl.pallas_call(
         body,
         out_shape=[jax.ShapeDtypeStruct(s, jnp.float32) for s in outs],
-        in_specs=[vmem] * len(ins),
+        in_specs=specs,
         out_specs=[vmem] * len(outs),
         scratch_shapes=list(scratch),
         input_output_aliases=aliases or {},
@@ -141,7 +144,18 @@
         scratch_shapes=[pltpu.VMEM((2, part.shape[0], SUB, width), jnp.float32) for part in parts]
         + [pltpu.SemaphoreType.DMA((3, 2))],
         compiler_params=pltpu.CompilerParams(vmem_limit_bytes=PACK_LIMIT * 2**20),
-    )(*parts)
+    )(*(pltpu.with_memory_space_constraint(part, pltpu.HBM) for part in parts))
+
+
+def fetch(sources, targets, sems):
+    copies = [pltpu.make_async_copy(s, t, sems.at[n]) for n, (s, t) in enumerate(zip(sources, targets))]
+    for copy in copies:
+        copy.start()
+    return copies
+
+
+def room(*arrays):
+    return [pltpu.VMEM(x.shape, x.dtype) for x in arrays] + [pltpu.SemaphoreType.DMA((len(arrays),))]
 
 
 def quarters(parts):
@@ -160,7 +174,9 @@
     return 0, WHOLE, 0
 
 
-def pack_lanes(e_in, h_in, t_in, to_a, to_b):
+def pack_lanes(e_far, h_far, t_far, to_a, to_b, e_in, h_in, t_in, sems):
+    for copy in fetch((e_far, h_far, t_far), (e_in, h_in, t_in), sems):
+        copy.wait()
     even = is_even("gy")
     width = e_in.shape[2]
     fields = [ref.at[c] for ref in (e_in, h_in, t_in) for c in range(ref.shape[0])]
@@ -255,7 +271,8 @@
     full_e[0, bottom, lanes] = one
 
 
-def assemble_body(e_in, h_in, t_in, xa, xb, ya, yb, fe, fh, ft, masks):
+def assemble_body(e_far, h_far, t_far, xa, xb, ya, yb, fe, fh, ft, masks, e_in, h_in, t_in, sems):
+    copies = fetch((e_far, h_far, t_far), (e_in, h_in, t_in), sems)
     rows, width = e_in.shape[1:]
     total_rows, total = fe.shape[1:]
     low_x, high_x = sorter("gx")
@@ -265,26 +282,32 @@
     left, right = slice(0, SIDE), slice(SIDE + width, total)
     top, bottom = slice(0, SUB), slice(SUB + rows, total_rows)
     count = e_in.shape[0] + h_in.shape[0] + t_in.shape[0]
-    k = 0
+    fields = []
     for own, full, factor in ((e_in, fe, None), (h_in, fh, courant), (t_in, ft, courant * courant)):
-        for c in range(own.shape[0]):
-            full[c, top, :] = jnp.zeros((SUB, total), jnp.float32)
-            full[c, bottom, :] = jnp.zeros((SUB, total), jnp.float32)
-            for lanes, value in (
-                (middle, own[c]),
-                (left, low_y(from_lanes(ya, k, count, True), from_lanes(yb, k, count, True))),
-                (right, high_y(from_lanes(ya, k, count, False), from_lanes(yb, k, count, False))),
-            ):
-                full[c, inner, lanes] = value if factor is None else value * factor
-            k += 1
+        fields += [(own, full, factor, c) for c in range(own.shape[0])]
+
+    def scaled_to(factor, value):
+        return value if factor is None else value * factor
+
+    for k, (own, full, factor, c) in enumerate(fields):
+        full[c, top, :] = jnp.zeros((SUB, total), jnp.float32)
+        full[c, bottom, :] = jnp.zeros((SUB, total), jnp.float32)
+        for lanes, side, tail in ((left, low_y, True), (right, high_y, False)):
+            value = side(from_lanes(ya, k, count, tail), from_lanes(yb, k, count, tail))
+            full[c, inner, lanes] = scaled_to(factor, value)
     depth = lax.rem(lax.broadcasted_iota(jnp.int32, (SUB, total), 1) + (NZ - SIDE % NZ), NZ)
     masks[0] = (depth != NZ - 1).astype(jnp.float32)
     masks[1] = (depth != 0).astype(jnp.float32)
     place_rows(fe, fh, ft, rows, middle, lambda s: low_x(xa[s], xb[s]), lambda s: high_x(xa[s], xb[s]))
-
-
-def main_body(fe_in, fh_in, ft_in, masks, saved, ca, cb, inverse, fe, fh, ft, scaled, to_a, to_b):
+    for copy in copies:
+        copy.wait()
+    for own, full, factor, c in fields:
+        full[c, inner, middle] = scaled_to(factor, own[c])
+
+
+def main_body(fe_in, fh_in, ft_in, masks, s_far, ca, cb, inverse, fe, fh, ft, scaled, to_a, to_b, saved, sems):
     del fe_in, fh_in, ft_in
+    (frames,) = fetch((s_far,), (saved,), sems)
     rows, width = scaled.shape
     total_rows, total = fe.shape[1:]
     tiles = total_rows // SUB
@@ -377,6 +400,8 @@
                     to_tile(fe, c, r, tile(fe, c, r) + curl[c])
             before = turned
 
+        if step == 0:
+            frames.wait()
         pair = 2 * SUB
         for r in range(rows // pair):
             at = slice(r * pair, (r + 1) * pair)
@@ -453,10 +478,11 @@
     full = (rows + 2 * SUB, width + 2 * SIDE)
     fulls = [(n, *full) for n in (3, 3, 9)]
 
+    own = (electric, magnetic, tensor)
     xa, xb = swap(*pack_x(electric, magnetic, tensor), "gx", "gy")
     count = electric.shape[0] + magnetic.shape[0] + tensor.shape[0]
     packet = (count + -(-count // (2 * PER_TILE)), rows, WHOLE)
-    ya, yb = swap(*call(pack_lanes, [packet, packet], (electric, magnetic, tensor), limit=8), "gy", "gx", fill=False)
+    ya, yb = swap(*call(pack_lanes, [packet, packet], own, room(*own), limit=8, far=(0, 1, 2)), "gy", "gx", fill=False)
     height = xa.shape[0]
     packet = (2 * height + up_to(height // 4, SUB), WHOLE)
     ca, cb = swap(*call(pack_corners, [packet, packet], (xa, xb), limit=8), "gy", "gx")
@@ -466,12 +492,14 @@
     cover = coverage(row_places, lax.axis_size("gx") * rows) * coverage(col_places, lax.axis_size("gy") * cols)
 
     masks = (2, SUB, full[1])
-    fields = call(assemble_body, [*fulls, masks], (electric, magnetic, tensor, xa, xb, ya, yb), cost=2**22)
+    fields = call(assemble_body, [*fulls, masks], (*own, xa, xb, ya, yb), room(*own), cost=2**22, far=(0, 1, 2))
     fe, fh, _, scaled, to_a, to_b = call(
         main_body,
         [*fulls, (rows, width), edge, edge],
         (*fields, saved, ca, cb, 1.0 / cover),
+        room(saved),
         limit=20,
+        far=(4,),
         aliases={0: 0, 1: 1, 2: 2},
         cost=2**23,
     )

time: 40.8 us -> 37.9 us (0.929)
  local copies, waits for them, and re-layouts: 3.1 us -> 0 us
  starting transfers between devices: 17.5 us -> 16.8 us
  Pallas kernels: 10.6 us -> 11.2 us
    unnamed x14 -> x0, local copies, waits for them, and re-layouts: 3.1 us -> none
    ppermute x5, starting transfers between devices: 11.7 us -> 10.9 us  [swap(): from_b = lax.ppermute(to_b, AXES, neighbours(axis, other, 1, fill))]
  transfers between devices with their start and end apart: 10 -> 10, of which waited for: 4 -> 4; matrix products, arithmetic and copies ran while one was open for 0% -> 0% of each run, Pallas kernels for 10% -> 11%
where the time goes in v5:
time: 37.9 us; the launch traced here: 37.6 us
  starting transfers between devices  16.8 us (44%)
  Pallas kernels  11.2 us (30%)
  waiting for transfers between devices  8.77 us (23%)
  between operations  0.75 us (2%)
    ppermute x5, starting transfers between devices, swap(): from_b = lax.ppermute(to_b, AXES, neighbours(axis, other, 1, fill))  10.9 us
    pallas_call x7, Pallas kernels, call(): pl.pallas_call(body, out_shape=[jax.ShapeDtypeStruct(s, jnp.float32) for...  9.82 us
    ppermute x5, starting transfers between devices, swap(): from_a = lax.ppermute(to_a, AXES, neighbours(axis, other, 0, fill))  5.83 us
    ppermute x5, waiting for transfers between devices, swap(): from_a = lax.ppermute(to_a, AXES, neighbours(axis, other, 0, fill))  5.68 us
    ppermute x5, waiting for transfers between devices, swap(): from_b = lax.ppermute(to_b, AXES, neighbours(axis, other, 1, fill))  3.09 us
    pallas_call x1, Pallas kernels, pack_x(): pl.pallas_call(pack_rows, name='pack_x', out_shape=[out, out], in_specs=[...  1.37 us
  transfers between devices with their start and end apart: 10, of which 4 were waited for; matrix products, arithmetic and copies ran while one was open for 0% of the time, Pallas kernels for 11%

profile of v5, /device:TPU:0, one launch (start us, length us, event | category | flops | bytes accessed | tf_op | source)
XLA Modules:
  0.0 37.6 jit_solution(3422966176109381314)
XLA Ops:
  0.6 1.4 %pack_x.1 = (f32[80,768]{1,0:T(8,128)S(1)}, f32[80,768]{1,0:T(8,128)S(1)}) custom-call(f32[3,32,768]{2,1,0:T(8,128)} %e_far.3, f32[3,32,768]{2,1,0:T(8,128)} %h_far.3, f32[9,32,768]{2,1,0:T(8,128)} %t_far.3), custom_call_target="tpu_custom_call" | custom-call | tf_op jit(solution)/shard_map/pack_x/pallas_call | solution.py:138
  2.0 3.0 %collective-permute-start = (f32[80,768]{1,0:T(8,128)S(1)}, f32[80,768]{1,0:T(8,128)S(1)}, u32[]{:S(2)}, u32[]{:S(2)}) collective-permute-start(f32[80,768]{1,0:T(8,128)S(1)} %get-tuple-element.23), channel_id=1, source_target_pairs={{0,8},{8,0},{1,9},{9,1},{2,10},{10,2},{3,11},{11,3},{4,12},{12,4},... | collective-permute-start | bytes 737288 | tf_op jit(solution)/shard_map/ppermute | solution.py:48
  5.0 0.0 collective-permute-start.1
  5.0 1.6 %shard_map.67 = (f32[17,32,256]{2,1,0:T(8,128)S(1)}, f32[17,32,256]{2,1,0:T(8,128)S(1)}) custom-call(f32[3,32,768]{2,1,0:T(8,128)} %e_far.3, f32[3,32,768]{2,1,0:T(8,128)} %h_far.3, f32[9,32,768]{2,1,0:T(8,128)} %t_far.3), custom_call_target="tpu_custom_call" | custom-call | flops 1048576 | bytes 1048576 | tf_op jit(solution)/shard_map/pallas_call | solution.py:75
  6.6 0.6 %collective-permute-start.2 = (f32[17,32,256]{2,1,0:T(8,128)S(1)}, f32[17,32,256]{2,1,0:T(8,128)S(1)}, u32[]{:S(2)}, u32[]{:S(2)}) collective-permute-start(f32[17,32,256]{2,1,0:T(8,128)S(1)} %get-tuple-element.25), channel_id=1, source_target_pairs={{0,1},{1,0},{8,9},{9,8},{16,17},{17,16},{24,25},{25,24},{2,3},{3,2... | collective-permute-start | bytes 1671176 | tf_op jit(solution)/shard_map/ppermute | solution.py:48
  7.2 0.7 %collective-permute-start.3 = (f32[17,32,256]{2,1,0:T(8,128)S(1)}, f32[17,32,256]{2,1,0:T(8,128)S(1)}, u32[]{:S(2)}, u32[]{:S(2)}) collective-permute-start(f32[17,32,256]{2,1,0:T(8,128)S(1)} %get-tuple-element.26), channel_id=1, source_target_pairs={{1,2},{2,1},{9,10},{10,9},{17,18},{18,17},{25,26},{26,25},{3,4},{4... | collective-permute-start | bytes 1671176 | tf_op jit(solution)/shard_map/ppermute | solution.py:47
  8.0 3.9 %collective-permute-done.xa = f32[80,768]{1,0:T(8,128)S(1)} collective-permute-done((f32[80,768]{1,0:T(8,128)S(1)}, f32[80,768]{1,0:T(8,128)S(1)}, u32[]{:S(2)}, u32[]{:S(2)}) %collective-permute-start) | collective-permute-done | bytes 245792 | tf_op jit(solution)/shard_map/ppermute | solution.py:48
  11.8 0.0 collective-permute-done.1.xb
  11.8 0.1 shard_map.69
  12.0 0.1 collective-permute-start.4
  12.0 7.2 %collective-permute-start.5 = (f32[184,256]{1,0:T(8,128)S(1)}, f32[184,256]{1,0:T(8,128)S(1)}, u32[]{:S(2)}, u32[]{:S(2)}) collective-permute-start(f32[184,256]{1,0:T(8,128)S(1)} %get-tuple-element.32), channel_id=1, source_target_pairs={{1,2},{2,1},{9,10},{10,9},{17,18},{18,17},{25,26},{26,25},{3,4},{4... | collective-permute-start | bytes 565256 | tf_op jit(solution)/shard_map/ppermute | solution.py:47
  19.2 0.1 multiply_divide_fusion.inverse
  19.3 0.0 collective-permute-done.2.ya
  19.3 0.0 collective-permute-done.3.yb
  19.3 1.5 %shard_map.68 = (f32[3,48,1536]{2,1,0:T(8,128)S(1)}, f32[3,48,1536]{2,1,0:T(8,128)S(1)}, f32[9,48,1536]{2,1,0:T(8,128)S(1)}, f32[2,8,1536]{2,1,0:T(8,128)S(1)}) custom-call(f32[3,32,768]{2,1,0:T(8,128)} %e_far.3, f32[3,32,768]{2,1,0:T(8,128)} %h_far.3, f32[9,32,768]{2,1,0:T(8,128)} %t_far.3, f32[80,768]{1,0:T(8,128)S(1)} %collective-permute-done.xa, ...), custom_call_target="tpu_custom_call" | custom-call | flops 4194304 | bytes 4194304 | tf_op jit(solution)/shard_map/pallas_call | solution.py:75
  20.9 0.0 collective-permute-done.4.ca
  20.9 1.9 %collective-permute-done.5.cb = f32[184,256]{1,0:T(8,128)S(1)} collective-permute-done((f32[184,256]{1,0:T(8,128)S(1)}, f32[184,256]{1,0:T(8,128)S(1)}, u32[]{:S(2)}, u32[]{:S(2)}) %collective-permute-start.5) | collective-permute-done | bytes 188448 | tf_op jit(solution)/shard_map/ppermute | solution.py:47
  22.8 4.5 %shard_map.70 = (f32[3,48,1536]{2,1,0:T(8,128)S(1)}, f32[3,48,1536]{2,1,0:T(8,128)S(1)}, f32[9,48,1536]{2,1,0:T(8,128)S(1)}, f32[32,768]{1,0:T(8,128)S(1)}, f32[8,768]{1,0:T(8,128)S(1)}, /*index=5*/f32[8,768]{1,0:T(8,128)S(1)}) custom-call(f32[3,48,1536]{2,1,0:T(8,128)S(1)} %get-tuple-element.27.fe_in, ...), custom_call_target="tpu_custom_call", output_to_operand_aliasing={{0}: (0, {}), {1}: (1, {}), {2}: (2, {})} | custom-call | flops 8388608 | bytes 8388608 | tf_op jit(solution)/shard_map/pallas_call | solution.py:75
  27.2 2.1 %collective-permute-start.6 = (f32[8,768]{1,0:T(8,128)S(1)}, f32[8,768]{1,0:T(8,128)S(1)}, u32[]{:S(2)}, u32[]{:S(2)}) collective-permute-start(f32[8,768]{1,0:T(8,128)S(1)} %get-tuple-element.38), channel_id=1, source_target_pairs={{0,8},{8,0},{1,9},{9,1},{2,10},{10,2},{3,11},{11,3},{4,12},{12,4},... | collective-permute-start | bytes 73736 | tf_op jit(solution)/shard_map/ppermute | solution.py:48
  29.3 0.0 collective-permute-start.7
  29.3 1.8 %collective-permute-done.6.xa = f32[8,768]{1,0:T(8,128)S(1)} collective-permute-done((f32[8,768]{1,0:T(8,128)S(1)}, f32[8,768]{1,0:T(8,128)S(1)}, u32[]{:S(2)}, u32[]{:S(2)}) %collective-permute-start.6) | collective-permute-done | bytes 24608 | tf_op jit(solution)/shard_map/ppermute | solution.py:48
  31.1 0.0 collective-permute-done.7.xb
  31.1 0.1 shard_map.72
  31.2 0.1 collective-permute-start.8
  31.3 3.1 %collective-permute-start.9 = (f32[32,384]{1,0:T(8,128)S(1)}, f32[32,384]{1,0:T(8,128)S(1)}, u32[]{:S(2)}, u32[]{:S(2)}) collective-permute-start(f32[32,384]{1,0:T(8,128)S(1)} %get-tuple-element.42), channel_id=1, source_target_pairs={{1,2},{2,1},{9,10},{10,9},{17,18},{18,17},{25,26},{26,25},{3,4},{4... | collective-permute-start | bytes 147464 | tf_op jit(solution)/shard_map/ppermute | solution.py:47
  34.4 0.9 %shard_map.71 = (f32[3,32,768]{2,1,0:T(8,128)}, f32[3,32,768]{2,1,0:T(8,128)}) custom-call(f32[3,48,1536]{2,1,0:T(8,128)S(1)} %get-tuple-element.33.fe, f32[3,48,1536]{2,1,0:T(8,128)S(1)} %get-tuple-element.34.fh), custom_call_target="tpu_custom_call" | custom-call | flops 1048576 | bytes 1048576 | tf_op jit(solution)/shard_map/pallas_call | solution.py:75
  35.2 0.0 collective-permute-done.8.ya
  35.2 1.2 %collective-permute-done.9.yb = f32[32,384]{1,0:T(8,128)S(1)} collective-permute-done((f32[32,384]{1,0:T(8,128)S(1)}, f32[32,384]{1,0:T(8,128)S(1)}, u32[]{:S(2)}, u32[]{:S(2)}) %collective-permute-start.9) | collective-permute-done | bytes 49184 | tf_op jit(solution)/shard_map/ppermute | solution.py:47
  36.5 1.2 %shard_map.73 = f32[32,768]{1,0:T(8,128)} custom-call(f32[32,768]{1,0:T(8,128)S(1)} %get-tuple-element.40.across, f32[32,384]{1,0:T(8,128)S(1)} %collective-permute-done.8.ya, f32[32,384]{1,0:T(8,128)S(1)} %collective-permute-done.9.yb), custom_call_target="tpu_custom_call" | custom-call | flops 1048576 | bytes 1048576 | tf_op jit(solution)/shard_map/pallas_call | solution.py:75
  (3 shorter events, 0.0 us)
Async XLA Ops:
  2.0 9.8 %collective-permute-start = (f32[80,768]{1,0:T(8,128)S(1)}, f32[80,768]{1,0:T(8,128)S(1)}, u32[]{:S(2)}, u32[]{:S(2)}) collective-permute-start(f32[80,768]{1,0:T(8,128)S(1)} %get-tuple-element.23), channel_id=1, source_target_pairs={{0,8},{8,0},{1,9},{9,1},{2,10},{10,2},{3,11},{11,3},{4,12},{12,4},... | collective-permute-start | bytes 737288 | tf_op jit(solution)/shard_map/ppermute | solution.py:48
  5.0 6.8 %collective-permute-start.1 = (f32[80,768]{1,0:T(8,128)S(1)}, f32[80,768]{1,0:T(8,128)S(1)}, u32[]{:S(2)}, u32[]{:S(2)}) collective-permute-start(f32[80,768]{1,0:T(8,128)S(1)} %get-tuple-element.24), channel_id=1, source_target_pairs={{8,16},{16,8},{9,17},{17,9},{10,18},{18,10},{11,19},{19,11},{12,20... | collective-permute-start | bytes 737288 | tf_op jit(solution)/shard_map/ppermute | solution.py:47
  6.6 12.7 %collective-permute-start.2 = (f32[17,32,256]{2,1,0:T(8,128)S(1)}, f32[17,32,256]{2,1,0:T(8,128)S(1)}, u32[]{:S(2)}, u32[]{:S(2)}) collective-permute-start(f32[17,32,256]{2,1,0:T(8,128)S(1)} %get-tuple-element.25), channel_id=1, source_target_pairs={{0,1},{1,0},{8,9},{9,8},{16,17},{17,16},{24,25},{25,24},{2,3},{3,2... | collective-permute-start | bytes 1671176 | tf_op jit(solution)/shard_map/ppermute | solution.py:48
  7.2 12.1 %collective-permute-start.3 = (f32[17,32,256]{2,1,0:T(8,128)S(1)}, f32[17,32,256]{2,1,0:T(8,128)S(1)}, u32[]{:S(2)}, u32[]{:S(2)}) collective-permute-start(f32[17,32,256]{2,1,0:T(8,128)S(1)} %get-tuple-element.26), channel_id=1, source_target_pairs={{1,2},{2,1},{9,10},{10,9},{17,18},{18,17},{25,26},{26,25},{3,4},{4... | collective-permute-start | bytes 1671176 | tf_op jit(solution)/shard_map/ppermute | solution.py:47
  12.0 8.9 %collective-permute-start.4 = (f32[184,256]{1,0:T(8,128)S(1)}, f32[184,256]{1,0:T(8,128)S(1)}, u32[]{:S(2)}, u32[]{:S(2)}) collective-permute-start(f32[184,256]{1,0:T(8,128)S(1)} %get-tuple-element.31), channel_id=1, source_target_pairs={{0,1},{1,0},{8,9},{9,8},{16,17},{17,16},{24,25},{25,24},{2,3},{3,2... | collective-permute-start | bytes 565256 | tf_op jit(solution)/shard_map/ppermute | solution.py:48
  12.0 10.7 %collective-permute-start.5 = (f32[184,256]{1,0:T(8,128)S(1)}, f32[184,256]{1,0:T(8,128)S(1)}, u32[]{:S(2)}, u32[]{:S(2)}) collective-permute-start(f32[184,256]{1,0:T(8,128)S(1)} %get-tuple-element.32), channel_id=1, source_target_pairs={{1,2},{2,1},{9,10},{10,9},{17,18},{18,17},{25,26},{26,25},{3,4},{4... | collective-permute-start | bytes 565256 | tf_op jit(solution)/shard_map/ppermute | solution.py:47
  27.2 3.9 %collective-permute-start.6 = (f32[8,768]{1,0:T(8,128)S(1)}, f32[8,768]{1,0:T(8,128)S(1)}, u32[]{:S(2)}, u32[]{:S(2)}) collective-permute-start(f32[8,768]{1,0:T(8,128)S(1)} %get-tuple-element.38), channel_id=1, source_target_pairs={{0,8},{8,0},{1,9},{9,1},{2,10},{10,2},{3,11},{11,3},{4,12},{12,4},... | collective-permute-start | bytes 73736 | tf_op jit(solution)/shard_map/ppermute | solution.py:48
  29.3 1.8 %collective-permute-start.7 = (f32[8,768]{1,0:T(8,128)S(1)}, f32[8,768]{1,0:T(8,128)S(1)}, u32[]{:S(2)}, u32[]{:S(2)}) collective-permute-start(f32[8,768]{1,0:T(8,128)S(1)} %get-tuple-element.39), channel_id=1, source_target_pairs={{8,16},{16,8},{9,17},{17,9},{10,18},{18,10},{11,19},{19,11},{12,20... | collective-permute-start | bytes 73736 | tf_op jit(solution)/shard_map/ppermute | solution.py:47
  31.2 4.0 %collective-permute-start.8 = (f32[32,384]{1,0:T(8,128)S(1)}, f32[32,384]{1,0:T(8,128)S(1)}, u32[]{:S(2)}, u32[]{:S(2)}) collective-permute-start(f32[32,384]{1,0:T(8,128)S(1)} %get-tuple-element.41), channel_id=1, source_target_pairs={{0,1},{1,0},{8,9},{9,8},{16,17},{17,16},{24,25},{25,24},{2,3},{3,2... | collective-permute-start | bytes 147464 | tf_op jit(solution)/shard_map/ppermute | solution.py:48
  31.3 5.1 %collective-permute-start.9 = (f32[32,384]{1,0:T(8,128)S(1)}, f32[32,384]{1,0:T(8,128)S(1)}, u32[]{:S(2)}, u32[]{:S(2)}) collective-permute-start(f32[32,384]{1,0:T(8,128)S(1)} %get-tuple-element.42), channel_id=1, source_target_pairs={{1,2},{2,1},{9,10},{10,9},{17,18},{18,17},{25,26},{26,25},{3,4},{4... | collective-permute-start | bytes 147464 | tf_op jit(solution)/shard_map/ppermute | solution.py:47

commit v6 on v5

--- a/solution.py
+++ b/solution.py
@@ -1,3 +1,5 @@
+import math
+
 import jax
 import jax.numpy as jnp
 from jax import lax
@@ -249,7 +251,12 @@
     return result
 
 
-def place_rows(full_e, full_h, full_t, rows, lanes, low, high):
+def put(full, c, rows, begin, value):
+    for n in range(value.shape[1] // LANE):
+        full[c, begin // LANE + n, rows, :] = value[:, n * LANE : (n + 1) * LANE]
+
+
+def place_rows(full_e, full_h, full_t, rows, begin, low, high):
     fields = [(full_e, c, None) for c in range(3)] + [(full_h, c, courant) for c in range(3)]
     fields += [(full_t, c, courant * courant) for c in range(9)]
     top, bottom = slice(SUB - FULL, SUB), slice(SUB + rows, SUB + rows + FULL)
@@ -257,159 +264,190 @@
         packet = slice(k * FULL, (k + 1) * FULL)
         for at, get in ((top, low), (bottom, high)):
             value = get(packet)
-            full[c, at, lanes] = value if factor is None else value * factor
+            put(full, c, at, begin, value if factor is None else value * factor)
     base = len(fields) * FULL
     extra = [slice(base + i, base + i + 1) for i in range(EXTRA)]
     top, bottom = slice(SUB - HALO, SUB - FULL), slice(SUB + rows + FULL, SUB + rows + HALO)
-    full_t[0, top, lanes] = low(extra[0]) * (courant * courant)
-    full_h[1, top, lanes] = low(extra[1]) * courant
-    full_h[2, top, lanes] = low(extra[2]) * courant
-    full_t[1, bottom, lanes] = high(extra[0]) * (courant * courant)
-    full_t[2, bottom, lanes] = high(extra[1]) * (courant * courant)
+    put(full_t, 0, top, begin, low(extra[0]) * (courant * courant))
+    put(full_h, 1, top, begin, low(extra[1]) * courant)
+    put(full_h, 2, top, begin, low(extra[2]) * courant)
+    put(full_t, 1, bottom, begin, high(extra[0]) * (courant * courant))
+    put(full_t, 2, bottom, begin, high(extra[1]) * (courant * courant))
     one = jnp.ones_like(low(extra[0]))
-    full_e[0, top, lanes] = one
-    full_e[0, bottom, lanes] = one
-
-
-def assemble_body(e_far, h_far, t_far, xa, xb, ya, yb, fe, fh, ft, masks, e_in, h_in, t_in, sems):
+    put(full_e, 0, top, begin, one)
+    put(full_e, 0, bottom, begin, one)
+
+
+def assemble_body(e_far, h_far, t_far, xa, xb, ya, yb, fe, fh, ft, e_in, h_in, t_in, sems):
     copies = fetch((e_far, h_far, t_far), (e_in, h_in, t_in), sems)
     rows, width = e_in.shape[1:]
-    total_rows, total = fe.shape[1:]
+    total_rows = fe.shape[2]
     low_x, high_x = sorter("gx")
     low_y, high_y = sorter("gy")
-    inner = slice(SUB, SUB + rows)
-    middle = slice(SIDE, SIDE + width)
-    left, right = slice(0, SIDE), slice(SIDE + width, total)
-    top, bottom = slice(0, SUB), slice(SUB + rows, total_rows)
-    count = e_in.shape[0] + h_in.shape[0] + t_in.shape[0]
+    inner, top, bottom = slice(SUB, SUB + rows), slice(0, SUB), slice(SUB + rows, total_rows)
     fields = []
     for own, full, factor in ((e_in, fe, None), (h_in, fh, courant), (t_in, ft, courant * courant)):
         fields += [(own, full, factor, c) for c in range(own.shape[0])]
+    count = len(fields)
 
     def scaled_to(factor, value):
         return value if factor is None else value * factor
 
     for k, (own, full, factor, c) in enumerate(fields):
-        full[c, top, :] = jnp.zeros((SUB, total), jnp.float32)
-        full[c, bottom, :] = jnp.zeros((SUB, total), jnp.float32)
-        for lanes, side, tail in ((left, low_y, True), (right, high_y, False)):
+        for n in range(full.shape[1]):
+            full[c, n, top, :] = jnp.zeros((SUB, LANE), jnp.float32)
+            full[c, n, bottom, :] = jnp.zeros((SUB, LANE), jnp.float32)
+        for begin, side, tail in ((0, low_y, True), (SIDE + width, high_y, False)):
             value = side(from_lanes(ya, k, count, tail), from_lanes(yb, k, count, tail))
-            full[c, inner, lanes] = scaled_to(factor, value)
-    depth = lax.rem(lax.broadcasted_iota(jnp.int32, (SUB, total), 1) + (NZ - SIDE % NZ), NZ)
-    masks[0] = (depth != NZ - 1).astype(jnp.float32)
-    masks[1] = (depth != 0).astype(jnp.float32)
-    place_rows(fe, fh, ft, rows, middle, lambda s: low_x(xa[s], xb[s]), lambda s: high_x(xa[s], xb[s]))
+            put(full, c, inner, begin, scaled_to(factor, value))
+    place_rows(fe, fh, ft, rows, SIDE, lambda s: low_x(xa[s], xb[s]), lambda s: high_x(xa[s], xb[s]))
     for copy in copies:
         copy.wait()
     for own, full, factor, c in fields:
-        full[c, inner, middle] = scaled_to(factor, own[c])
-
-
-def main_body(fe_in, fh_in, ft_in, masks, s_far, ca, cb, inverse, fe, fh, ft, scaled, to_a, to_b, saved, sems):
+        put(full, c, inner, SIDE, scaled_to(factor, own[c]))
+
+
+def main_body(fe_in, fh_in, ft_in, s_far, ca, cb, inverse, fe, fh, ft, scaled, to_a, to_b, saved, sems, fg):
     del fe_in, fh_in, ft_in
     (frames,) = fetch((s_far,), (saved,), sems)
     rows, width = scaled.shape
-    total_rows, total = fe.shape[1:]
+    total_rows = fe.shape[2]
     tiles = total_rows // SUB
-    middle = slice(SIDE, SIDE + width)
     low_x, high_x = sorter("gx")
     low_y, high_y = sorter("gy")
     even_x = is_even("gx")
 
     height = up_to(FULL * 15 + EXTRA, 2 * SUB)
-    for lanes, side, tail in ((slice(0, SIDE), low_y, True), (slice(SIDE + width, total), high_y, False)):
-        packets = [
-            side(a, b) for a, b in zip(from_corners(ca, height, tail), from_corners(cb, height, tail))
-        ]
+    for begin, side, tail in ((0, low_y, True), (SIDE + width, high_y, False)):
+        packets = [side(a, b) for a, b in zip(from_corners(ca, height, tail), from_corners(cb, height, tail))]
         low, high = low_x(*packets), high_x(*packets)
-        place_rows(fe, fh, ft, rows, lanes, lambda s, low=low: low[s], lambda s, high=high: high[s])
+        place_rows(fe, fh, ft, rows, begin, lambda s, low=low: low[s], lambda s, high=high: high[s])
 
     inside_x = jnp.where(lax.axis_index("gx") > 0, 1.0, 0.0).astype(jnp.float32)
     inside_y = jnp.where(lax.axis_index("gy") > 0, 1.0, 0.0).astype(jnp.float32)
+    lane = lax.broadcasted_iota(jnp.int32, (SUB, LANE), 1)
+    depths = [lax.rem(lane + n * LANE, NZ) for n in range(NZ // math.gcd(NZ, LANE))]
+    uppers = [(d != NZ - 1).astype(jnp.float32) for d in depths]
+    lowers = [(d != 0).astype(jnp.float32) for d in depths]
+
+    sub = lax.broadcasted_iota(jnp.int32, (SUB, LANE), 0)
+    joint = tiles - 1
+    joint_mask = jnp.where(sub >= SUB // 2, inside_x, 1.0)
+
+    def at(r, shift=0):
+        return slice(r * SUB + shift, (r + 1) * SUB + shift)
+
+    def tiles_of(before, after):
+        return range((SIDE - before * NZ) // LANE, up_to(SIDE + width + after * NZ, LANE) // LANE)
+
+    def ahead(values, places, n):
+        turned = pltpu.roll(values[n], LANE - places, 1)
+        if n + 1 not in values or (places == 1 and (n + 1) * LANE % NZ == 0):
+            return turned
+        return jnp.where(lane < LANE - places, turned, pltpu.roll(values[n + 1], LANE - places, 1))
+
+    def behind(values, places, n):
+        turned = pltpu.roll(values[n], places, 1)
+        if n - 1 not in values or (places == 1 and n * LANE % NZ == 0):
+            return turned
+        return jnp.where(lane >= places, turned, pltpu.roll(values[n - 1], places, 1))
 
     for step in range(STEPS):
-        left_over = STEPS - step
-        begin = (SIDE - left_over * NZ) // LANE * LANE
-        end = up_to(SIDE + width + left_over * NZ, LANE)
-        span = end - begin
-        lanes = slice(begin, end)
-        sub = lax.broadcasted_iota(jnp.int32, (SUB, span), 0)
-        upper, lower = masks[0, :, lanes], masks[1, :, lanes]
-        low = SIDE - begin
-        last = step == STEPS - 1
-
-        def tile(ref, c, r):
-            return ref[c, r * SUB : (r + 1) * SUB, lanes]
-
-        def to_tile(ref, c, r, value):
-            ref[c, r * SUB : (r + 1) * SUB, lanes] = value
-
-        def from_next_y(f):
-            return pltpu.roll(f, span - NZ, 1)
-
-        def from_next_z(f):
-            return pltpu.roll(f, span - 1, 1) * upper
-
-        def from_prev_y(f):
-            return pltpu.roll(f, NZ, 1)
-
-        def from_prev_z(f):
-            return pltpu.roll(f, 1, 1) * lower
-
-        after = None
-        for r in reversed(range(tiles)):
-            e = [tile(fe, c, r) for c in range(3)]
-            g = [
-                (tile(ft, c, r) * e[0] + tile(ft, 3 + c, r) * e[1]) + tile(ft, 6 + c, r) * e[2]
-                for c in range(3)
+        left = STEPS - 1 - step
+        lanes_g, lanes_h, lanes_e = tiles_of(left + 1, left + 1), tiles_of(left + 1, left), tiles_of(left, left)
+        last = left == 0
+        g = [[{}, {}, {}] for _ in range(tiles)]
+        h = [[{}, {}, {}] for _ in range(tiles)]
+        joined = left + 1 <= SUB // 2
+        if joined and left + 2 > SUB // 2:
+            for full in (fe, fh, ft):
+                for c in range(full.shape[0]):
+                    for n in lanes_g:
+                        full[c, n, at(joint), :] = jnp.where(
+                            sub < SUB // 2, full[c, n, at(joint), :], full[c, n, at(0), :]
+                        )
+
+        def turn(r, n):
+            e = [fe[c, n, at(r), :] for c in range(3)]
+            for c in range(3):
+                t = [ft[3 * i + c, n, at(r), :] for i in range(3)]
+                g[r][c][n] = (t[0] * e[0] + t[1] * e[1]) + t[2] * e[2]
+                if c > 0:
+                    fg[c - 1, n, at(r), :] = g[r][c][n]
+                    if joined and r == 1:
+                        fg[c - 1, n, at(tiles), :] = g[r][c][n]
+
+        def update_h(r, n):
+            upper = uppers[n % len(uppers)]
+            own = g[r]
+            if r == tiles - 1 and not joined:
+                next_x = [None] + [pltpu.roll(own[c][n], SUB - 1, 0) for c in (1, 2)]
+            else:
+                next_x = [None] + [fg[c - 1, n, at(r, 1), :] for c in (1, 2)]
+            curl = [
+                (ahead(own[2], NZ, n) - own[2][n]) - (ahead(own[1], 1, n) * upper - own[1][n]),
+                (ahead(own[0], 1, n) * upper - own[0][n]) - (next_x[2] - own[2][n]),
+                (next_x[1] - own[1][n]) - (ahead(own[0], NZ, n) - own[0][n]),
             ]
-            turned = [None] + [pltpu.roll(g[c], SUB - 1, 0) for c in (1, 2)]
-            if after is None:
-                after = turned
-            if not (last and r == tiles - 1):
-                next_x = [None] + [jnp.where(sub == SUB - 1, after[c], turned[c]) for c in (1, 2)]
-                curl = [
-                    (from_next_y(g[2]) - g[2]) - (from_next_z(g[1]) - g[1]),
-                    (from_next_z(g[0]) - g[0]) - (next_x[2] - g[2]),
-                    (next_x[1] - g[1]) - (from_next_y(g[0]) - g[0]),
-                ]
-                for c in range(3):
-                    h = tile(fh, c, r) - curl[c]
-                    if r == 0:
-                        h = h * inside_x
-                    h = jnp.concatenate([h[:, :low] * inside_y, h[:, low:]], axis=1)
-                    to_tile(fh, c, r, h)
-            after = turned
-
-        before = None
-        for r in range(tiles):
-            if last and r == tiles - 1:
-                continue
-            h = [tile(fh, c, r) for c in range(3)]
-            turned = [None] + [pltpu.roll(h[c], 1, 0) for c in (1, 2)]
-            if before is None:
-                before = turned
-            if not (last and r == 0):
-                prev_x = [None] + [jnp.where(sub == 0, before[c], turned[c]) for c in (1, 2)]
-                curl = [
-                    (h[2] - from_prev_y(h[2])) - (h[1] - from_prev_z(h[1])),
-                    (h[0] - from_prev_z(h[0])) - (h[2] - prev_x[2]),
-                    (h[1] - prev_x[1]) - (h[0] - from_prev_y(h[0])),
-                ]
-                for c in range(3):
-                    to_tile(fe, c, r, tile(fe, c, r) + curl[c])
-            before = turned
+            for c in range(3):
+                value = fh[c, n, at(r), :] - curl[c]
+                if r == 0:
+                    value = value * inside_x
+                if r == joint and joined:
+                    value = value * joint_mask
+                if n < SIDE // LANE:
+                    value = value * inside_y
+                fh[c, n, at(r), :] = value
+                if r == joint and joined and c > 0:
+                    fh[c, n, at(0), :] = value
+                h[r][c][n] = value
+
+        def update_e(r, n):
+            lower = lowers[n % len(lowers)]
+            own = h[r]
+            if r == 0:
+                prev_x = [None] + [pltpu.roll(own[c][n], 1, 0) for c in (1, 2)]
+            else:
+                prev_x = [None] + [fh[c, n, at(r, -1), :] for c in (1, 2)]
+            curl = [
+                (own[2][n] - behind(own[2], NZ, n)) - (own[1][n] - behind(own[1], 1, n) * lower),
+                (own[0][n] - behind(own[0], 1, n) * lower) - (own[2][n] - prev_x[2]),
+                (own[1][n] - prev_x[1]) - (own[0][n] - behind(own[0], NZ, n)),
+            ]
+            for c in range(3):
+                fe[c, n, at(r), :] = fe[c, n, at(r), :] + curl[c]
+
+        if joined:
+            inner = list(range(tiles - 2, 0, -1))
+            stages = [(joint, None, None)] + [
+                (r, r, r + 1 if n > 0 else None) for n, r in enumerate(inner)
+            ]
+            stages += [(None, joint, None), (None, None, 1)] + ([] if last else [(None, None, joint)])
+        else:
+            stages = [(r - 1 if r > 0 else None, r if r < tiles else None, r + 1 if r + 1 < tiles else None) for r in range(tiles, -2, -1)]
+            stages = [(a, b if b is not None and b >= 0 else None, c) for a, b, c in stages]
+        for to_turn, to_h, to_e in stages:
+            for n in lanes_g:
+                if to_turn is not None:
+                    turn(to_turn, n)
+            for n in lanes_g:
+                if to_h is not None and n in lanes_h:
+                    update_h(to_h, n)
+                if to_e is not None and n in lanes_e:
+                    update_e(to_e, n)
 
         if step == 0:
             frames.wait()
         pair = 2 * SUB
         for r in range(rows // pair):
-            at = slice(r * pair, (r + 1) * pair)
-            at_full = slice(SUB + r * pair, SUB + (r + 1) * pair)
-            s = [saved[step, c, at].astype(jnp.float32) for c in range(3)]
-            e = [fe[c, at_full, middle] for c in range(3)]
-            term = (e[0] * s[0] + e[1] * s[1]) + e[2] * s[2]
-            scaled[at] = term if step == 0 else scaled[at] + term
+            for n in range(width // LANE):
+                here = slice(r * pair, (r + 1) * pair)
+                full = slice(SUB + r * pair, SUB + (r + 1) * pair)
+                lanes = slice(n * LANE, (n + 1) * LANE)
+                s = [saved[step, c, here, lanes].astype(jnp.float32) for c in range(3)]
+                e = [fe[c, n + SIDE // LANE, full, :] for c in range(3)]
+                term = (e[0] * s[0] + e[1] * s[1]) + e[2] * s[2]
+                scaled[here, lanes] = term if step == 0 else scaled[here, lanes] + term
 
     scaled[...] = scaled[...] * inverse[...]
     head, tail = scaled[:RADIUS], scaled[rows - RADIUS :]
@@ -420,8 +458,10 @@
 def emit_body(fe, fh, e_out, h_out):
     rows, width = e_out.shape[1:]
     for c in range(3):
-        e_out[c] = fe[c, SUB : SUB + rows, SIDE : SIDE + width]
-        h_out[c] = fh[c, SUB : SUB + rows, SIDE : SIDE + width] * (1.0 / courant)
+        for n in range(width // LANE):
+            lanes = slice(n * LANE, (n + 1) * LANE)
+            e_out[c, :, lanes] = fe[c, n + SIDE // LANE, SUB : SUB + rows, :]
+            h_out[c, :, lanes] = fh[c, n + SIDE // LANE, SUB : SUB + rows, :] * (1.0 / courant)
 
 
 def box(values, unit, axis):
@@ -475,7 +515,7 @@
     rows, width = electric.shape[1:]
     cols = width // NZ
     edge = (RADIUS, width)
-    full = (rows + 2 * SUB, width + 2 * SIDE)
+    full = ((width + 2 * SIDE) // LANE, rows + 2 * SUB, LANE)
     fulls = [(n, *full) for n in (3, 3, 9)]
 
     own = (electric, magnetic, tensor)
@@ -491,15 +531,14 @@
     col_places = lax.axis_index("gy") * cols + lax.broadcasted_iota(jnp.int32, (rows, width), 1) // NZ
     cover = coverage(row_places, lax.axis_size("gx") * rows) * coverage(col_places, lax.axis_size("gy") * cols)
 
-    masks = (2, SUB, full[1])
-    fields = call(assemble_body, [*fulls, masks], (*own, xa, xb, ya, yb), room(*own), cost=2**22, far=(0, 1, 2))
+    fields = call(assemble_body, fulls, (*own, xa, xb, ya, yb), room(*own), cost=2**22, far=(0, 1, 2))
     fe, fh, _, scaled, to_a, to_b = call(
         main_body,
         [*fulls, (rows, width), edge, edge],
         (*fields, saved, ca, cb, 1.0 / cover),
-        room(saved),
+        [*room(saved), pltpu.VMEM((2, full[0], full[1] + SUB, LANE), jnp.float32)],
         limit=20,
-        far=(4,),
+        far=(3,),
         aliases={0: 0, 1: 1, 2: 2},
         cost=2**23,
     )

time: 37.9 us -> 37.3 us (0.984)
  Pallas kernels: 11.2 us -> 10.8 us
    pallas_call x7, Pallas kernels: 9.82 us -> 9.4 us  [call(): pl.pallas_call(body, out_shape=[jax.ShapeDtypeStruct(s, jnp.float32) for...]
  transfers between devices with their start and end apart: 10 -> 10, of which waited for: 4 -> 4; matrix products, arithmetic and copies ran while one was open for 0% -> 0% of each run, Pallas kernels for 11% -> 12%
where the time goes in v6:
time: 37.3 us; the launch traced here: 37 us
  starting transfers between devices  16.8 us (45%)
  Pallas kernels  10.8 us (29%)
  waiting for transfers between devices  8.61 us (23%)
  between operations  0.75 us (2%)
    ppermute x5, starting transfers between devices, swap(): from_b = lax.ppermute(to_b, AXES, neighbours(axis, other, 1, fill))  10.9 us
    pallas_call x7, Pallas kernels, call(): pl.pallas_call(body, out_shape=[jax.ShapeDtypeStruct(s, jnp.float32) for...  9.4 us
    ppermute x5, starting transfers between devices, swap(): from_a = lax.ppermute(to_a, AXES, neighbours(axis, other, 0, fill))  5.83 us
    ppermute x5, waiting for transfers between devices, swap(): from_a = lax.ppermute(to_a, AXES, neighbours(axis, other, 0, fill))  5.68 us
    ppermute x5, waiting for transfers between devices, swap(): from_b = lax.ppermute(to_b, AXES, neighbours(axis, other, 1, fill))  2.93 us
    pallas_call x1, Pallas kernels, pack_x(): pl.pallas_call(pack_rows, name='pack_x', out_shape=[out, out], in_specs=[...  1.37 us
  transfers between devices with their start and end apart: 10, of which 4 were waited for; matrix products, arithmetic and copies ran while one was open for 0% of the time, Pallas kernels for 12%

profile of v6, /device:TPU:0, one launch (start us, length us, event | category | flops | bytes accessed | tf_op | source)
XLA Modules:
  0.0 37.0 jit_solution(873147380757304680)
XLA Ops:
  0.6 1.4 %pack_x.1 = (f32[80,768]{1,0:T(8,128)S(1)}, f32[80,768]{1,0:T(8,128)S(1)}) custom-call(f32[3,32,768]{2,1,0:T(8,128)} %e_far.3, f32[3,32,768]{2,1,0:T(8,128)} %h_far.3, f32[9,32,768]{2,1,0:T(8,128)} %t_far.3), custom_call_target="tpu_custom_call" | custom-call | tf_op jit(solution)/shard_map/pack_x/pallas_call | solution.py:140
  2.0 3.0 %collective-permute-start = (f32[80,768]{1,0:T(8,128)S(1)}, f32[80,768]{1,0:T(8,128)S(1)}, u32[]{:S(2)}, u32[]{:S(2)}) collective-permute-start(f32[80,768]{1,0:T(8,128)S(1)} %get-tuple-element.22), channel_id=1, source_target_pairs={{0,8},{8,0},{1,9},{9,1},{2,10},{10,2},{3,11},{11,3},{4,12},{12,4},... | collective-permute-start | bytes 737288 | tf_op jit(solution)/shard_map/ppermute | solution.py:50
  5.0 0.0 collective-permute-start.1
  5.0 1.6 %shard_map.67 = (f32[17,32,256]{2,1,0:T(8,128)S(1)}, f32[17,32,256]{2,1,0:T(8,128)S(1)}) custom-call(f32[3,32,768]{2,1,0:T(8,128)} %e_far.3, f32[3,32,768]{2,1,0:T(8,128)} %h_far.3, f32[9,32,768]{2,1,0:T(8,128)} %t_far.3), custom_call_target="tpu_custom_call" | custom-call | flops 1048576 | bytes 1048576 | tf_op jit(solution)/shard_map/pallas_call | solution.py:77
  6.6 0.6 %collective-permute-start.2 = (f32[17,32,256]{2,1,0:T(8,128)S(1)}, f32[17,32,256]{2,1,0:T(8,128)S(1)}, u32[]{:S(2)}, u32[]{:S(2)}) collective-permute-start(f32[17,32,256]{2,1,0:T(8,128)S(1)} %get-tuple-element.24), channel_id=1, source_target_pairs={{0,1},{1,0},{8,9},{9,8},{16,17},{17,16},{24,25},{25,24},{2,3},{3,2... | collective-permute-start | bytes 1671176 | tf_op jit(solution)/shard_map/ppermute | solution.py:50
  7.2 0.7 %collective-permute-start.3 = (f32[17,32,256]{2,1,0:T(8,128)S(1)}, f32[17,32,256]{2,1,0:T(8,128)S(1)}, u32[]{:S(2)}, u32[]{:S(2)}) collective-permute-start(f32[17,32,256]{2,1,0:T(8,128)S(1)} %get-tuple-element.25), channel_id=1, source_target_pairs={{1,2},{2,1},{9,10},{10,9},{17,18},{18,17},{25,26},{26,25},{3,4},{4... | collective-permute-start | bytes 1671176 | tf_op jit(solution)/shard_map/ppermute | solution.py:49
  8.0 3.9 %collective-permute-done.xa = f32[80,768]{1,0:T(8,128)S(1)} collective-permute-done((f32[80,768]{1,0:T(8,128)S(1)}, f32[80,768]{1,0:T(8,128)S(1)}, u32[]{:S(2)}, u32[]{:S(2)}) %collective-permute-start) | collective-permute-done | bytes 245792 | tf_op jit(solution)/shard_map/ppermute | solution.py:50
  11.8 0.0 collective-permute-done.1.xb
  11.8 0.1 shard_map.69
  12.0 0.1 collective-permute-start.4
  12.0 7.2 %collective-permute-start.5 = (f32[184,256]{1,0:T(8,128)S(1)}, f32[184,256]{1,0:T(8,128)S(1)}, u32[]{:S(2)}, u32[]{:S(2)}) collective-permute-start(f32[184,256]{1,0:T(8,128)S(1)} %get-tuple-element.30), channel_id=1, source_target_pairs={{1,2},{2,1},{9,10},{10,9},{17,18},{18,17},{25,26},{26,25},{3,4},{4... | collective-permute-start | bytes 565256 | tf_op jit(solution)/shard_map/ppermute | solution.py:49
  19.2 0.1 multiply_divide_fusion.inverse
  19.3 0.0 collective-permute-done.2.ya
  19.3 0.0 collective-permute-done.3.yb
  19.3 1.7 %shard_map.68 = (f32[3,12,48,128]{3,2,1,0:T(8,128)S(1)}, f32[3,12,48,128]{3,2,1,0:T(8,128)S(1)}, f32[9,12,48,128]{3,2,1,0:T(8,128)S(1)}) custom-call(f32[3,32,768]{2,1,0:T(8,128)} %e_far.3, f32[3,32,768]{2,1,0:T(8,128)} %h_far.3, f32[9,32,768]{2,1,0:T(8,128)} %t_far.3, f32[80,768]{1,0:T(8,128)S(1)} %collective-permute-done.xa, ...), custom_call_target="tpu_custom_call" | custom-call | flops 4194304 | bytes 4194304 | tf_op jit(solution)/shard_map/pallas_call | solution.py:77
  21.0 0.0 collective-permute-done.4.ca
  21.1 1.7 %collective-permute-done.5.cb = f32[184,256]{1,0:T(8,128)S(1)} collective-permute-done((f32[184,256]{1,0:T(8,128)S(1)}, f32[184,256]{1,0:T(8,128)S(1)}, u32[]{:S(2)}, u32[]{:S(2)}) %collective-permute-start.5) | collective-permute-done | bytes 188448 | tf_op jit(solution)/shard_map/ppermute | solution.py:49
  22.8 3.9 %shard_map.70 = (f32[3,12,48,128]{3,2,1,0:T(8,128)S(1)}, f32[3,12,48,128]{3,2,1,0:T(8,128)S(1)}, f32[9,12,48,128]{3,2,1,0:T(8,128)S(1)}, f32[32,768]{1,0:T(8,128...) custom-call(f32[3,12,48,128]{3,2,1,0:T(8,128)S(1)} %get-tuple-elemen, ...), custom_call_target="tpu_custom_call", output_to_operand_aliasing={{0}: (0, {}), {1}: (1, {}), {2}: (2, {})} | custom-call | flops 8388608 | bytes 8388608 | tf_op jit(solution)/shard_map/pallas_call | solution.py:77
  26.6 2.1 %collective-permute-start.6 = (f32[8,768]{1,0:T(8,128)S(1)}, f32[8,768]{1,0:T(8,128)S(1)}, u32[]{:S(2)}, u32[]{:S(2)}) collective-permute-start(f32[8,768]{1,0:T(8,128)S(1)} %get-tuple-element.36), channel_id=1, source_target_pairs={{0,8},{8,0},{1,9},{9,1},{2,10},{10,2},{3,11},{11,3},{4,12},{12,4},... | collective-permute-start | bytes 73736 | tf_op jit(solution)/shard_map/ppermute | solution.py:50
  28.7 0.0 collective-permute-start.7
  28.7 1.8 %collective-permute-done.6.xa = f32[8,768]{1,0:T(8,128)S(1)} collective-permute-done((f32[8,768]{1,0:T(8,128)S(1)}, f32[8,768]{1,0:T(8,128)S(1)}, u32[]{:S(2)}, u32[]{:S(2)}) %collective-permute-start.6) | collective-permute-done | bytes 24608 | tf_op jit(solution)/shard_map/ppermute | solution.py:50
  30.5 0.0 collective-permute-done.7.xb
  30.5 0.1 shard_map.72
  30.7 0.1 collective-permute-start.8
  30.7 3.1 %collective-permute-start.9 = (f32[32,384]{1,0:T(8,128)S(1)}, f32[32,384]{1,0:T(8,128)S(1)}, u32[]{:S(2)}, u32[]{:S(2)}) collective-permute-start(f32[32,384]{1,0:T(8,128)S(1)} %get-tuple-element.40), channel_id=1, source_target_pairs={{1,2},{2,1},{9,10},{10,9},{17,18},{18,17},{25,26},{26,25},{3,4},{4... | collective-permute-start | bytes 147464 | tf_op jit(solution)/shard_map/ppermute | solution.py:49
  33.8 0.9 %shard_map.71 = (f32[3,32,768]{2,1,0:T(8,128)}, f32[3,32,768]{2,1,0:T(8,128)}) custom-call(f32[3,12,48,128]{3,2,1,0:T(8,128)S(1)} %get-tuple-element.31.fe, f32[3,12,48,128]{3,2,1,0:T(8,128)S(1)} %get-tuple-element.32.fh), custom_call_target="tpu_custom_call" | custom-call | flops 1048576 | bytes 1048576 | tf_op jit(solution)/shard_map/pallas_call | solution.py:77
  34.7 0.0 collective-permute-done.8.ya
  34.7 1.2 %collective-permute-done.9.yb = f32[32,384]{1,0:T(8,128)S(1)} collective-permute-done((f32[32,384]{1,0:T(8,128)S(1)}, f32[32,384]{1,0:T(8,128)S(1)}, u32[]{:S(2)}, u32[]{:S(2)}) %collective-permute-start.9) | collective-permute-done | bytes 49184 | tf_op jit(solution)/shard_map/ppermute | solution.py:49
  35.9 1.2 %shard_map.73 = f32[32,768]{1,0:T(8,128)} custom-call(f32[32,768]{1,0:T(8,128)S(1)} %get-tuple-element.38.across, f32[32,384]{1,0:T(8,128)S(1)} %collective-permute-done.8.ya, f32[32,384]{1,0:T(8,128)S(1)} %collective-permute-done.9.yb), custom_call_target="tpu_custom_call" | custom-call | flops 1048576 | bytes 1048576 | tf_op jit(solution)/shard_map/pallas_call | solution.py:77
  (3 shorter events, 0.0 us)
Async XLA Ops:
  2.0 9.8 %collective-permute-start = (f32[80,768]{1,0:T(8,128)S(1)}, f32[80,768]{1,0:T(8,128)S(1)}, u32[]{:S(2)}, u32[]{:S(2)}) collective-permute-start(f32[80,768]{1,0:T(8,128)S(1)} %get-tuple-element.22), channel_id=1, source_target_pairs={{0,8},{8,0},{1,9},{9,1},{2,10},{10,2},{3,11},{11,3},{4,12},{12,4},... | collective-permute-start | bytes 737288 | tf_op jit(solution)/shard_map/ppermute | solution.py:50
  5.0 6.8 %collective-permute-start.1 = (f32[80,768]{1,0:T(8,128)S(1)}, f32[80,768]{1,0:T(8,128)S(1)}, u32[]{:S(2)}, u32[]{:S(2)}) collective-permute-start(f32[80,768]{1,0:T(8,128)S(1)} %get-tuple-element.23), channel_id=1, source_target_pairs={{8,16},{16,8},{9,17},{17,9},{10,18},{18,10},{11,19},{19,11},{12,20... | collective-permute-start | bytes 737288 | tf_op jit(solution)/shard_map/ppermute | solution.py:49
  6.6 12.7 %collective-permute-start.2 = (f32[17,32,256]{2,1,0:T(8,128)S(1)}, f32[17,32,256]{2,1,0:T(8,128)S(1)}, u32[]{:S(2)}, u32[]{:S(2)}) collective-permute-start(f32[17,32,256]{2,1,0:T(8,128)S(1)} %get-tuple-element.24), channel_id=1, source_target_pairs={{0,1},{1,0},{8,9},{9,8},{16,17},{17,16},{24,25},{25,24},{2,3},{3,2... | collective-permute-start | bytes 1671176 | tf_op jit(solution)/shard_map/ppermute | solution.py:50
  7.2 12.1 %collective-permute-start.3 = (f32[17,32,256]{2,1,0:T(8,128)S(1)}, f32[17,32,256]{2,1,0:T(8,128)S(1)}, u32[]{:S(2)}, u32[]{:S(2)}) collective-permute-start(f32[17,32,256]{2,1,0:T(8,128)S(1)} %get-tuple-element.25), channel_id=1, source_target_pairs={{1,2},{2,1},{9,10},{10,9},{17,18},{18,17},{25,26},{26,25},{3,4},{4... | collective-permute-start | bytes 1671176 | tf_op jit(solution)/shard_map/ppermute | solution.py:49
  12.0 9.1 %collective-permute-start.4 = (f32[184,256]{1,0:T(8,128)S(1)}, f32[184,256]{1,0:T(8,128)S(1)}, u32[]{:S(2)}, u32[]{:S(2)}) collective-permute-start(f32[184,256]{1,0:T(8,128)S(1)} %get-tuple-element.29), channel_id=1, source_target_pairs={{0,1},{1,0},{8,9},{9,8},{16,17},{17,16},{24,25},{25,24},{2,3},{3,2... | collective-permute-start | bytes 565256 | tf_op jit(solution)/shard_map/ppermute | solution.py:50
  12.0 10.7 %collective-permute-start.5 = (f32[184,256]{1,0:T(8,128)S(1)}, f32[184,256]{1,0:T(8,128)S(1)}, u32[]{:S(2)}, u32[]{:S(2)}) collective-permute-start(f32[184,256]{1,0:T(8,128)S(1)} %get-tuple-element.30), channel_id=1, source_target_pairs={{1,2},{2,1},{9,10},{10,9},{17,18},{18,17},{25,26},{26,25},{3,4},{4... | collective-permute-start | bytes 565256 | tf_op jit(solution)/shard_map/ppermute | solution.py:49
  26.6 3.9 %collective-permute-start.6 = (f32[8,768]{1,0:T(8,128)S(1)}, f32[8,768]{1,0:T(8,128)S(1)}, u32[]{:S(2)}, u32[]{:S(2)}) collective-permute-start(f32[8,768]{1,0:T(8,128)S(1)} %get-tuple-element.36), channel_id=1, source_target_pairs={{0,8},{8,0},{1,9},{9,1},{2,10},{10,2},{3,11},{11,3},{4,12},{12,4},... | collective-permute-start | bytes 73736 | tf_op jit(solution)/shard_map/ppermute | solution.py:50
  28.7 1.8 %collective-permute-start.7 = (f32[8,768]{1,0:T(8,128)S(1)}, f32[8,768]{1,0:T(8,128)S(1)}, u32[]{:S(2)}, u32[]{:S(2)}) collective-permute-start(f32[8,768]{1,0:T(8,128)S(1)} %get-tuple-element.37), channel_id=1, source_target_pairs={{8,16},{16,8},{9,17},{17,9},{10,18},{18,10},{11,19},{19,11},{12,20... | collective-permute-start | bytes 73736 | tf_op jit(solution)/shard_map/ppermute | solution.py:49
  30.7 4.0 %collective-permute-start.8 = (f32[32,384]{1,0:T(8,128)S(1)}, f32[32,384]{1,0:T(8,128)S(1)}, u32[]{:S(2)}, u32[]{:S(2)}) collective-permute-start(f32[32,384]{1,0:T(8,128)S(1)} %get-tuple-element.39), channel_id=1, source_target_pairs={{0,1},{1,0},{8,9},{9,8},{16,17},{17,16},{24,25},{25,24},{2,3},{3,2... | collective-permute-start | bytes 147464 | tf_op jit(solution)/shard_map/ppermute | solution.py:50
  30.7 5.1 %collective-permute-start.9 = (f32[32,384]{1,0:T(8,128)S(1)}, f32[32,384]{1,0:T(8,128)S(1)}, u32[]{:S(2)}, u32[]{:S(2)}) collective-permute-start(f32[32,384]{1,0:T(8,128)S(1)} %get-tuple-element.40), channel_id=1, source_target_pairs={{1,2},{2,1},{9,10},{10,9},{17,18},{18,17},{25,26},{26,25},{3,4},{4... | collective-permute-start | bytes 147464 | tf_op jit(solution)/shard_map/ppermute | solution.py:49

commit v7 on v6

--- a/solution.py
+++ b/solution.py
@@ -31,13 +31,14 @@
 PACK_LIMIT = 8
 
 
-def neighbours(axis, other, first, fill):
+def neighbours(axis, other, first, fill, apart=False):
     count, wide = lax.axis_size(axis), lax.axis_size(other)
     pairs = [((i, j), (i + 1, j)) for i in range(first, count - 1, 2) for j in range(wide)]
     if fill and wide % 2 == 0:
         paired = {i for i, _ in (p for pair in pairs for p in pair)}
         idle = [i for i in range(count) if i not in paired]
-        pairs += [((i, j), (i, j + 1)) for i in idle for j in range(0, wide, 2)]
+        step = wide // 2 if apart else 1
+        pairs += [((i, j), (i, j + step)) for i in idle for j in range(wide) if j // step % 2 == 0]
     route = []
     for (i, j), (k, m) in pairs:
         one, two = (i * wide + j, k * wide + m) if axis == AXES[0] else (j * count + i, m * count + k)
@@ -45,8 +46,8 @@
     return route
 
 
-def swap(to_a, to_b, axis, other, fill=True):
-    from_b = lax.ppermute(to_b, AXES, neighbours(axis, other, 1, fill))
+def swap(to_a, to_b, axis, other, fill=True, apart=False):
+    from_b = lax.ppermute(to_b, AXES, neighbours(axis, other, 1, fill, apart))
     from_a = lax.ppermute(to_a, AXES, neighbours(axis, other, 0, fill))
     return from_a, from_b
 
@@ -76,7 +77,7 @@
     ins = [pltpu.with_memory_space_constraint(x, pltpu.HBM) if n in far else x for n, x in enumerate(ins)]
     return pl.pallas_call(
         body,
-        out_shape=[jax.ShapeDtypeStruct(s, jnp.float32) for s in outs],
+        out_shape=[jax.ShapeDtypeStruct(s, jnp.float32) if isinstance(s, tuple) else s for s in outs],
         in_specs=specs,
         out_specs=[vmem] * len(outs),
         scratch_shapes=list(scratch),
@@ -278,51 +279,8 @@
     put(full_e, 0, bottom, begin, one)
 
 
-def assemble_body(e_far, h_far, t_far, xa, xb, ya, yb, fe, fh, ft, e_in, h_in, t_in, sems):
-    copies = fetch((e_far, h_far, t_far), (e_in, h_in, t_in), sems)
-    rows, width = e_in.shape[1:]
-    total_rows = fe.shape[2]
-    low_x, high_x = sorter("gx")
-    low_y, high_y = sorter("gy")
-    inner, top, bottom = slice(SUB, SUB + rows), slice(0, SUB), slice(SUB + rows, total_rows)
-    fields = []
-    for own, full, factor in ((e_in, fe, None), (h_in, fh, courant), (t_in, ft, courant * courant)):
-        fields += [(own, full, factor, c) for c in range(own.shape[0])]
-    count = len(fields)
-
-    def scaled_to(factor, value):
-        return value if factor is None else value * factor
-
-    for k, (own, full, factor, c) in enumerate(fields):
-        for n in range(full.shape[1]):
-            full[c, n, top, :] = jnp.zeros((SUB, LANE), jnp.float32)
-            full[c, n, bottom, :] = jnp.zeros((SUB, LANE), jnp.float32)
-        for begin, side, tail in ((0, low_y, True), (SIDE + width, high_y, False)):
-            value = side(from_lanes(ya, k, count, tail), from_lanes(yb, k, count, tail))
-            put(full, c, inner, begin, scaled_to(factor, value))
-    place_rows(fe, fh, ft, rows, SIDE, lambda s: low_x(xa[s], xb[s]), lambda s: high_x(xa[s], xb[s]))
-    for copy in copies:
-        copy.wait()
-    for own, full, factor, c in fields:
-        put(full, c, inner, SIDE, scaled_to(factor, own[c]))
-
-
-def main_body(fe_in, fh_in, ft_in, s_far, ca, cb, inverse, fe, fh, ft, scaled, to_a, to_b, saved, sems, fg):
-    del fe_in, fh_in, ft_in
-    (frames,) = fetch((s_far,), (saved,), sems)
-    rows, width = scaled.shape
-    total_rows = fe.shape[2]
-    tiles = total_rows // SUB
-    low_x, high_x = sorter("gx")
-    low_y, high_y = sorter("gy")
-    even_x = is_even("gx")
-
-    height = up_to(FULL * 15 + EXTRA, 2 * SUB)
-    for begin, side, tail in ((0, low_y, True), (SIDE + width, high_y, False)):
-        packets = [side(a, b) for a, b in zip(from_corners(ca, height, tail), from_corners(cb, height, tail))]
-        low, high = low_x(*packets), high_x(*packets)
-        place_rows(fe, fh, ft, rows, begin, lambda s, low=low: low[s], lambda s, high=high: high[s])
-
+def sweeper(fe, fh, ft, fg, width):
+    tiles = fe.shape[2] // SUB
     inside_x = jnp.where(lax.axis_index("gx") > 0, 1.0, 0.0).astype(jnp.float32)
     inside_y = jnp.where(lax.axis_index("gy") > 0, 1.0, 0.0).astype(jnp.float32)
     lane = lax.broadcasted_iota(jnp.int32, (SUB, LANE), 1)
@@ -352,7 +310,7 @@
             return turned
         return jnp.where(lane >= places, turned, pltpu.roll(values[n - 1], places, 1))
 
-    for step in range(STEPS):
+    def sweep(step, part):
         left = STEPS - 1 - step
         lanes_g, lanes_h, lanes_e = tiles_of(left + 1, left + 1), tiles_of(left + 1, left), tiles_of(left, left)
         last = left == 0
@@ -417,15 +375,23 @@
             for c in range(3):
                 fe[c, n, at(r), :] = fe[c, n, at(r), :] + curl[c]
 
+        inner = list(range(tiles - 2, 0, -1))
         if joined:
-            inner = list(range(tiles - 2, 0, -1))
             stages = [(joint, None, None)] + [
                 (r, r, r + 1 if n > 0 else None) for n, r in enumerate(inner)
             ]
             stages += [(None, joint, None), (None, None, 1)] + ([] if last else [(None, None, joint)])
+        elif part == "inner":
+            stages = [(inner[0], None, None)] + [
+                (r, r, r + 1 if n > 0 else None) for n, r in enumerate(inner[1:])
+            ]
+        elif part == "rest":
+            stages = [(joint, None, None), (joint - 1, joint, None), (None, joint - 1, joint), (1, None, joint - 1)]
+            stages += [(0, None, None), (None, 0, 1), (None, None, 0)]
+            h[1] = [{n: fh[c, n, at(1), :] for n in lanes_h} for c in range(3)]
         else:
-            stages = [(r - 1 if r > 0 else None, r if r < tiles else None, r + 1 if r + 1 < tiles else None) for r in range(tiles, -2, -1)]
-            stages = [(a, b if b is not None and b >= 0 else None, c) for a, b, c in stages]
+            stages = [(r - 1, r, r + 1) for r in range(tiles, -2, -1)]
+            stages = [[r if 0 <= r < tiles else None for r in stage] for stage in stages]
         for to_turn, to_h, to_e in stages:
             for n in lanes_g:
                 if to_turn is not None:
@@ -436,8 +402,56 @@
                 if to_e is not None and n in lanes_e:
                     update_e(to_e, n)
 
-        if step == 0:
-            frames.wait()
+    return sweep
+
+
+def assemble_body(e_far, h_far, t_far, s_far, xa, xb, ya, yb, fe, fh, ft, saved, e_in, h_in, t_in, sems, fg):
+    *copies, frames = fetch((e_far, h_far, t_far, s_far), (e_in, h_in, t_in, saved), sems)
+    rows, width = e_in.shape[1:]
+    total_rows = fe.shape[2]
+    low_x, high_x = sorter("gx")
+    low_y, high_y = sorter("gy")
+    inner, top, bottom = slice(SUB, SUB + rows), slice(0, SUB), slice(SUB + rows, total_rows)
+    fields = []
+    for own, full, factor in ((e_in, fe, None), (h_in, fh, courant), (t_in, ft, courant * courant)):
+        fields += [(own, full, factor, c) for c in range(own.shape[0])]
+    count = len(fields)
+
+    def scaled_to(factor, value):
+        return value if factor is None else value * factor
+
+    for k, (own, full, factor, c) in enumerate(fields):
+        for n in range(full.shape[1]):
+            full[c, n, top, :] = jnp.zeros((SUB, LANE), jnp.float32)
+            full[c, n, bottom, :] = jnp.zeros((SUB, LANE), jnp.float32)
+        for begin, side, tail in ((0, low_y, True), (SIDE + width, high_y, False)):
+            value = side(from_lanes(ya, k, count, tail), from_lanes(yb, k, count, tail))
+            put(full, c, inner, begin, scaled_to(factor, value))
+    place_rows(fe, fh, ft, rows, SIDE, lambda s: low_x(xa[s], xb[s]), lambda s: high_x(xa[s], xb[s]))
+    for copy in copies:
+        copy.wait()
+    for own, full, factor, c in fields:
+        put(full, c, inner, SIDE, scaled_to(factor, own[c]))
+    sweeper(fe, fh, ft, fg, width)(0, "inner")
+    frames.wait()
+
+
+def main_body(fe_in, fh_in, ft_in, saved, ca, cb, inverse, fe, fh, ft, scaled, to_a, to_b, fg):
+    del fe_in, fh_in, ft_in
+    rows, width = scaled.shape
+    low_x, high_x = sorter("gx")
+    low_y, high_y = sorter("gy")
+    even_x = is_even("gx")
+
+    height = up_to(FULL * 15 + EXTRA, 2 * SUB)
+    for begin, side, tail in ((0, low_y, True), (SIDE + width, high_y, False)):
+        packets = [side(a, b) for a, b in zip(from_corners(ca, height, tail), from_corners(cb, height, tail))]
+        low, high = low_x(*packets), high_x(*packets)
+        place_rows(fe, fh, ft, rows, begin, lambda s, low=low: low[s], lambda s, high=high: high[s])
+
+    sweep = sweeper(fe, fh, ft, fg, width)
+    for step in range(STEPS):
+        sweep(step, "rest" if step == 0 else "all")
         pair = 2 * SUB
         for r in range(rows // pair):
             for n in range(width // LANE):
@@ -525,20 +539,27 @@
     ya, yb = swap(*call(pack_lanes, [packet, packet], own, room(*own), limit=8, far=(0, 1, 2)), "gy", "gx", fill=False)
     height = xa.shape[0]
     packet = (2 * height + up_to(height // 4, SUB), WHOLE)
-    ca, cb = swap(*call(pack_corners, [packet, packet], (xa, xb), limit=8), "gy", "gx")
+    ca, cb = swap(*call(pack_corners, [packet, packet], (xa, xb), limit=8), "gy", "gx", apart=True)
 
     row_places = lax.axis_index("gx") * rows + lax.broadcasted_iota(jnp.int32, (rows, width), 0)
     col_places = lax.axis_index("gy") * cols + lax.broadcasted_iota(jnp.int32, (rows, width), 1) // NZ
     cover = coverage(row_places, lax.axis_size("gx") * rows) * coverage(col_places, lax.axis_size("gy") * cols)
 
-    fields = call(assemble_body, fulls, (*own, xa, xb, ya, yb), room(*own), cost=2**22, far=(0, 1, 2))
+    shifted = pltpu.VMEM((2, full[0], full[1] + SUB, LANE), jnp.float32)
+    *fields, frames = call(
+        assemble_body,
+        [*fulls, jax.ShapeDtypeStruct(saved.shape, saved.dtype)],
+        (*own, saved, xa, xb, ya, yb),
+        [*room(*own)[:-1], pltpu.SemaphoreType.DMA((4,)), shifted],
+        cost=2**22,
+        far=(0, 1, 2, 3),
+    )
     fe, fh, _, scaled, to_a, to_b = call(
         main_body,
         [*fulls, (rows, width), edge, edge],
-        (*fields, saved, ca, cb, 1.0 / cover),
-        [*room(saved), pltpu.VMEM((2, full[0], full[1] + SUB, LANE), jnp.float32)],
+        (*fields, frames, ca, cb, 1.0 / cover),
+        [shifted],
         limit=20,
-        far=(3,),
         aliases={0: 0, 1: 1, 2: 2},
         cost=2**23,
     )
@@ -546,7 +567,7 @@
     e, h = call(emit_body, [electric.shape, magnetic.shape], (fe, fh))
     side = (rows, REACH)
     across, to_a, to_b = call(filter_rows, [(rows, width), side, side], (scaled, xa, xb))
-    ya, yb = swap(to_a, to_b, "gy", "gx")
+    ya, yb = swap(to_a, to_b, "gy", "gx", apart=True)
     (gradient,) = call(filter_columns, [(rows, width)], (across, ya, yb))
     return e, h, gradient
 

time: 37.3 us -> 36.5 us (0.979)
    ppermute x5, starting transfers between devices: 10.9 us -> 9.61 us  [swap(): from_b = lax.ppermute(to_b, AXES, neighbours(axis, other, 1, fill, apart))]
    ppermute x5, starting transfers between devices: 5.83 us -> 7.07 us  [swap(): from_a = lax.ppermute(to_a, AXES, neighbours(axis, other, 0, fill))]
  transfers between devices with their start and end apart: 10 -> 10, of which waited for: 4 -> 4; matrix products, arithmetic and copies ran while one was open for 0% -> 0% of each run, Pallas kernels for 12% -> 13%
where the time goes in v7:
time: 36.5 us; the launch traced here: 36.3 us
  starting transfers between devices  16.7 us (46%)
  Pallas kernels  10.5 us (29%)
  waiting for transfers between devices  8.24 us (23%)
  between operations  0.75 us (2%)
    ppermute x5, starting transfers between devices, swap(): from_b = lax.ppermute(to_b, AXES, neighbours(axis, other, 1, fill, apart))  9.61 us
    pallas_call x7, Pallas kernels, call(): pl.pallas_call(body, out_shape=[jax.ShapeDtypeStruct(s, jnp.float32) if i...  9.14 us
    ppermute x5, starting transfers between devices, swap(): from_a = lax.ppermute(to_a, AXES, neighbours(axis, other, 0, fill))  7.07 us
    ppermute x5, waiting for transfers between devices, swap(): from_a = lax.ppermute(to_a, AXES, neighbours(axis, other, 0, fill))  5.68 us
    ppermute x5, waiting for transfers between devices, swap(): from_b = lax.ppermute(to_b, AXES, neighbours(axis, other, 1, fill, apart))  2.56 us
    pallas_call x1, Pallas kernels, pack_x(): pl.pallas_call(pack_rows, name='pack_x', out_shape=[out, out], in_specs=[...  1.37 us
  transfers between devices with their start and end apart: 10, of which 4 were waited for; matrix products, arithmetic and copies ran while one was open for 0% of the time, Pallas kernels for 13%

profile of v7, /device:TPU:0, one launch (start us, length us, event | category | flops | bytes accessed | tf_op | source)
XLA Modules:
  0.0 36.3 jit_solution(1016325097207418765)
XLA Ops:
  0.6 1.4 %pack_x.1 = (f32[80,768]{1,0:T(8,128)S(1)}, f32[80,768]{1,0:T(8,128)S(1)}) custom-call(f32[3,32,768]{2,1,0:T(8,128)} %e_far.3, f32[3,32,768]{2,1,0:T(8,128)} %h_far.3, f32[9,32,768]{2,1,0:T(8,128)} %t_far.3), custom_call_target="tpu_custom_call" | custom-call | tf_op jit(solution)/shard_map/pack_x/pallas_call | solution.py:141
  2.0 3.0 %collective-permute-start = (f32[80,768]{1,0:T(8,128)S(1)}, f32[80,768]{1,0:T(8,128)S(1)}, u32[]{:S(2)}, u32[]{:S(2)}) collective-permute-start(f32[80,768]{1,0:T(8,128)S(1)} %get-tuple-element.23), channel_id=1, source_target_pairs={{0,8},{8,0},{1,9},{9,1},{2,10},{10,2},{3,11},{11,3},{4,12},{12,4},... | collective-permute-start | bytes 737288 | tf_op jit(solution)/shard_map/ppermute | solution.py:51
  5.0 0.0 collective-permute-start.1
  5.0 1.6 %shard_map.67 = (f32[17,32,256]{2,1,0:T(8,128)S(1)}, f32[17,32,256]{2,1,0:T(8,128)S(1)}) custom-call(f32[3,32,768]{2,1,0:T(8,128)} %e_far.3, f32[3,32,768]{2,1,0:T(8,128)} %h_far.3, f32[9,32,768]{2,1,0:T(8,128)} %t_far.3), custom_call_target="tpu_custom_call" | custom-call | flops 1048576 | bytes 1048576 | tf_op jit(solution)/shard_map/pallas_call | solution.py:78
  6.6 0.6 %collective-permute-start.2 = (f32[17,32,256]{2,1,0:T(8,128)S(1)}, f32[17,32,256]{2,1,0:T(8,128)S(1)}, u32[]{:S(2)}, u32[]{:S(2)}) collective-permute-start(f32[17,32,256]{2,1,0:T(8,128)S(1)} %get-tuple-element.25), channel_id=1, source_target_pairs={{0,1},{1,0},{8,9},{9,8},{16,17},{17,16},{24,25},{25,24},{2,3},{3,2... | collective-permute-start | bytes 1671176 | tf_op jit(solution)/shard_map/ppermute | solution.py:51
  7.2 0.7 %collective-permute-start.3 = (f32[17,32,256]{2,1,0:T(8,128)S(1)}, f32[17,32,256]{2,1,0:T(8,128)S(1)}, u32[]{:S(2)}, u32[]{:S(2)}) collective-permute-start(f32[17,32,256]{2,1,0:T(8,128)S(1)} %get-tuple-element.26), channel_id=1, source_target_pairs={{1,2},{2,1},{9,10},{10,9},{17,18},{18,17},{25,26},{26,25},{3,4},{4... | collective-permute-start | bytes 1671176 | tf_op jit(solution)/shard_map/ppermute | solution.py:50
  8.0 3.9 %collective-permute-done.xa = f32[80,768]{1,0:T(8,128)S(1)} collective-permute-done((f32[80,768]{1,0:T(8,128)S(1)}, f32[80,768]{1,0:T(8,128)S(1)}, u32[]{:S(2)}, u32[]{:S(2)}) %collective-permute-start) | collective-permute-done | bytes 245792 | tf_op jit(solution)/shard_map/ppermute | solution.py:51
  11.8 0.0 collective-permute-done.1.xb
  11.8 0.1 shard_map.69
  12.0 0.1 collective-permute-start.4
  12.0 5.9 %collective-permute-start.5 = (f32[184,256]{1,0:T(8,128)S(1)}, f32[184,256]{1,0:T(8,128)S(1)}, u32[]{:S(2)}, u32[]{:S(2)}) collective-permute-start(f32[184,256]{1,0:T(8,128)S(1)} %get-tuple-element.32), channel_id=1, source_target_pairs={{1,2},{2,1},{9,10},{10,9},{17,18},{18,17},{25,26},{26,25},{3,4},{4... | collective-permute-start | bytes 565256 | tf_op jit(solution)/shard_map/ppermute | solution.py:50
  18.0 0.1 multiply_divide_fusion.inverse
  18.1 0.0 collective-permute-done.2.ya
  18.1 0.0 collective-permute-done.3.yb
  18.1 2.1 %shard_map.68 = (f32[3,12,48,128]{3,2,1,0:T(8,128)S(1)}, f32[3,12,48,128]{3,2,1,0:T(8,128)S(1)}, f32[9,12,48,128]{3,2,1,0:T(8,128)S(1)}, bf16[6,3,32,768]{3,2,1,0:T(8,128)(2,1)S(1)}) custom-call(f32[3,32,768]{2,1,0:T(8,128)} %e_far.3, f32[3,32,768]{2,1,0:T(8,128)} %h_far.3, f32[9,32,768]{2,1,0:T(8,128)} %t_far.3, bf16[6,3,32,768]{3,2,1,0:T(8,128)(2,1)} %s_far.1, ...), custom_call_target="tpu_custom_call" | custom-call | flops 4194304 | bytes 4194304 | tf_op jit(solution)/shard_map/pallas_call | solution.py:78
  20.2 0.0 collective-permute-done.4.ca
  20.2 1.3 %collective-permute-done.5.cb = f32[184,256]{1,0:T(8,128)S(1)} collective-permute-done((f32[184,256]{1,0:T(8,128)S(1)}, f32[184,256]{1,0:T(8,128)S(1)}, u32[]{:S(2)}, u32[]{:S(2)}) %collective-permute-start.5) | collective-permute-done | bytes 188448 | tf_op jit(solution)/shard_map/ppermute | solution.py:50
  21.5 3.2 %shard_map.70 = (f32[3,12,48,128]{3,2,1,0:T(8,128)S(1)}, f32[3,12,48,128]{3,2,1,0:T(8,128)S(1)}, f32[9,12,48,128]{3,2,1,0:T(8,128)S(1)}, f32[32,768]{1,0:T(8,128...) custom-call(f32[3,12,48,128]{3,2,1,0:T(8,128)S(1)} %get-tuple-elemen, ...), custom_call_target="tpu_custom_call", output_to_operand_aliasing={{0}: (0, {}), {1}: (1, {}), {2}: (2, {})} | custom-call | flops 8388608 | bytes 8388608 | tf_op jit(solution)/shard_map/pallas_call | solution.py:78
  24.8 3.3 %collective-permute-start.6 = (f32[8,768]{1,0:T(8,128)S(1)}, f32[8,768]{1,0:T(8,128)S(1)}, u32[]{:S(2)}, u32[]{:S(2)}) collective-permute-start(f32[8,768]{1,0:T(8,128)S(1)} %get-tuple-element.38), channel_id=1, source_target_pairs={{0,8},{8,0},{1,9},{9,1},{2,10},{10,2},{3,11},{11,3},{4,12},{12,4},... | collective-permute-start | bytes 73736 | tf_op jit(solution)/shard_map/ppermute | solution.py:51
  28.1 0.0 collective-permute-start.7
  28.1 1.8 %collective-permute-done.6.xa = f32[8,768]{1,0:T(8,128)S(1)} collective-permute-done((f32[8,768]{1,0:T(8,128)S(1)}, f32[8,768]{1,0:T(8,128)S(1)}, u32[]{:S(2)}, u32[]{:S(2)}) %collective-permute-start.6) | collective-permute-done | bytes 24608 | tf_op jit(solution)/shard_map/ppermute | solution.py:51
  29.9 0.0 collective-permute-done.7.xb
  29.9 0.1 shard_map.72
  30.0 0.1 collective-permute-start.8
  30.1 3.0 %collective-permute-start.9 = (f32[32,384]{1,0:T(8,128)S(1)}, f32[32,384]{1,0:T(8,128)S(1)}, u32[]{:S(2)}, u32[]{:S(2)}) collective-permute-start(f32[32,384]{1,0:T(8,128)S(1)} %get-tuple-element.42), channel_id=1, source_target_pairs={{1,2},{2,1},{9,10},{10,9},{17,18},{18,17},{25,26},{26,25},{3,4},{4... | collective-permute-start | bytes 147464 | tf_op jit(solution)/shard_map/ppermute | solution.py:50
  33.1 0.9 %shard_map.71 = (f32[3,32,768]{2,1,0:T(8,128)}, f32[3,32,768]{2,1,0:T(8,128)}) custom-call(f32[3,12,48,128]{3,2,1,0:T(8,128)S(1)} %get-tuple-element.33.fe, f32[3,12,48,128]{3,2,1,0:T(8,128)S(1)} %get-tuple-element.34.fh), custom_call_target="tpu_custom_call" | custom-call | flops 1048576 | bytes 1048576 | tf_op jit(solution)/shard_map/pallas_call | solution.py:78
  33.9 0.0 collective-permute-done.8.ya
  34.0 1.2 %collective-permute-done.9.yb = f32[32,384]{1,0:T(8,128)S(1)} collective-permute-done((f32[32,384]{1,0:T(8,128)S(1)}, f32[32,384]{1,0:T(8,128)S(1)}, u32[]{:S(2)}, u32[]{:S(2)}) %collective-permute-start.9) | collective-permute-done | bytes 49184 | tf_op jit(solution)/shard_map/ppermute | solution.py:50
  35.2 1.2 %shard_map.73 = f32[32,768]{1,0:T(8,128)} custom-call(f32[32,768]{1,0:T(8,128)S(1)} %get-tuple-element.40.across, f32[32,384]{1,0:T(8,128)S(1)} %collective-permute-done.8.ya, f32[32,384]{1,0:T(8,128)S(1)} %collective-permute-done.9.yb), custom_call_target="tpu_custom_call" | custom-call | flops 1048576 | bytes 1048576 | tf_op jit(solution)/shard_map/pallas_call | solution.py:78
  (3 shorter events, 0.0 us)
Async XLA Ops:
  2.0 9.8 %collective-permute-start = (f32[80,768]{1,0:T(8,128)S(1)}, f32[80,768]{1,0:T(8,128)S(1)}, u32[]{:S(2)}, u32[]{:S(2)}) collective-permute-start(f32[80,768]{1,0:T(8,128)S(1)} %get-tuple-element.23), channel_id=1, source_target_pairs={{0,8},{8,0},{1,9},{9,1},{2,10},{10,2},{3,11},{11,3},{4,12},{12,4},... | collective-permute-start | bytes 737288 | tf_op jit(solution)/shard_map/ppermute | solution.py:51
  5.0 6.8 %collective-permute-start.1 = (f32[80,768]{1,0:T(8,128)S(1)}, f32[80,768]{1,0:T(8,128)S(1)}, u32[]{:S(2)}, u32[]{:S(2)}) collective-permute-start(f32[80,768]{1,0:T(8,128)S(1)} %get-tuple-element.24), channel_id=1, source_target_pairs={{8,16},{16,8},{9,17},{17,9},{10,18},{18,10},{11,19},{19,11},{12,20... | collective-permute-start | bytes 737288 | tf_op jit(solution)/shard_map/ppermute | solution.py:50
  6.6 11.4 %collective-permute-start.2 = (f32[17,32,256]{2,1,0:T(8,128)S(1)}, f32[17,32,256]{2,1,0:T(8,128)S(1)}, u32[]{:S(2)}, u32[]{:S(2)}) collective-permute-start(f32[17,32,256]{2,1,0:T(8,128)S(1)} %get-tuple-element.25), channel_id=1, source_target_pairs={{0,1},{1,0},{8,9},{9,8},{16,17},{17,16},{24,25},{25,24},{2,3},{3,2... | collective-permute-start | bytes 1671176 | tf_op jit(solution)/shard_map/ppermute | solution.py:51
  7.2 10.9 %collective-permute-start.3 = (f32[17,32,256]{2,1,0:T(8,128)S(1)}, f32[17,32,256]{2,1,0:T(8,128)S(1)}, u32[]{:S(2)}, u32[]{:S(2)}) collective-permute-start(f32[17,32,256]{2,1,0:T(8,128)S(1)} %get-tuple-element.26), channel_id=1, source_target_pairs={{1,2},{2,1},{9,10},{10,9},{17,18},{18,17},{25,26},{26,25},{3,4},{4... | collective-permute-start | bytes 1671176 | tf_op jit(solution)/shard_map/ppermute | solution.py:50
  12.0 8.2 %collective-permute-start.4 = (f32[184,256]{1,0:T(8,128)S(1)}, f32[184,256]{1,0:T(8,128)S(1)}, u32[]{:S(2)}, u32[]{:S(2)}) collective-permute-start(f32[184,256]{1,0:T(8,128)S(1)} %get-tuple-element.31), channel_id=1, source_target_pairs={{0,1},{1,0},{8,9},{9,8},{16,17},{17,16},{24,25},{25,24},{2,3},{3,2... | collective-permute-start | bytes 565256 | tf_op jit(solution)/shard_map/ppermute | solution.py:51
  12.0 9.5 %collective-permute-start.5 = (f32[184,256]{1,0:T(8,128)S(1)}, f32[184,256]{1,0:T(8,128)S(1)}, u32[]{:S(2)}, u32[]{:S(2)}) collective-permute-start(f32[184,256]{1,0:T(8,128)S(1)} %get-tuple-element.32), channel_id=1, source_target_pairs={{1,2},{2,1},{9,10},{10,9},{17,18},{18,17},{25,26},{26,25},{3,4},{4... | collective-permute-start | bytes 565256 | tf_op jit(solution)/shard_map/ppermute | solution.py:50
  24.8 5.1 %collective-permute-start.6 = (f32[8,768]{1,0:T(8,128)S(1)}, f32[8,768]{1,0:T(8,128)S(1)}, u32[]{:S(2)}, u32[]{:S(2)}) collective-permute-start(f32[8,768]{1,0:T(8,128)S(1)} %get-tuple-element.38), channel_id=1, source_target_pairs={{0,8},{8,0},{1,9},{9,1},{2,10},{10,2},{3,11},{11,3},{4,12},{12,4},... | collective-permute-start | bytes 73736 | tf_op jit(solution)/shard_map/ppermute | solution.py:51
  28.1 1.8 %collective-permute-start.7 = (f32[8,768]{1,0:T(8,128)S(1)}, f32[8,768]{1,0:T(8,128)S(1)}, u32[]{:S(2)}, u32[]{:S(2)}) collective-permute-start(f32[8,768]{1,0:T(8,128)S(1)} %get-tuple-element.39), channel_id=1, source_target_pairs={{8,16},{16,8},{9,17},{17,9},{10,18},{18,10},{11,19},{19,11},{12,20... | collective-permute-start | bytes 73736 | tf_op jit(solution)/shard_map/ppermute | solution.py:50
  30.0 3.9 %collective-permute-start.8 = (f32[32,384]{1,0:T(8,128)S(1)}, f32[32,384]{1,0:T(8,128)S(1)}, u32[]{:S(2)}, u32[]{:S(2)}) collective-permute-start(f32[32,384]{1,0:T(8,128)S(1)} %get-tuple-element.41), channel_id=1, source_target_pairs={{0,1},{1,0},{8,9},{9,8},{16,17},{17,16},{24,25},{25,24},{2,3},{3,2... | collective-permute-start | bytes 147464 | tf_op jit(solution)/shard_map/ppermute | solution.py:51
  30.1 5.1 %collective-permute-start.9 = (f32[32,384]{1,0:T(8,128)S(1)}, f32[32,384]{1,0:T(8,128)S(1)}, u32[]{:S(2)}, u32[]{:S(2)}) collective-permute-start(f32[32,384]{1,0:T(8,128)S(1)} %get-tuple-element.42), channel_id=1, source_target_pairs={{1,2},{2,1},{9,10},{10,9},{17,18},{18,17},{25,26},{26,25},{3,4},{4... | collective-permute-start | bytes 147464 | tf_op jit(solution)/shard_map/ppermute | solution.py:50

commit v8 on v7

--- a/solution.py
+++ b/solution.py
@@ -70,7 +70,7 @@
     return low, high
 
 
-def call(body, outs, ins, scratch=(), limit=16, aliases=None, cost=2**20, far=()):
+def call(body, outs, ins, scratch=(), limit=16, aliases=None, cost=2**20, far=(), space=pltpu.VMEM):
     vmem = pl.BlockSpec(memory_space=pltpu.VMEM)
     hbm = pl.BlockSpec(memory_space=pltpu.HBM)
     specs = [hbm if n in far else vmem for n in range(len(ins))]
@@ -79,7 +79,7 @@
         body,
         out_shape=[jax.ShapeDtypeStruct(s, jnp.float32) if isinstance(s, tuple) else s for s in outs],
         in_specs=specs,
-        out_specs=[vmem] * len(outs),
+        out_specs=[pl.BlockSpec(memory_space=space)] * len(outs),
         scratch_shapes=list(scratch),
         input_output_aliases=aliases or {},
         cost_estimate=pl.CostEstimate(flops=cost, bytes_accessed=cost, transcendentals=0),
@@ -445,7 +445,7 @@
 
     height = up_to(FULL * 15 + EXTRA, 2 * SUB)
     for begin, side, tail in ((0, low_y, True), (SIDE + width, high_y, False)):
-        packets = [side(a, b) for a, b in zip(from_corners(ca, height, tail), from_corners(cb, height, tail))]
+        packets = from_corners(side(ca[...], cb[...]), height, tail)
         low, high = low_x(*packets), high_x(*packets)
         place_rows(fe, fh, ft, rows, begin, lambda s, low=low: low[s], lambda s, high=high: high[s])
 
@@ -503,14 +503,19 @@
     to_b[...] = jnp.where(even_y, head, tail)
 
 
-def filter_columns(across, ya, yb, gradient):
+def filter_columns(across, ya, yb, gradient, made, sems):
     width = across.shape[1]
     low, high = sorter("gy")
+    copies = []
     for r in range(across.shape[0] // SUB):
         at = slice(r * SUB, (r + 1) * SUB)
         a, b = ya[at], yb[at]
         extended = jnp.concatenate([low(a, b), across[at], high(a, b)], axis=1)
-        gradient[at] = box(box(extended, NZ, 1), NZ, 1)[:, :width] * (1.0 / (RADIUS + 1.0))
+        made[at] = box(box(extended, NZ, 1), NZ, 1)[:, :width] * (1.0 / (RADIUS + 1.0))
+        copies.append(pltpu.make_async_copy(made.at[at], gradient.at[at], sems.at[r]))
+        copies[-1].start()
+    for copy in copies:
+        copy.wait()
 
 
 def tent(offset):
@@ -568,7 +573,13 @@
     side = (rows, REACH)
     across, to_a, to_b = call(filter_rows, [(rows, width), side, side], (scaled, xa, xb))
     ya, yb = swap(to_a, to_b, "gy", "gx", apart=True)
-    (gradient,) = call(filter_columns, [(rows, width)], (across, ya, yb))
+    (gradient,) = call(
+        filter_columns,
+        [(rows, width)],
+        (across, ya, yb),
+        [pltpu.VMEM((rows, width), jnp.float32), pltpu.SemaphoreType.DMA((rows // SUB,))],
+        space=pltpu.HBM,
+    )
     return e, h, gradient
 
 

time: 36.5 us -> 36.5 us (level)
  no operation moved by 1% of the time
where the time goes in v8:
time: 36.5 us; the launch traced here: 36.3 us
  starting transfers between devices  16.7 us (46%)
  Pallas kernels  10.5 us (29%)
  waiting for transfers between devices  8.24 us (23%)
  between operations  0.75 us (2%)
    ppermute x5, starting transfers between devices, swap(): from_b = lax.ppermute(to_b, AXES, neighbours(axis, other, 1, fill, apart))  9.61 us
    pallas_call x7, Pallas kernels, call(): pl.pallas_call(body, out_shape=[jax.ShapeDtypeStruct(s, jnp.float32) if i...  9.11 us
    ppermute x5, starting transfers between devices, swap(): from_a = lax.ppermute(to_a, AXES, neighbours(axis, other, 0, fill))  7.07 us
    ppermute x5, waiting for transfers between devices, swap(): from_a = lax.ppermute(to_a, AXES, neighbours(axis, other, 0, fill))  5.68 us
    ppermute x5, waiting for transfers between devices, swap(): from_b = lax.ppermute(to_b, AXES, neighbours(axis, other, 1, fill, apart))  2.56 us
    pallas_call x1, Pallas kernels, pack_x(): pl.pallas_call(pack_rows, name='pack_x', out_shape=[out, out], in_specs=[...  1.37 us
  transfers between devices with their start and end apart: 10, of which 4 were waited for; matrix products, arithmetic and copies ran while one was open for 0% of the time, Pallas kernels for 13%

profile of v8, /device:TPU:0, one launch (start us, length us, event | category | flops | bytes accessed | tf_op | source)
XLA Modules:
  0.0 36.3 jit_solution(13230710501885709209)
XLA Ops:
  0.6 1.4 %pack_x.1 = (f32[80,768]{1,0:T(8,128)S(1)}, f32[80,768]{1,0:T(8,128)S(1)}) custom-call(f32[3,32,768]{2,1,0:T(8,128)} %e_far.3, f32[3,32,768]{2,1,0:T(8,128)} %h_far.3, f32[9,32,768]{2,1,0:T(8,128)} %t_far.3), custom_call_target="tpu_custom_call" | custom-call | tf_op jit(solution)/shard_map/pack_x/pallas_call | solution.py:141
  2.0 3.0 %collective-permute-start = (f32[80,768]{1,0:T(8,128)S(1)}, f32[80,768]{1,0:T(8,128)S(1)}, u32[]{:S(2)}, u32[]{:S(2)}) collective-permute-start(f32[80,768]{1,0:T(8,128)S(1)} %get-tuple-element.23), channel_id=1, source_target_pairs={{0,8},{8,0},{1,9},{9,1},{2,10},{10,2},{3,11},{11,3},{4,12},{12,4},... | collective-permute-start | bytes 737288 | tf_op jit(solution)/shard_map/ppermute | solution.py:51
  5.0 0.0 collective-permute-start.1
  5.0 1.6 %shard_map.67 = (f32[17,32,256]{2,1,0:T(8,128)S(1)}, f32[17,32,256]{2,1,0:T(8,128)S(1)}) custom-call(f32[3,32,768]{2,1,0:T(8,128)} %e_far.3, f32[3,32,768]{2,1,0:T(8,128)} %h_far.3, f32[9,32,768]{2,1,0:T(8,128)} %t_far.3), custom_call_target="tpu_custom_call" | custom-call | flops 1048576 | bytes 1048576 | tf_op jit(solution)/shard_map/pallas_call | solution.py:78
  6.6 0.6 %collective-permute-start.2 = (f32[17,32,256]{2,1,0:T(8,128)S(1)}, f32[17,32,256]{2,1,0:T(8,128)S(1)}, u32[]{:S(2)}, u32[]{:S(2)}) collective-permute-start(f32[17,32,256]{2,1,0:T(8,128)S(1)} %get-tuple-element.25), channel_id=1, source_target_pairs={{0,1},{1,0},{8,9},{9,8},{16,17},{17,16},{24,25},{25,24},{2,3},{3,2... | collective-permute-start | bytes 1671176 | tf_op jit(solution)/shard_map/ppermute | solution.py:51
  7.2 0.7 %collective-permute-start.3 = (f32[17,32,256]{2,1,0:T(8,128)S(1)}, f32[17,32,256]{2,1,0:T(8,128)S(1)}, u32[]{:S(2)}, u32[]{:S(2)}) collective-permute-start(f32[17,32,256]{2,1,0:T(8,128)S(1)} %get-tuple-element.26), channel_id=1, source_target_pairs={{1,2},{2,1},{9,10},{10,9},{17,18},{18,17},{25,26},{26,25},{3,4},{4... | collective-permute-start | bytes 1671176 | tf_op jit(solution)/shard_map/ppermute | solution.py:50
  8.0 3.9 %collective-permute-done.xa = f32[80,768]{1,0:T(8,128)S(1)} collective-permute-done((f32[80,768]{1,0:T(8,128)S(1)}, f32[80,768]{1,0:T(8,128)S(1)}, u32[]{:S(2)}, u32[]{:S(2)}) %collective-permute-start) | collective-permute-done | bytes 245792 | tf_op jit(solution)/shard_map/ppermute | solution.py:51
  11.8 0.0 collective-permute-done.1.xb
  11.8 0.1 shard_map.69
  12.0 0.1 collective-permute-start.4
  12.0 5.9 %collective-permute-start.5 = (f32[184,256]{1,0:T(8,128)S(1)}, f32[184,256]{1,0:T(8,128)S(1)}, u32[]{:S(2)}, u32[]{:S(2)}) collective-permute-start(f32[184,256]{1,0:T(8,128)S(1)} %get-tuple-element.32), channel_id=1, source_target_pairs={{1,2},{2,1},{9,10},{10,9},{17,18},{18,17},{25,26},{26,25},{3,4},{4... | collective-permute-start | bytes 565256 | tf_op jit(solution)/shard_map/ppermute | solution.py:50
  18.0 0.1 multiply_divide_fusion.inverse
  18.1 0.0 collective-permute-done.2.ya
  18.1 0.0 collective-permute-done.3.yb
  18.1 2.1 %shard_map.68 = (f32[3,12,48,128]{3,2,1,0:T(8,128)S(1)}, f32[3,12,48,128]{3,2,1,0:T(8,128)S(1)}, f32[9,12,48,128]{3,2,1,0:T(8,128)S(1)}, bf16[6,3,32,768]{3,2,1,0:T(8,128)(2,1)S(1)}) custom-call(f32[3,32,768]{2,1,0:T(8,128)} %e_far.3, f32[3,32,768]{2,1,0:T(8,128)} %h_far.3, f32[9,32,768]{2,1,0:T(8,128)} %t_far.3, bf16[6,3,32,768]{3,2,1,0:T(8,128)(2,1)} %s_far.1, ...), custom_call_target="tpu_custom_call" | custom-call | flops 4194304 | bytes 4194304 | tf_op jit(solution)/shard_map/pallas_call | solution.py:78
  20.2 0.0 collective-permute-done.4.ca
  20.2 1.3 %collective-permute-done.5.cb = f32[184,256]{1,0:T(8,128)S(1)} collective-permute-done((f32[184,256]{1,0:T(8,128)S(1)}, f32[184,256]{1,0:T(8,128)S(1)}, u32[]{:S(2)}, u32[]{:S(2)}) %collective-permute-start.5) | collective-permute-done | bytes 188448 | tf_op jit(solution)/shard_map/ppermute | solution.py:50
  21.5 3.2 %shard_map.70 = (f32[3,12,48,128]{3,2,1,0:T(8,128)S(1)}, f32[3,12,48,128]{3,2,1,0:T(8,128)S(1)}, f32[9,12,48,128]{3,2,1,0:T(8,128)S(1)}, f32[32,768]{1,0:T(8,128...) custom-call(f32[3,12,48,128]{3,2,1,0:T(8,128)S(1)} %get-tuple-elemen, ...), custom_call_target="tpu_custom_call", output_to_operand_aliasing={{0}: (0, {}), {1}: (1, {}), {2}: (2, {})} | custom-call | flops 8388608 | bytes 8388608 | tf_op jit(solution)/shard_map/pallas_call | solution.py:78
  24.7 3.3 %collective-permute-start.6 = (f32[8,768]{1,0:T(8,128)S(1)}, f32[8,768]{1,0:T(8,128)S(1)}, u32[]{:S(2)}, u32[]{:S(2)}) collective-permute-start(f32[8,768]{1,0:T(8,128)S(1)} %get-tuple-element.38), channel_id=1, source_target_pairs={{0,8},{8,0},{1,9},{9,1},{2,10},{10,2},{3,11},{11,3},{4,12},{12,4},... | collective-permute-start | bytes 73736 | tf_op jit(solution)/shard_map/ppermute | solution.py:51
  28.1 0.0 collective-permute-start.7
  28.1 1.8 %collective-permute-done.6.xa = f32[8,768]{1,0:T(8,128)S(1)} collective-permute-done((f32[8,768]{1,0:T(8,128)S(1)}, f32[8,768]{1,0:T(8,128)S(1)}, u32[]{:S(2)}, u32[]{:S(2)}) %collective-permute-start.6) | collective-permute-done | bytes 24608 | tf_op jit(solution)/shard_map/ppermute | solution.py:51
  29.9 0.0 collective-permute-done.7.xb
  29.9 0.1 shard_map.72
  30.0 0.1 collective-permute-start.8
  30.1 3.0 %collective-permute-start.9 = (f32[32,384]{1,0:T(8,128)S(1)}, f32[32,384]{1,0:T(8,128)S(1)}, u32[]{:S(2)}, u32[]{:S(2)}) collective-permute-start(f32[32,384]{1,0:T(8,128)S(1)} %get-tuple-element.42), channel_id=1, source_target_pairs={{1,2},{2,1},{9,10},{10,9},{17,18},{18,17},{25,26},{26,25},{3,4},{4... | collective-permute-start | bytes 147464 | tf_op jit(solution)/shard_map/ppermute | solution.py:50
  33.1 0.9 %shard_map.71 = (f32[3,32,768]{2,1,0:T(8,128)}, f32[3,32,768]{2,1,0:T(8,128)}) custom-call(f32[3,12,48,128]{3,2,1,0:T(8,128)S(1)} %get-tuple-element.33.fe, f32[3,12,48,128]{3,2,1,0:T(8,128)S(1)} %get-tuple-element.34.fh), custom_call_target="tpu_custom_call" | custom-call | flops 1048576 | bytes 1048576 | tf_op jit(solution)/shard_map/pallas_call | solution.py:78
  33.9 0.0 collective-permute-done.8.ya
  33.9 1.2 %collective-permute-done.9.yb = f32[32,384]{1,0:T(8,128)S(1)} collective-permute-done((f32[32,384]{1,0:T(8,128)S(1)}, f32[32,384]{1,0:T(8,128)S(1)}, u32[]{:S(2)}, u32[]{:S(2)}) %collective-permute-start.9) | collective-permute-done | bytes 49184 | tf_op jit(solution)/shard_map/ppermute | solution.py:50
  35.1 1.2 %shard_map.73 = f32[32,768]{1,0:T(8,128)} custom-call(f32[32,768]{1,0:T(8,128)S(1)} %get-tuple-element.40.across, f32[32,384]{1,0:T(8,128)S(1)} %collective-permute-done.8.ya, f32[32,384]{1,0:T(8,128)S(1)} %collective-permute-done.9.yb), custom_call_target="tpu_custom_call" | custom-call | flops 1048576 | bytes 1048576 | tf_op jit(solution)/shard_map/pallas_call | solution.py:78
  (3 shorter events, 0.0 us)
Async XLA Ops:
  2.0 9.8 %collective-permute-start = (f32[80,768]{1,0:T(8,128)S(1)}, f32[80,768]{1,0:T(8,128)S(1)}, u32[]{:S(2)}, u32[]{:S(2)}) collective-permute-start(f32[80,768]{1,0:T(8,128)S(1)} %get-tuple-element.23), channel_id=1, source_target_pairs={{0,8},{8,0},{1,9},{9,1},{2,10},{10,2},{3,11},{11,3},{4,12},{12,4},... | collective-permute-start | bytes 737288 | tf_op jit(solution)/shard_map/ppermute | solution.py:51
  5.0 6.8 %collective-permute-start.1 = (f32[80,768]{1,0:T(8,128)S(1)}, f32[80,768]{1,0:T(8,128)S(1)}, u32[]{:S(2)}, u32[]{:S(2)}) collective-permute-start(f32[80,768]{1,0:T(8,128)S(1)} %get-tuple-element.24), channel_id=1, source_target_pairs={{8,16},{16,8},{9,17},{17,9},{10,18},{18,10},{11,19},{19,11},{12,20... | collective-permute-start | bytes 737288 | tf_op jit(solution)/shard_map/ppermute | solution.py:50
  6.6 11.4 %collective-permute-start.2 = (f32[17,32,256]{2,1,0:T(8,128)S(1)}, f32[17,32,256]{2,1,0:T(8,128)S(1)}, u32[]{:S(2)}, u32[]{:S(2)}) collective-permute-start(f32[17,32,256]{2,1,0:T(8,128)S(1)} %get-tuple-element.25), channel_id=1, source_target_pairs={{0,1},{1,0},{8,9},{9,8},{16,17},{17,16},{24,25},{25,24},{2,3},{3,2... | collective-permute-start | bytes 1671176 | tf_op jit(solution)/shard_map/ppermute | solution.py:51
  7.2 10.9 %collective-permute-start.3 = (f32[17,32,256]{2,1,0:T(8,128)S(1)}, f32[17,32,256]{2,1,0:T(8,128)S(1)}, u32[]{:S(2)}, u32[]{:S(2)}) collective-permute-start(f32[17,32,256]{2,1,0:T(8,128)S(1)} %get-tuple-element.26), channel_id=1, source_target_pairs={{1,2},{2,1},{9,10},{10,9},{17,18},{18,17},{25,26},{26,25},{3,4},{4... | collective-permute-start | bytes 1671176 | tf_op jit(solution)/shard_map/ppermute | solution.py:50
  12.0 8.2 %collective-permute-start.4 = (f32[184,256]{1,0:T(8,128)S(1)}, f32[184,256]{1,0:T(8,128)S(1)}, u32[]{:S(2)}, u32[]{:S(2)}) collective-permute-start(f32[184,256]{1,0:T(8,128)S(1)} %get-tuple-element.31), channel_id=1, source_target_pairs={{0,1},{1,0},{8,9},{9,8},{16,17},{17,16},{24,25},{25,24},{2,3},{3,2... | collective-permute-start | bytes 565256 | tf_op jit(solution)/shard_map/ppermute | solution.py:51
  12.0 9.5 %collective-permute-start.5 = (f32[184,256]{1,0:T(8,128)S(1)}, f32[184,256]{1,0:T(8,128)S(1)}, u32[]{:S(2)}, u32[]{:S(2)}) collective-permute-start(f32[184,256]{1,0:T(8,128)S(1)} %get-tuple-element.32), channel_id=1, source_target_pairs={{1,2},{2,1},{9,10},{10,9},{17,18},{18,17},{25,26},{26,25},{3,4},{4... | collective-permute-start | bytes 565256 | tf_op jit(solution)/shard_map/ppermute | solution.py:50
  24.7 5.1 %collective-permute-start.6 = (f32[8,768]{1,0:T(8,128)S(1)}, f32[8,768]{1,0:T(8,128)S(1)}, u32[]{:S(2)}, u32[]{:S(2)}) collective-permute-start(f32[8,768]{1,0:T(8,128)S(1)} %get-tuple-element.38), channel_id=1, source_target_pairs={{0,8},{8,0},{1,9},{9,1},{2,10},{10,2},{3,11},{11,3},{4,12},{12,4},... | collective-permute-start | bytes 73736 | tf_op jit(solution)/shard_map/ppermute | solution.py:51
  28.1 1.8 %collective-permute-start.7 = (f32[8,768]{1,0:T(8,128)S(1)}, f32[8,768]{1,0:T(8,128)S(1)}, u32[]{:S(2)}, u32[]{:S(2)}) collective-permute-start(f32[8,768]{1,0:T(8,128)S(1)} %get-tuple-element.39), channel_id=1, source_target_pairs={{8,16},{16,8},{9,17},{17,9},{10,18},{18,10},{11,19},{19,11},{12,20... | collective-permute-start | bytes 73736 | tf_op jit(solution)/shard_map/ppermute | solution.py:50
  30.0 3.9 %collective-permute-start.8 = (f32[32,384]{1,0:T(8,128)S(1)}, f32[32,384]{1,0:T(8,128)S(1)}, u32[]{:S(2)}, u32[]{:S(2)}) collective-permute-start(f32[32,384]{1,0:T(8,128)S(1)} %get-tuple-element.41), channel_id=1, source_target_pairs={{0,1},{1,0},{8,9},{9,8},{16,17},{17,16},{24,25},{25,24},{2,3},{3,2... | collective-permute-start | bytes 147464 | tf_op jit(solution)/shard_map/ppermute | solution.py:51
  30.1 5.1 %collective-permute-start.9 = (f32[32,384]{1,0:T(8,128)S(1)}, f32[32,384]{1,0:T(8,128)S(1)}, u32[]{:S(2)}, u32[]{:S(2)}) collective-permute-start(f32[32,384]{1,0:T(8,128)S(1)} %get-tuple-element.42), channel_id=1, source_target_pairs={{1,2},{2,1},{9,10},{10,9},{17,18},{18,17},{25,26},{26,25},{3,4},{4... | collective-permute-start | bytes 147464 | tf_op jit(solution)/shard_map/ppermute | solution.py:50
